TPU v7x, 32 devices: a whole 2x2x4 slice. The times are simulated.
32 devices in a mesh: dp: 4 (over y, core), adapter: 8 (over z, x).
Axes of the slice: x: 2, y: 2, z: 4, core: 2. Of those that a mesh axis runs over, the one named last changes fastest.
Arguments:
- activations: bfloat16 [4096, 28672], P('adapter', 'dp'), may hold values from -6 to 6
- cotangent: bfloat16 [4096, 8192], P('adapter', 'dp'), may hold values from -6 to 6
- factor_in: bfloat16 [256, 16, 28672], P('adapter', None, 'dp'), may hold values from -0.03125 to 0.03125
- factor_out: bfloat16 [256, 16, 8192], P('adapter', None, 'dp'), may hold values from -0.0625 to 0.0625
- adapter_ids: int32 [16, 8], P('adapter'), may hold values from 0 to 255, as said below
- router_weights: float32 [16, 8], P('adapter'), may hold values from 0.25 to 1
Outputs:
- input_grad: float32 [4096, 28672], P('adapter', 'dp')
- grad_factor_in: bfloat16 [256, 16, 28672], P('adapter', None, 'dp')
- grad_factor_out: bfloat16 [256, 16, 8192], P('adapter', None, 'dp')
- router_grad: float32 [16, 8], P('adapter')
Inputs may be any that keep to these rules, and one draw needn't show every extreme that they name: `adapter_ids`: the 8 adapters of a request are different. The owner of adapter e is e // 32. Requests are taken in aligned groups of 2 (those of one index of adapter); among the 16 adapters named by one group no owner holds more than 2, and in every group some owner holds exactly 2.
All inputs are finite; a program needn't handle non-finite values.
Results may differ from a plain program's by a relative error of at most 0.012.
Values may be sent and summed in bfloat16 or wider, within the bound.
No kernel may reach another device: no remote copies, remote signals or barrier semaphores. Data moves between devices by JAX's collectives and lax.ppermute only.
A program may use at most 128 MiB of HBM per device.

v0:
```python
import jax
import jax.numpy as jnp
from jax import lax
from jax.sharding import PartitionSpec as P

CAP = 2


def body(activations, cotangent, factor_in, factor_out, adapter_ids, router_weights):
    owner_count = lax.axis_size("adapter")
    my_index = lax.axis_index("adapter")
    exp_count = factor_in.shape[0]
    rank_width = factor_in.shape[1]
    req_count = adapter_ids.shape[0]
    top_count = adapter_ids.shape[1]
    pair_count = req_count * top_count
    length = activations.shape[0] // req_count
    slot_count = owner_count * CAP
    my_pairs = adapter_ids.reshape(pair_count)
    my_owner = my_pairs // exp_count
    before = jnp.arange(pair_count)[:, None] > jnp.arange(pair_count)[None, :]
    my_slot = jnp.sum((my_owner[:, None] == my_owner[None, :]) & before, axis=1)
    target = my_owner * CAP + my_slot
    picker = target[:, None] == jnp.arange(slot_count)[None, :]
    all_ids = lax.all_gather(adapter_ids, "adapter", axis=0, tiled=True).reshape(
        owner_count, pair_count
    )
    all_owner = all_ids // exp_count
    all_slot = jnp.sum(
        (all_owner[:, :, None] == all_owner[:, None, :]) & before[None, :, :], axis=2
    )
    is_mine = all_owner == my_index
    local_idx = all_ids - my_index * exp_count
    matches = (
        is_mine[:, :, None, None]
        & (all_slot[:, :, None, None] == jnp.arange(CAP)[None, None, :, None])
        & (local_idx[:, :, None, None] == jnp.arange(exp_count)[None, None, None, :])
    )
    selector = jnp.any(matches, axis=1)
    selector = selector.astype(jnp.bfloat16)
    send_in = jnp.einsum(
        "jce,erf->jcrf", selector, factor_in, preferred_element_type=jnp.float32
    ).astype(jnp.bfloat16)
    send_out = jnp.einsum(
        "jce,erd->jcrd", selector, factor_out, preferred_element_type=jnp.float32
    ).astype(jnp.bfloat16)
    rows_in = activations.reshape(req_count, length, -1)
    rows_out = cotangent.reshape(req_count, length, -1)
    picker_bf = picker.astype(jnp.bfloat16)
    request_picker = picker.astype(jnp.float32).reshape(req_count, top_count, slot_count)
    piece_in = lax.all_to_all(send_in[:, None], "adapter", split_axis=0, concat_axis=1, tiled=True)
    piece_out = lax.all_to_all(
        send_out[:, None], "adapter", split_axis=0, concat_axis=1, tiled=True
    )
    proj_piece = jnp.einsum(
        "anirf,tf->anirt", piece_in, activations, preferred_element_type=jnp.float32
    )
    pull_piece = jnp.einsum(
        "anird,td->anirt", piece_out, cotangent, preferred_element_type=jnp.float32
    )
    got_in = piece_in
    got_out = piece_out
    full_proj = proj_piece
    full_pull = pull_piece
    got_in = got_in.reshape(slot_count, rank_width, -1)
    got_out = got_out.reshape(slot_count, rank_width, -1)
    pair_in = jnp.einsum(
        "qs,srf->qrf", picker_bf, got_in, preferred_element_type=jnp.float32
    ).astype(jnp.bfloat16)
    pair_in = pair_in.reshape(req_count, top_count * rank_width, -1)
    full_proj = full_proj.reshape(slot_count, rank_width, req_count, length)
    full_pull = full_pull.reshape(slot_count, rank_width, req_count, length)
    part_proj = jnp.einsum("bks,srbl->blkr", request_picker, full_proj).reshape(
        req_count, length, top_count * rank_width
    )
    part_pull = jnp.einsum("bks,srbl->blkr", request_picker, full_pull).reshape(
        req_count, length, top_count * rank_width
    )
    projected, pulled = lax.psum((part_proj, part_pull), "dp")
    router_grad = jnp.sum(
        (projected * pulled).reshape(req_count, length, top_count, rank_width), axis=(1, 3)
    )
    row_scale = jnp.repeat(router_weights, rank_width, axis=1)
    pulled_weighted = (pulled * row_scale[:, None, :]).astype(jnp.bfloat16)
    projected_weighted = (projected * row_scale[:, None, :]).astype(jnp.bfloat16)
    input_grad = jnp.einsum(
        "blj,bjf->blf", pulled_weighted, pair_in, preferred_element_type=jnp.float32
    ).reshape(req_count * length, -1)
    term_in = jnp.einsum(
        "blj,blf->bjf", pulled_weighted, rows_in, preferred_element_type=jnp.float32
    ).astype(jnp.bfloat16)
    term_out = jnp.einsum(
        "blj,bld->bjd", projected_weighted, rows_out, preferred_element_type=jnp.float32
    ).astype(jnp.bfloat16)
    back_in = jnp.einsum(
        "qs,qrf->srf",
        picker_bf,
        term_in.reshape(pair_count, rank_width, -1),
        preferred_element_type=jnp.float32,
    ).astype(jnp.bfloat16)
    back_out = jnp.einsum(
        "qs,qrd->srd",
        picker_bf,
        term_out.reshape(pair_count, rank_width, -1),
        preferred_element_type=jnp.float32,
    ).astype(jnp.bfloat16)
    back_in = back_in.reshape(owner_count, CAP, rank_width, -1)
    back_out = back_out.reshape(owner_count, CAP, rank_width, -1)
    ret_in, ret_out = (
        lax.all_to_all(back_in, "adapter", split_axis=0, concat_axis=0, tiled=True),
        lax.all_to_all(back_out, "adapter", split_axis=0, concat_axis=0, tiled=True),
    )
    grad_factor_in = jnp.einsum(
        "jce,jcrf->erf", selector, ret_in, preferred_element_type=jnp.float32
    ).astype(jnp.bfloat16)
    grad_factor_out = jnp.einsum(
        "jce,jcrd->erd", selector, ret_out, preferred_element_type=jnp.float32
    ).astype(jnp.bfloat16)
    return (input_grad, grad_factor_in, grad_factor_out, router_grad)


def solution(mesh):
    return jax.shard_map(
        body,
        mesh=mesh,
        in_specs=(
            P("adapter", "dp"),
            P("adapter", "dp"),
            P("adapter", None, "dp"),
            P("adapter", None, "dp"),
            P("adapter", None),
            P("adapter", None),
        ),
        out_specs=(
            P("adapter", "dp"),
            P("adapter", None, "dp"),
            P("adapter", None, "dp"),
            P("adapter", None),
        ),
        check_vma=False,
    )
```

profile of v0, /device:TPU:0, one launch (start us, length us, event | category | flops | bytes accessed | tf_op | source)
XLA Modules:
  0.0 328.2 jit_solution(13576167594300134911)
XLA Ops:
  7.2 22.7 %all-gather = s32[8,2,8]{2,1,0:T(2,128)S(1)} all-gather(s32[1,2,8]{2,1,0:T(2,128)} %bitcast.88), channel_id=1, replica_groups=mesh['dp'=4,'adapter'=8] {'adapter'}, dimensions={0}, use_global_device_ids=true | all-gather | bytes 576 | tf_op jit(solution)/shard_map/all_gather | solution.py:25
  29.9 0.1 reshape.272
  30.0 0.1 iota_compare_fusion
  30.1 0.3 convert_reduce_fusion
  30.4 0.1 and_reduce_fusion
  30.5 3.9 %fusion.6 = bf16[8,1,2,16,2048]{4,0,3,2,1:T(8,128)(2,1)S(1)} fusion(bf16[32,16,2048]{2,1,0:T(8,128)(2,1)} %param.9, pred[8,2,32,1]{2,1,0,3:T(4,128)(4,1)S(1)} %bitcast.86), kind=kOutput, calls=%fused_computation.15 | convolution fusion | flops 34078720 | bytes 3146240 | tf_op jit(solution)/shard_map/jce,erd->jcrd/dot_general | solution.py:44
  34.4 1.5 copy.58
  36.0 3.8 %all-to-all-start = ((bf16[8,1,2,16,2048]{4,3,2,1,0:T(8,128)(2,1)}), bf16[8,1,2,16,2048]{4,3,2,1,0:T(8,128)(2,1)S(1)}, u32[]{:S(2)}, u32[]{:S(2)}) async-start(bf16[8,1,2,16,2048]{4,3,2,1,0:T(8,128)(2,1)} %copy.58), calls=%async_computation | async-start | bytes 2097152 | tf_op jit(solution)/shard_map/all_to_all | solution.py:52
  39.8 11.1 %fusion = bf16[8,1,2,16,7168]{4,0,3,2,1:T(8,128)(2,1)S(1)} fusion(bf16[32,16,7168]{2,1,0:T(8,128)(2,1)} %param.8, pred[8,2,32,1]{2,1,0,3:T(4,128)(4,1)S(1)} %bitcast.87), kind=kOutput, calls=%fused_computation.5 | convolution fusion | flops 119275520 | bytes 11010560 | tf_op jit(solution)/shard_map/jce,erf->jcrf/dot_general | solution.py:41
  50.8 3.8 %copy.63 = bf16[8,1,2,16,7168]{4,3,2,1,0:T(8,128)(2,1)} copy(bf16[8,1,2,16,7168]{4,0,3,2,1:T(8,128)(2,1)S(1)} %fusion) | data formatting | bytes 7340032 | tf_op jit(solution)/shard_map/broadcast_in_dim | solution.py:51
  54.7 7.5 %all-to-all-done = bf16[8,1,2,16,2048]{4,3,2,1,0:T(8,128)(2,1)S(1)} async-done(((bf16[8,1,2,16,2048]{4,3,2,1,0:T(8,128)(2,1)}), bf16[8,1,2,16,2048]{4,3,2,1,0:T(8,128)(2,1)S(1)}, u32[]{:S(2)}, u32[]{:S(2)}) %all-to-all-start) | async-done | bytes 1048608 | tf_op jit(solution)/shard_map/all_to_all | solution.py:52
  62.1 4.5 %all-to-all-start.1 = ((bf16[8,1,2,16,7168]{4,3,2,1,0:T(8,128)(2,1)}), bf16[8,1,2,16,7168]{4,3,2,1,0:T(8,128)(2,1)}, u32[]{:S(2)}, u32[]{:S(2)}) async-start(bf16[8,1,2,16,7168]{4,3,2,1,0:T(8,128)(2,1)} %copy.63), calls=%async_computation.1 | async-start | bytes 7340032 | tf_op jit(solution)/shard_map/all_to_all | solution.py:51
  66.6 0.3 all-reduce.3.cloned.1.call-start
  66.9 0.1 reshape.273
  67.0 0.2 convert_reduce_fusion.1
  67.2 0.1 reduce_sum.38
  67.3 1.1 fusion.12
  68.5 0.8 copy.60
  69.2 77.2 %all-to-all-done.1 = bf16[8,1,2,16,7168]{4,3,2,1,0:T(8,128)(2,1)} async-done(((bf16[8,1,2,16,7168]{4,3,2,1,0:T(8,128)(2,1)}), bf16[8,1,2,16,7168]{4,3,2,1,0:T(8,128)(2,1)}, u32[]{:S(2)}, u32[]{:S(2)}) %all-to-all-start.1) | async-done | bytes 3670048 | tf_op jit(solution)/shard_map/all_to_all | solution.py:51
  146.4 6.3 %fusion.44 = bf16[16,16,2,256]{3,1,2,0:T(8,128)(2,1)S(1)} fusion(bf16[16,16,7168,1]{2,1,3,0:T(8,128)(2,1)} %bitcast.28, bf16[2,256,7168,1]{2,1,0,3:T(8,128)(2,1)} %bitcast.80), kind=kOutput, calls=%fused_computation.72 | convolution fusion | flops 1879048192 | bytes 11272192 | tf_op jit(solution)/shard_map/anirf,tf->anirt/dot_general | solution.py:55
  152.7 0.3 convolution_bitcast_fusion
  153.0 0.8 copy.73
  153.8 0.0 all-reduce.3.cloned.1.call-update
  153.8 0.1 broadcast_in_dim.7
  153.9 0.1 mul.34
  154.0 32.6 %all-reduce.3.cloned.1.call-done = (f32[2,256,128]{1,2,0:T(8,128)}, f32[2,256,128]{1,2,0:T(8,128)}) async-done(((f32[2,256,128]{1,2,0:T(8,128)}, f32[2,256,128]{1,2,0:T(8,128)}), (f32[2,256,128]{1,2,0:T(8,128)}, f32[2,256,128]{1,2,0:T(8,128)})) %all-reduce.3.cloned.1.call-update) | async-done | bytes 524304 | tf_op jit(solution)/shard_map/psum | solution.py:79
  186.5 1.4 convolution_convert_fusion.4
  188.0 1.2 convolution_convert_fusion.6
  189.2 0.7 reshape.283
  190.0 1.9 copy.75
  191.8 6.0 %all-to-all-start.3 = ((bf16[8,2,16,2048]{3,1,2,0:T(2,128)(2,1)}), bf16[8,2,16,2048]{3,1,2,0:T(2,128)(2,1)S(1)}, u32[]{:S(2)}, u32[]{:S(2)}) async-start(bf16[8,2,16,2048]{3,1,2,0:T(2,128)(2,1)} %copy.75), calls=%async_computation.3 | async-start | bytes 2097152 | tf_op jit(solution)/shard_map/all_to_all | solution.py:111
  197.8 4.3 %convolution_convert_fusion.1 = bf16[2,128,7168]{2,1,0:T(8,128)(2,1)S(1)} fusion(bf16[2,256,7168]{2,1,0:T(8,128)(2,1)} %bitcast.81, f32[2,256,128]{1,2,0:T(8,128)S(1)} %copy-done.2, f32[2,128]{1,0:T(2,128)S(1)} %mul.34), kind=kOutput, calls=%fused_computation.2 | convolution fusion | flops 941490176 | bytes 11273216 | tf_op jit(solution)/shard_map/blj,blf->bjf/dot_general | solution.py:89
  202.1 6.0 %convolution_convert_fusion.2 = bf16[16,16,7168]{2,0,1:T(8,128)(2,1)} fusion(bf16[16,16,7168]{2,1,0:T(8,128)(2,1)S(1)} %bitcast.79, s32[16]{0:T(128)S(1)} %multiply_add_fusion.1), kind=kOutput, calls=%fused_computation.3 | convolution fusion | flops 60555520 | bytes 7340096 | tf_op jit(solution)/shard_map/qs,qrf->srf/dot_general | solution.py:95
  208.1 8.1 %reshape.280 = bf16[8,2,16,7168]{3,1,0,2:T(2,128)(2,1)} reshape(bf16[16,16,7168]{2,0,1:T(8,128)(2,1)} %convolution_convert_fusion.2) | data formatting | bytes 7340032 | tf_op jit(solution)/shard_map/reshape | solution.py:107
  216.3 6.5 %copy.69 = bf16[8,2,16,7168]{3,1,2,0:T(2,128)(2,1)} copy(bf16[8,2,16,7168]{3,1,0,2:T(2,128)(2,1)} %reshape.280) | data formatting | bytes 7340032 | tf_op jit(solution)/shard_map/reshape | solution.py:107
  222.7 0.1 all-to-all-done.3
  222.8 6.0 %all-to-all-start.2 = ((bf16[8,2,16,7168]{3,1,2,0:T(2,128)(2,1)}), bf16[8,2,16,7168]{3,1,2,0:T(2,128)(2,1)}, u32[]{:S(2)}, u32[]{:S(2)}) async-start(bf16[8,2,16,7168]{3,1,2,0:T(2,128)(2,1)} %copy.69), calls=%async_computation.2 | async-start | bytes 7340032 | tf_op jit(solution)/shard_map/all_to_all | solution.py:110
  228.9 6.2 %convolution_convert_fusion.3 = bf16[16,16,7168]{2,0,1:T(8,128)(2,1)S(1)} fusion(bf16[16,16,7168]{2,1,0:T(8,128)(2,1)} %bitcast.17, s32[16]{0:T(128)S(1)} %multiply_add_fusion.1), kind=kOutput, calls=%fused_computation.4 | convolution fusion | flops 60555520 | bytes 7340096 | tf_op jit(solution)/shard_map/qs,srf->qrf/dot_general | solution.py:67
  235.1 3.8 %copy.66 = bf16[16,16,7168]{2,1,0:T(8,128)(2,1)} copy(bf16[16,16,7168]{2,0,1:T(8,128)(2,1)S(1)} %convolution_convert_fusion.3) | data formatting | bytes 7340032 | tf_op jit(solution)/shard_map/convert_element_type | solution.py:69
  238.9 0.1 multiply_reduce_fusion
  239.1 0.1 reduce_sum.40
  239.1 0.7 reduce_sum.41
  239.8 9.7 %fusion.23 = f32[2,256,7168]{2,1,0:T(8,128)} fusion(bf16[2,128,7168]{2,1,0:T(8,128)(2,1)} %bitcast.77, f32[2,256,128]{1,2,0:T(8,128)S(1)} %copy-done.2, f32[2,128]{1,0:T(2,128)S(1)} %mul.34), kind=kOutput, calls=%fused_computation.34 | convolution fusion | flops 939655168 | bytes 18613248 | tf_op jit(solution)/shard_map/blj,bjf->blf/dot_general | solution.py:86
  249.5 0.8 bitcast_convert_fusion.1
  250.3 2.5 copy.79
  252.8 56.5 %all-to-all-done.2 = bf16[8,2,16,7168]{3,1,2,0:T(2,128)(2,1)} async-done(((bf16[8,2,16,7168]{3,1,2,0:T(2,128)(2,1)}), bf16[8,2,16,7168]{3,1,2,0:T(2,128)(2,1)}, u32[]{:S(2)}, u32[]{:S(2)}) %all-to-all-start.2) | async-done | bytes 3670048 | tf_op jit(solution)/shard_map/all_to_all | solution.py:110
  309.3 4.8 %bitcast_convert_fusion = bf16[32,16,7168]{2,0,1:T(8,128)(2,1)S(1)} fusion(bf16[8,2,16,7168]{3,1,2,0:T(2,128)(2,1)} %all-to-all-done.2, pred[8,2,32]{2,1,0:T(4,128)(4,1)S(1)} %and_reduce_fusion), kind=kOutput, calls=%fused_computation | convolution fusion | flops 121110528 | bytes 11010560 | tf_op jit(solution)/shard_map/jce,jcrf->erf/dot_general | solution.py:113
  314.1 7.1 %copy.78 = bf16[32,16,7168]{2,1,0:T(8,128)(2,1)} copy(bf16[32,16,7168]{2,0,1:T(8,128)(2,1)S(1)} %bitcast_convert_fusion) | data formatting | bytes 14680064
  (19 shorter events, 0.1 us)
Async XLA Ops:
  7.2 60.2 %copy-start = (bf16[512,2048]{1,0:T(8,128)(2,1)S(1)}, bf16[512,2048]{1,0:T(8,128)(2,1)}, u32[]{:S(2)}) copy-start(bf16[512,2048]{1,0:T(8,128)(2,1)} %param.7) | copy-start | bytes 6291460
  36.0 26.1 %all-to-all-start = ((bf16[8,1,2,16,2048]{4,3,2,1,0:T(8,128)(2,1)}), bf16[8,1,2,16,2048]{4,3,2,1,0:T(8,128)(2,1)S(1)}, u32[]{:S(2)}, u32[]{:S(2)}) async-start(bf16[8,1,2,16,2048]{4,3,2,1,0:T(8,128)(2,1)} %copy.58), calls=%async_computation | async-start | bytes 2097152 | tf_op jit(solution)/shard_map/all_to_all | solution.py:52
  54.7 12.3 %copy-start.4 = (s32[2,8]{1,0:T(2,128)S(1)}, s32[2,8]{1,0:T(2,128)}, u32[]{:S(2)}) copy-start(s32[2,8]{1,0:T(2,128)} %param.10) | copy-start | bytes 196
  62.1 84.3 %all-to-all-start.1 = ((bf16[8,1,2,16,7168]{4,3,2,1,0:T(8,128)(2,1)}), bf16[8,1,2,16,7168]{4,3,2,1,0:T(8,128)(2,1)}, u32[]{:S(2)}, u32[]{:S(2)}) async-start(bf16[8,1,2,16,7168]{4,3,2,1,0:T(8,128)(2,1)} %copy.63), calls=%async_computation.1 | async-start | bytes 7340032 | tf_op jit(solution)/shard_map/all_to_all | solution.py:51
  66.6 119.9 %all-reduce.3.cloned.1.call-start = ((), (), s32[]{:S(2)}) async-start(), calls=%async_computation.4 | async-start | bytes 1048576 | tf_op jit(solution)/shard_map/psum | solution.py:79
  146.4 7.4 %copy-start.5 = (f32[2,8]{1,0:T(2,128)S(1)}, f32[2,8]{1,0:T(2,128)}, u32[]{:S(2)}) copy-start(f32[2,8]{1,0:T(2,128)} %param.11) | copy-start | bytes 196
  189.2 8.6 %copy-start.2 = (f32[2,256,128]{1,2,0:T(8,128)S(1)}, f32[2,256,128]{1,2,0:T(8,128)}, u32[]{:S(2)}) copy-start(f32[2,256,128]{1,2,0:T(8,128)} %get-tuple-element.20) | copy-start | bytes 786436
  191.8 31.0 %all-to-all-start.3 = ((bf16[8,2,16,2048]{3,1,2,0:T(2,128)(2,1)}), bf16[8,2,16,2048]{3,1,2,0:T(2,128)(2,1)S(1)}, u32[]{:S(2)}, u32[]{:S(2)}) async-start(bf16[8,2,16,2048]{3,1,2,0:T(2,128)(2,1)} %copy.75), calls=%async_computation.3 | async-start | bytes 2097152 | tf_op jit(solution)/shard_map/all_to_all | solution.py:111
  222.8 86.5 %all-to-all-start.2 = ((bf16[8,2,16,7168]{3,1,2,0:T(2,128)(2,1)}), bf16[8,2,16,7168]{3,1,2,0:T(2,128)(2,1)}, u32[]{:S(2)}, u32[]{:S(2)}) async-start(bf16[8,2,16,7168]{3,1,2,0:T(2,128)(2,1)} %copy.69), calls=%async_computation.2 | async-start | bytes 7340032 | tf_op jit(solution)/shard_map/all_to_all | solution.py:110
  235.1 3.9 %copy-start.3 = (f32[2,256,128]{1,2,0:T(8,128)S(1)}, f32[2,256,128]{1,2,0:T(8,128)}, u32[]{:S(2)}) copy-start(f32[2,256,128]{1,2,0:T(8,128)} %get-tuple-element.21) | copy-start | bytes 786436
  314.1 7.1 %copy-start.1 = (bf16[512,2048]{1,0:T(8,128)(2,1)S(1)}, bf16[512,2048]{1,0:T(8,128)(2,1)}, u32[]{:S(2)}) copy-start(bf16[512,2048]{1,0:T(8,128)(2,1)} %param.7) | copy-start | bytes 6291460
Sparse Core Ops, SparseCore 0:
  153.9 32.5 all-reduce.2
where the time goes:
time: 332 us; the launch traced here: 328 us
  waiting for transfers between devices  174 us (52%)
  matrix products  57.2 us (17%)
  local copies, waits for them, and re-layouts  38 us (11%)
  blocking collectives  22.7 us (7%)
  starting transfers between devices  20.6 us (6%)
  between operations  14.5 us (4%)
    all_to_all x1, waiting for transfers between devices, body(): lax.all_to_all(send_in[:, None], 'adapter', split_axis=0, concat_axis=1,...  77.2 us
    all_to_all x1, waiting for transfers between devices, body(): lax.all_to_all(back_in, 'adapter', split_axis=0, concat_axis=0, tiled=True)  56.5 us
    psum x1, waiting for transfers between devices, body(): projected, pulled = lax.psum((part_proj, part_pull), 'dp')  32.6 us
    all_gather x1, blocking collectives, body(): lax.all_gather(adapter_ids, 'adapter', axis=0, tiled=True)  22.7 us
    reshape x2, local copies, waits for them, and re-layouts, body(): back_in = back_in.reshape(owner_count, CAP, rank_width, -1)  14.6 us
    dot_general x1, matrix products, body(): jnp.einsum('jce,erf->jcrf', selector, factor_in, preferred_element_type=j...  11.1 us
    dot_general x1, matrix products, body(): jnp.einsum('blj,bjf->blf', pulled_weighted, pair_in, preferred_element_ty...  9.67 us
    unnamed x14, local copies, waits for them, and re-layouts  9.57 us
  transfers between devices with their start and end apart: 5, of which 5 were waited for; matrix products, arithmetic and copies ran while one was open for 20% of the time, Pallas kernels for 0%

commit v1 on v0

v1 whole, which is shorter than its diff:
```python
import functools
import math

import jax
import jax.numpy as jnp
from jax import lax
from jax.experimental import pallas as pl
from jax.experimental.pallas import tpu as pltpu
from jax.sharding import PartitionSpec as P


CAP = 2
BF = jnp.bfloat16
F32 = jnp.float32
ANY = pl.BlockSpec(memory_space=pl.ANY)
SMEM = pl.BlockSpec(memory_space=pltpu.SMEM)


def swap(x, axis, count, offset):
    return lax.ppermute(x, axis, [(i, i ^ offset) for i in range(count)])


def pick_kernel(groups, me_ref, ids_ref, fin, fout, table_ref, *refs):
    outs = refs[:groups]
    hold, in_sem, out_sem = refs[groups:]
    exp_count, rank, wide = fin.shape
    base = me_ref[0] * exp_count
    loads = []
    for m in range(groups):
        found = jnp.int32(0)
        picks = [jnp.int32(-1)] * CAP
        for b in range(ids_ref.shape[1]):
            for k in range(ids_ref.shape[2]):
                local = ids_ref[m, b, k] - base
                mine = (local >= 0) & (local < exp_count)
                for c in range(CAP):
                    picks[c] = jnp.where(mine & (found == c), local, picks[c])
                found = found + mine.astype(jnp.int32)
        for c in range(CAP):
            table_ref[m, c] = picks[c]
            e = jnp.maximum(picks[c], 0)
            rows = pl.ds(c * rank, rank)
            one = pltpu.make_async_copy(
                fin.at[e], hold.at[m, rows, pl.ds(0, wide)], in_sem.at[m, c, 0]
            )
            two = pltpu.make_async_copy(
                fout.at[e], hold.at[m, rows, pl.ds(wide, fout.shape[2])], in_sem.at[m, c, 1]
            )
            one.start()
            two.start()
            loads.append((one, two))
    stores = []
    for m in range(groups):
        for c in range(CAP):
            for load in loads[m * CAP + c]:
                load.wait()
        store = pltpu.make_async_copy(hold.at[m], outs[m], out_sem.at[m])
        store.start()
        stores.append(store)
    for store in stores:
        store.wait()


def project_kernel(groups, in_tiles, tiles, mask_ref, x_ref, g_ref, *refs):
    pieces = refs[:groups]
    out_ref, rows, total = refs[groups:]
    i = pl.program_id(0)
    rank = pieces[0].shape[0]
    for d in range(groups):
        rows[pl.ds(d * rank, rank), :] = pieces[d][...]
    dims = (((1,), (1,)), ((), ()))

    def add(side, data_ref, first):
        part = lax.dot_general(data_ref[...], rows[...], dims, preferred_element_type=F32)

        @pl.when(first)
        def _():
            total[side] = part

        @pl.when(jnp.logical_not(first))
        def _():
            total[side] += part

    @pl.when(i < in_tiles)
    def _():
        add(0, x_ref, i == 0)

    @pl.when(i >= in_tiles)
    def _():
        add(1, g_ref, i == in_tiles)

    @pl.when(i == tiles - 1)
    def _():
        length = out_ref.shape[1]
        for side in range(2):
            acc = jnp.zeros(out_ref.shape[1:], F32)
            for b in range(mask_ref.shape[0]):
                part = total[side, pl.ds(b * length, length), :]
                acc = jnp.where(mask_ref[b : b + 1, :] > 0, part, acc)
            out_ref[side] = acc


def term_kernel(groups, in_tiles, sums_ref, weight_ref, x_ref, g_ref, *refs):
    outs = refs[:groups]
    weighted_ref, pulled, projected = refs[groups:]
    i = pl.program_id(0)
    rank = outs[0].shape[0]

    @pl.when(i == 0)
    def _():
        length = sums_ref.shape[1]
        for b in range(weight_ref.shape[0]):
            w = weight_ref[b : b + 1, :]
            span = pl.ds(b * length, length)
            part = sums_ref[1] * w
            weighted_ref[span, :] = part.astype(BF)
            pulled[:, span] = part.T.astype(BF)
            projected[:, span] = (sums_ref[0] * w).T.astype(BF)

    @pl.when(i < in_tiles)
    def _():
        part = jnp.dot(pulled[...], x_ref[...], preferred_element_type=F32).astype(BF)
        for d in range(groups):
            outs[d][...] = part[d * rank : (d + 1) * rank]

    @pl.when(i >= in_tiles)
    def _():
        part = jnp.dot(projected[...], g_ref[...], preferred_element_type=F32).astype(BF)
        for d in range(groups):
            outs[d][...] = part[d * rank : (d + 1) * rank]


def input_kernel(chunks, count, *refs):
    weighted = refs[:chunks]
    pieces = refs[chunks : chunks + count]
    out_ref, rows, left = refs[chunks + count :]
    rank = pieces[0].shape[0]
    half = weighted[0].shape[1]

    @pl.when(pl.program_id(0) == 0)
    def _():
        for c in range(chunks):
            left[:, pl.ds(c * half, half)] = weighted[c][...]

    for m in range(count):
        rows[pl.ds(m * rank, rank), :] = pieces[m][...]
    out_ref[...] = jnp.dot(left[...], rows[...], preferred_element_type=F32)


def place(refs, m, rank):
    return refs[m // CAP].at[pl.ds((m % CAP) * rank, rank), :]


def collect_kernel(count, table_ref, *refs):
    pieces = refs[: count // CAP]
    in_ref, out_ref, total = refs[count // CAP :]
    block, rank, wide = in_ref.shape
    for s in range(block):
        e = pl.program_id(0) * block + s
        total[...] = jnp.zeros_like(total)
        for m in range(count):

            @pl.when(table_ref[m] == e)
            def _():
                total[...] += place(pieces, m, rank)[...].astype(F32)

        in_ref[s] = total[:, :wide].astype(BF)
        out_ref[s] = total[:, wide:].astype(BF)


def finish_kernel(late, early, late_ref, early_ref, *refs):
    a, b = late // CAP, early // CAP
    late_hbm, early_hbm = refs[:a], refs[a : a + b]
    in_hbm, out_hbm, held, kept, stage, total, held_sem, kept_sem, out_sem = refs[a + b + 2 :]
    rank, full = total.shape
    wide = in_hbm.shape[2]

    def used(m):
        hit = late_ref[0] == early_ref[m]
        for s in range(1, late):
            hit = hit | (late_ref[s] == early_ref[m])
        return hit & (early_ref[m] >= 0)

    def first(s):
        fresh = late_ref[s] >= 0
        for r in range(s):
            fresh = fresh & (late_ref[r] != late_ref[s])
        return fresh

    def load_late(j):
        return pltpu.make_async_copy(late_hbm[j], held.at[j], held_sem.at[j])

    def load_early(m):
        return pltpu.make_async_copy(place(early_hbm, m, rank), kept.at[m], kept_sem.at[m])

    def stores(s):
        e = jnp.maximum(late_ref[s], 0)
        return (
            pltpu.make_async_copy(stage.at[s, :, pl.ds(0, wide)], in_hbm.at[e], out_sem.at[s, 0]),
            pltpu.make_async_copy(
                stage.at[s, :, pl.ds(wide, full - wide)], out_hbm.at[e], out_sem.at[s, 1]
            ),
        )

    for j in range(a):
        load_late(j).start()
    for m in range(early):

        @pl.when(used(m))
        def _():
            load_early(m).start()

    for j in range(a):
        load_late(j).wait()
    for s in range(late):

        @pl.when(first(s))
        def _():
            total[...] = held[s // CAP, pl.ds((s % CAP) * rank, rank), :].astype(F32)
            for r in range(s + 1, late):

                @pl.when(late_ref[r] == late_ref[s])
                def _():
                    total[...] += held[r // CAP, pl.ds((r % CAP) * rank, rank), :].astype(F32)

            for m in range(early):

                @pl.when(late_ref[s] == early_ref[m])
                def _():
                    load_early(m).wait()
                    total[...] += kept[m].astype(F32)

            stage[s] = total[...].astype(BF)
            for store in stores(s):
                store.start()

    for s in range(late):

        @pl.when(first(s))
        def _():
            for store in stores(s):
                store.wait()


def body(activations, cotangent, factor_in, factor_out, adapter_ids, router_weights):
    groups = lax.axis_size("adapter")
    dp = lax.axis_size("dp")
    me = lax.axis_index("adapter")
    exp_count, rank, wide = factor_in.shape
    narrow = factor_out.shape[2]
    req_count, top_count = adapter_ids.shape
    pair_count = req_count * top_count
    tokens = activations.shape[0]
    length = tokens // req_count
    full = wide + narrow
    tile = math.gcd(wide, narrow)
    in_tiles, tiles = wide // tile, full // tile
    me_arr = me.astype(jnp.int32).reshape(1)
    both = CAP * rank
    piece = jax.ShapeDtypeStruct((both, full), BF)

    def pick(lists):
        count = lists.shape[0]
        return pl.pallas_call(
            functools.partial(pick_kernel, count),
            out_shape=[jax.ShapeDtypeStruct((count, CAP), jnp.int32)] + [piece] * count,
            in_specs=[SMEM, SMEM, ANY, ANY],
            out_specs=[SMEM] + [ANY] * count,
            scratch_shapes=[
                pltpu.VMEM((count, both, full), BF),
                pltpu.SemaphoreType.DMA((count, CAP, 2)),
                pltpu.SemaphoreType.DMA((count,)),
            ],
        )(me_arr, lists, factor_in, factor_out)

    steps = [groups >> (i + 1) for i in range(groups.bit_length() - 1)]
    lists, known = adapter_ids[None], [0]
    slot_table, sent, got = {}, {}, {}
    arrivals = []
    for step in steps:
        fresh = swap(lists, "adapter", groups, step)
        arrivals.append(([d ^ step for d in known], fresh))
        lists = jnp.concatenate([lists, fresh], axis=0)
        known = known + [d ^ step for d in known]
    arrivals.append(([0], adapter_ids[None]))
    for which, fresh in arrivals:
        picked = pick(fresh)
        for m, d in enumerate(which):
            slot_table[d] = picked[0][m]
            sent[d] = picked[1 + m]
    last = steps[-1]
    chunks = [
        [d for d in known if not d & last],
        [d for d in known if d & last],
    ]
    chunks = [sorted(c, key=lambda d: (d >= groups // 2, d)) for c in chunks]
    for chunk in chunks:
        for d in chunk:
            got[d] = sent[d] if d == 0 else swap(sent[d], "adapter", groups, d)

    my_pairs = adapter_ids.reshape(pair_count)
    my_owner = my_pairs // exp_count
    order = jnp.arange(pair_count)
    before = order[:, None] > order[None, :]
    my_slot = jnp.sum((my_owner[:, None] == my_owner[None, :]) & before, axis=1)
    far = jnp.array([d for c in chunks for d in c], jnp.int32) ^ me
    chosen = (
        (my_owner[None, None, :] == far[:, None, None])
        & (my_slot[None, None, :] == jnp.arange(CAP)[None, :, None])
    ).astype(F32)
    by_request = chosen.reshape(groups * CAP, req_count, top_count)
    mask = jnp.repeat(jnp.sum(by_request, axis=2).T, rank, axis=1)
    weight = jnp.repeat(jnp.sum(by_request * router_weights[None], axis=2).T, rank, axis=1)

    rows = len(chunks[0]) * both
    x_spec = pl.BlockSpec((tokens, tile), lambda i: (0, jnp.minimum(i, in_tiles - 1)))
    g_spec = pl.BlockSpec((tokens, tile), lambda i: (0, jnp.maximum(i - in_tiles, 0)))
    piece_spec = pl.BlockSpec((both, tile), lambda i: (0, i))
    small = pl.BlockSpec((req_count, rows), lambda i: (0, 0))
    sums_spec = pl.BlockSpec((2, length, rows), lambda i: (0, 0, 0))
    weighted_spec = pl.BlockSpec((tokens, rows), lambda i: (0, 0))

    back, weighted, sums = {}, [], []
    for n, chunk in enumerate(chunks):
        count = len(chunk)
        my_mask = mask[:, n * rows : (n + 1) * rows]
        if n:
            my_mask, weighted[-1] = lax.optimization_barrier((my_mask, weighted[-1]))
        part = pl.pallas_call(
            functools.partial(project_kernel, count, in_tiles, tiles),
            out_shape=jax.ShapeDtypeStruct((2, length, rows), F32),
            grid=(tiles,),
            in_specs=[small, x_spec, g_spec] + [piece_spec] * count,
            out_specs=sums_spec,
            scratch_shapes=[pltpu.VMEM((rows, tile), BF), pltpu.VMEM((2, tokens, rows), F32)],
        )(my_mask, activations, cotangent, *[got[d] for d in chunk])
        step = 1
        while step < dp:
            part = part + swap(part, "dp", dp, step)
            step *= 2
        done = pl.pallas_call(
            functools.partial(term_kernel, count, in_tiles),
            out_shape=[piece] * count + [jax.ShapeDtypeStruct((tokens, rows), BF)],
            grid=(tiles,),
            in_specs=[sums_spec, small, x_spec, g_spec],
            out_specs=[piece_spec] * count + [weighted_spec],
            scratch_shapes=[pltpu.VMEM((rows, tokens), BF)] * 2,
        )(part, weight[:, n * rows : (n + 1) * rows], activations, cotangent)
        sums.append(part)
        weighted.append(done[-1])
        for m, d in enumerate(chunk):
            back[d] = done[m] if d == 0 else swap(done[m], "adapter", groups, d)

    everything = [d for c in chunks for d in c]
    input_grad = pl.pallas_call(
        functools.partial(input_kernel, len(chunks), groups),
        out_shape=jax.ShapeDtypeStruct((tokens, wide), F32),
        grid=(in_tiles,),
        in_specs=[weighted_spec] * len(chunks) + [piece_spec] * groups,
        out_specs=pl.BlockSpec((tokens, tile), lambda i: (0, i)),
        scratch_shapes=[
            pltpu.VMEM((groups * both, tile), BF),
            pltpu.VMEM((tokens, len(chunks) * rows), BF),
        ],
        name="input",
    )(*weighted, *[got[d] for d in everything])

    per_slot = jnp.concatenate([jnp.sum(s[0] * s[1], axis=0) for s in sums])
    per_slot = jnp.sum(per_slot.reshape(groups * CAP, rank), axis=1)
    router_grad = jnp.sum(by_request * per_slot[:, None, None], axis=0)

    tables = [jnp.concatenate([slot_table[d] for d in c]) for c in chunks]
    early, late = len(chunks[0]) * CAP, len(chunks[1]) * CAP
    block = math.gcd(exp_count, 4)
    grads = [
        jax.ShapeDtypeStruct(factor_in.shape, BF),
        jax.ShapeDtypeStruct(factor_out.shape, BF),
    ]
    grads = pl.pallas_call(
        functools.partial(collect_kernel, early),
        out_shape=grads,
        grid=(exp_count // block,),
        in_specs=[SMEM] + [pl.BlockSpec(memory_space=pltpu.VMEM)] * len(chunks[0]),
        out_specs=[
            pl.BlockSpec((block, rank, wide), lambda i: (i, 0, 0)),
            pl.BlockSpec((block, rank, narrow), lambda i: (i, 0, 0)),
        ],
        scratch_shapes=[pltpu.VMEM((rank, full), F32)],
        name="collect",
    )(tables[0], *[back[d] for d in chunks[0]])
    grad_factor_in, grad_factor_out = pl.pallas_call(
        functools.partial(finish_kernel, late, early),
        out_shape=[jax.ShapeDtypeStruct(g.shape, BF) for g in grads],
        in_specs=[SMEM] * 2 + [ANY] * (groups + 2),
        out_specs=[ANY] * 2,
        scratch_shapes=[
            pltpu.VMEM((len(chunks[1]), both, full), BF),
            pltpu.VMEM((early, rank, full), BF),
            pltpu.VMEM((late, rank, full), BF),
            pltpu.VMEM((rank, full), F32),
            pltpu.SemaphoreType.DMA((len(chunks[1]),)),
            pltpu.SemaphoreType.DMA((early,)),
            pltpu.SemaphoreType.DMA((late, 2)),
        ],
        input_output_aliases={groups + 2: 0, groups + 3: 1},
        name="finish",
    )(tables[1], tables[0], *[back[d] for d in chunks[1]], *[back[d] for d in chunks[0]], *grads)
    return (input_grad, grad_factor_in, grad_factor_out, router_grad)


def solution(mesh):
    return jax.shard_map(
        body,
        mesh=mesh,
        in_specs=(
            P("adapter", "dp"),
            P("adapter", "dp"),
            P("adapter", None, "dp"),
            P("adapter", None, "dp"),
            P("adapter", None),
            P("adapter", None),
        ),
        out_specs=(
            P("adapter", "dp"),
            P("adapter", None, "dp"),
            P("adapter", None, "dp"),
            P("adapter", None),
        ),
        check_vma=False,
    )
```

time: 332 us -> 235 us (0.71)
  the two profiles are of different devices: /device:TPU:0 before, /device:TPU:22 now
where the time goes in v1:
time: 235 us; the launch traced here: 234 us
  waiting for transfers between devices  119 us (51%)
  Pallas kernels  76.1 us (32%)
  starting transfers between devices  24.2 us (10%)
  other arithmetic  6.86 us (3%)
  local copies, waits for them, and re-layouts  6.28 us (3%)
    ppermute x21, waiting for transfers between devices, swap(): return lax.ppermute(x, axis, [(i, i ^ offset) for i in range(count)])  119 us
    ppermute x21, starting transfers between devices, swap(): return lax.ppermute(x, axis, [(i, i ^ offset) for i in range(count)])  24.2 us
    pallas_call x2, Pallas kernels, body(): pl.pallas_call(functools.partial(project_kernel, count, in_tiles, tiles),...  19.8 us
    pallas_call x2, Pallas kernels, body(): pl.pallas_call(functools.partial(term_kernel, count, in_tiles), out_shape...  19.5 us
    pallas_call x4, Pallas kernels, pick(): pl.pallas_call(functools.partial(pick_kernel, count), out_shape=[jax.Shap...  14.3 us
    pallas_call x1, Pallas kernels, body(): pl.pallas_call(functools.partial(input_kernel, len(chunks), groups), out_...  9.47 us
    pallas_call x1, Pallas kernels, body(): pl.pallas_call(functools.partial(collect_kernel, early), out_shape=grads,...  8.2 us
    pallas_call x1, Pallas kernels, body(): pl.pallas_call(functools.partial(finish_kernel, late, early), out_shape=[...  4.94 us
  transfers between devices with their start and end apart: 21, of which 13 were waited for; matrix products, arithmetic and copies ran while one was open for 4% of the time, Pallas kernels for 30%

profile of v1, /device:TPU:22, one launch (start us, length us, event | category | flops | bytes accessed | tf_op | source)
XLA Modules:
  0.0 233.6 jit_solution(3371859491243370554)
XLA Ops:
  1.0 0.8 reshape.172
  2.0 0.7 broadcast_xor_fusion
  2.8 2.6 %collective-permute-done.ids_ref = s32[1,2,8]{2,1,0:T(2,128)S(1)} collective-permute-done((s32[1,2,8]{2,1,0:T(2,128)}, s32[1,2,8]{2,1,0:T(2,128)S(1)}, u32[]{:S(2)}, u32[]{:S(2)}) %collective-permute-start) | collective-permute-done | bytes 96 | tf_op jit(solution)/shard_map/ppermute | solution.py:20
  5.4 0.7 pad_add_fusion.1
  6.1 1.6 collective-permute-start.1
  7.6 3.3 %shard_map.104 = (s32[1,2]{1,0:T(1,128)}, bf16[32,9216]{1,0:T(8,128)(2,1)}) custom-call(s32[1]{0:T(128)} %bitcast.1.me_ref, s32[1,2,8]{2,1,0:T(2,128)} %copy-done.12, bf16[32,16,7168]{2,1,0:T(8,128)(2,1)} %fin.7, bf16[32,16,2048]{2,1,0:T(8,128)(2,1)} %fout.7), custom_call_target="tpu_custom_call" | custom-call | tf_op jit(solution)/shard_map/pallas_call | solution.py:264
  11.4 0.6 copy-done.14
  12.0 3.6 %shard_map.103 = (s32[2,2]{1,0:T(2,128)}, bf16[32,9216]{1,0:T(8,128)(2,1)}, bf16[32,9216]{1,0:T(8,128)(2,1)}) custom-call(s32[1]{0:T(128)} %bitcast.1.me_ref, s32[2,2,8]{2,1,0:T(2,128)} %copy-done.14, bf16[32,16,7168]{2,1,0:T(8,128)(2,1)} %fin.7, bf16[32,16,2048]{2,1,0:T(8,128)(2,1)} %fout.7), custom_call_target="tpu_custom_call" | custom-call | tf_op jit(solution)/shard_map/pallas_call | solution.py:264
  16.1 2.7 %collective-permute-start.4 = (bf16[32,9216]{1,0:T(8,128)(2,1)}, bf16[32,9216]{1,0:T(8,128)(2,1)S(1)}, u32[]{:S(2)}, u32[]{:S(2)}) collective-permute-start(bf16[32,9216]{1,0:T(8,128)(2,1)} %get-tuple-element.35), channel_id=1, source_target_pairs={{0,6},{1,7},{2,4},{3,5},{4,2},{5,3},{6,0},{7,1},{8,14},{9,15},{10,... | collective-permute-start | bytes 1769480 | tf_op jit(solution)/shard_map/ppermute | solution.py:20
  19.0 0.7 pad_add_fusion
  20.5 2.8 %collective-permute-done.7.ids_ref = s32[4,2,8]{2,1,0:T(2,128)S(1)} collective-permute-done((s32[4,2,8]{2,1,0:T(2,128)S(1)}, s32[4,2,8]{2,1,0:T(2,128)S(1)}, u32[]{:S(2)}, u32[]{:S(2)}) %collective-permute-start.7) | collective-permute-done | bytes 288 | tf_op jit(solution)/shard_map/ppermute | solution.py:20
  23.3 0.6 copy-done.15
  23.9 4.1 %shard_map.107 = (s32[4,2]{1,0:T(4,128)}, bf16[32,9216]{1,0:T(8,128)(2,1)}, bf16[32,9216]{1,0:T(8,128)(2,1)}, bf16[32,9216]{1,0:T(8,128)(2,1)}, bf16[32,9216]{1,0:T(8,128)(2,1)}) custom-call(s32[1]{0:T(128)} %bitcast.1.me_ref, s32[4,2,8]{2,1,0:T(2,128)} %copy-done.15, bf16[32,16,7168]{2,1,0:T(8,128)(2,1)} %fin.7, bf16[32,16,2048]{2,1,0:T(8,128)(2,1)} %fout.7), custom_call_target="tpu_custom_call" | custom-call | tf_op jit(solution)/shard_map/pallas_call | solution.py:264
  28.1 0.6 collective-permute-start.8
  29.2 3.2 %shard_map.102 = (s32[1,2]{1,0:T(1,128)}, bf16[32,9216]{1,0:T(8,128)(2,1)}) custom-call(s32[1]{0:T(128)} %bitcast.1.me_ref, s32[1,2,8]{2,1,0:T(2,128)} %bitcast.22, bf16[32,16,7168]{2,1,0:T(8,128)(2,1)} %fin.7, bf16[32,16,2048]{2,1,0:T(8,128)(2,1)} %fout.7), custom_call_target="tpu_custom_call" | custom-call | tf_op jit(solution)/shard_map/pallas_call | solution.py:264
  32.5 2.3 %collective-permute-start.9 = (bf16[32,9216]{1,0:T(8,128)(2,1)}, bf16[32,9216]{1,0:T(8,128)(2,1)}, u32[]{:S(2)}, u32[]{:S(2)}) collective-permute-start(bf16[32,9216]{1,0:T(8,128)(2,1)} %get-tuple-element.40), channel_id=1, source_target_pairs={{0,3},{1,2},{2,1},{3,0},{4,7},{5,6},{6,5},{7,4},{8,11},{9,10},{10,... | collective-permute-start | bytes 1769480 | tf_op jit(solution)/shard_map/ppermute | solution.py:20
  34.8 3.0 %collective-permute-done.3.refs_2_.refs_4_ = bf16[32,9216]{1,0:T(8,128)(2,1)S(1)} collective-permute-done((bf16[32,9216]{1,0:T(8,128)(2,1)}, bf16[32,9216]{1,0:T(8,128)(2,1)S(1)}, u32[]{:S(2)}, u32[]{:S(2)}) %collective-permute-start.3) | collective-permute-done | bytes 589856 | tf_op jit(solution)/shard_map/ppermute | solution.py:20
  37.8 3.5 %collective-permute-start.10 = (bf16[32,9216]{1,0:T(8,128)(2,1)}, bf16[32,9216]{1,0:T(8,128)(2,1)}, u32[]{:S(2)}, u32[]{:S(2)}) collective-permute-start(bf16[32,9216]{1,0:T(8,128)(2,1)} %get-tuple-element.41), channel_id=1, source_target_pairs={{0,5},{1,4},{2,7},{3,6},{4,1},{5,0},{6,3},{7,2},{8,13},{9,12},{10,... | collective-permute-start | bytes 1769480 | tf_op jit(solution)/shard_map/ppermute | solution.py:20
  41.3 12.9 %collective-permute-done.2.refs_1_.refs_3_ = bf16[32,9216]{1,0:T(8,128)(2,1)S(1)} collective-permute-done((bf16[32,9216]{1,0:T(8,128)(2,1)}, bf16[32,9216]{1,0:T(8,128)(2,1)S(1)}, u32[]{:S(2)}, u32[]{:S(2)}) %collective-permute-start.2) | collective-permute-done | bytes 589856 | tf_op jit(solution)/shard_map/ppermute | solution.py:20
  54.3 3.7 %collective-permute-start.11 = (bf16[32,9216]{1,0:T(8,128)(2,1)S(1)}, bf16[32,9216]{1,0:T(8,128)(2,1)}, u32[]{:S(2)}, u32[]{:S(2)}) collective-permute-start(bf16[32,9216]{1,0:T(8,128)(2,1)S(1)} %copy-done.21), channel_id=1, source_target_pairs={{0,7},{1,6},{2,5},{3,4},{4,3},{5,2},{6,1},{7,0},{8,15},{9,14},{10,... | collective-permute-start | bytes 1769480 | tf_op jit(solution)/shard_map/ppermute | solution.py:20
  58.0 8.4 %collective-permute-done.4.refs_3_.refs_5_ = bf16[32,9216]{1,0:T(8,128)(2,1)S(1)} collective-permute-done((bf16[32,9216]{1,0:T(8,128)(2,1)}, bf16[32,9216]{1,0:T(8,128)(2,1)S(1)}, u32[]{:S(2)}, u32[]{:S(2)}) %collective-permute-start.4) | collective-permute-done | bytes 589856 | tf_op jit(solution)/shard_map/ppermute | solution.py:20
  66.4 0.8 copy-done.5
  67.2 9.9 %shard_map.105 = f32[2,256,128]{2,1,0:T(8,128)} custom-call(f32[2,128]{1,0:T(2,128)} %get-tuple-element.68.mask_ref, bf16[512,7168]{1,0:T(8,128)(2,1)} %x_ref.7, bf16[512,2048]{1,0:T(8,128)(2,1)} %g_ref.7, bf16[32,9216]{1,0:T(8,128)(2,1)} %get-tuple-element.32.refs_0_.refs_2_, bf16[32,9216]{1,0:T(8,128)(2,1)} %copy-done.4, bf16[32,9216]{1,0:T(8,128)(2,1)} %copy-done.3, ...), custom_call_target="tpu_custom_call" | custom-call | tf_op jit(solution)/shard_map/pallas_call | solution.py:329
  77.1 1.7 collective-permute-done.5
  78.8 1.0 add.25
  81.2 7.0 %collective-permute-done.6 = f32[2,256,128]{2,1,0:T(8,128)S(1)} collective-permute-done((f32[2,256,128]{2,1,0:T(8,128)S(1)}, f32[2,256,128]{2,1,0:T(8,128)S(1)}, u32[]{:S(2)}, u32[]{:S(2)}) %collective-permute-start.6) | collective-permute-done | bytes 262176 | tf_op jit(solution)/shard_map/ppermute | solution.py:20
  88.2 0.7 add.26.sums_ref
  89.0 9.7 %shard_map.106 = (bf16[32,9216]{1,0:T(8,128)(2,1)}, bf16[32,9216]{1,0:T(8,128)(2,1)}, bf16[32,9216]{1,0:T(8,128)(2,1)}, bf16[32,9216]{1,0:T(8,128)(2,1)}, bf16[512,128]{1,0:T(8,128)(2,1)}) custom-call(f32[2,256,128]{2,1,0:T(8,128)} %add.26.sums_ref, f32[2,128]{1,0:T(2,128)} %get-tuple-element.67.weight_ref, bf16[512,7168]{1,0:T(8,128)(2,1)} %x_ref.7, ...), custom_call_target="tpu_custom_call" | custom-call | tf_op jit(solution)/shard_map/pallas_call | solution.py:341
  98.8 0.8 collective-permute-start.19
  99.5 40.3 %collective-permute-done.11.refs_3_.refs_9_ = bf16[32,9216]{1,0:T(8,128)(2,1)} collective-permute-done((bf16[32,9216]{1,0:T(8,128)(2,1)S(1)}, bf16[32,9216]{1,0:T(8,128)(2,1)}, u32[]{:S(2)}, u32[]{:S(2)}) %collective-permute-start.11) | collective-permute-done | bytes 589856 | tf_op jit(solution)/shard_map/ppermute | solution.py:20
  139.8 10.0 %shard_map.108 = f32[2,256,128]{2,1,0:T(8,128)} custom-call(f32[2,128]{1,0:T(2,128)} %get-tuple-element.38.mask_ref, bf16[512,7168]{1,0:T(8,128)(2,1)} %x_ref.7, bf16[512,2048]{1,0:T(8,128)(2,1)} %g_ref.7, bf16[32,9216]{1,0:T(8,128)(2,1)} %copy-done.6, bf16[32,9216]{1,0:T(8,128)(2,1)} %collective-permute-done.9.refs_1_.refs_7_, ...), custom_call_target="tpu_custom_call" | custom-call | tf_op jit(solution)/shard_map/pallas_call | solution.py:329
  149.9 1.7 collective-permute-done.12
  151.6 1.0 add.27
  153.2 7.8 %collective-permute-done.13 = f32[2,256,128]{2,1,0:T(8,128)S(1)} collective-permute-done((f32[2,256,128]{2,1,0:T(8,128)S(1)}, f32[2,256,128]{2,1,0:T(8,128)S(1)}, u32[]{:S(2)}, u32[]{:S(2)}) %collective-permute-start.13) | collective-permute-done | bytes 262176 | tf_op jit(solution)/shard_map/ppermute | solution.py:20
  161.0 0.7 add.28.sums_ref
  161.7 9.8 %shard_map.109 = (bf16[32,9216]{1,0:T(8,128)(2,1)}, bf16[32,9216]{1,0:T(8,128)(2,1)}, bf16[32,9216]{1,0:T(8,128)(2,1)}, bf16[32,9216]{1,0:T(8,128)(2,1)}, bf16[512,128]{1,0:T(8,128)(2,1)}) custom-call(f32[2,256,128]{2,1,0:T(8,128)} %add.28.sums_ref, f32[2,128]{1,0:T(2,128)} %get-tuple-element.66.weight_ref, bf16[512,7168]{1,0:T(8,128)(2,1)} %x_ref.7, ...), custom_call_target="tpu_custom_call" | custom-call | tf_op jit(solution)/shard_map/pallas_call | solution.py:341
  171.5 1.6 collective-permute-start.14
  173.1 0.9 collective-permute-start.16
  174.0 3.5 %collective-permute-start.17 = (bf16[32,9216]{1,0:T(8,128)(2,1)}, bf16[32,9216]{1,0:T(8,128)(2,1)}, u32[]{:S(2)}, u32[]{:S(2)}) collective-permute-start(bf16[32,9216]{1,0:T(8,128)(2,1)} %get-tuple-element.51), channel_id=1, source_target_pairs={{0,7},{1,6},{2,5},{3,4},{4,3},{5,2},{6,1},{7,0},{8,15},{9,14},{10,... | collective-permute-start | bytes 1769480 | tf_op jit(solution)/shard_map/ppermute | solution.py:20
  177.5 0.7 pad_add_fusion.2
  178.7 0.7 reduce_sum.72
  179.4 9.5 %input.1 = f32[512,7168]{1,0:T(8,128)} custom-call(bf16[512,128]{1,0:T(8,128)(2,1)} %get-tuple-element.37.refs_0_, bf16[512,128]{1,0:T(8,128)(2,1)} %get-tuple-element.43.refs_1_, bf16[32,9216]{1,0:T(8,128)(2,1)} %get-tuple-element.32.refs_0_.refs_2_, bf16[32,9216]{1,0:T(8,128)(2,1)} %copy-done.4, bf16[32,9216]{1,0:T(8,128)(2,1)} %copy-done.3, ...), custom_call_target="tpu_custom_call" | custom-call | tf_op jit(solution)/shard_map/input/pallas_call | solution.py:355
  188.9 0.8 copy-done.2
  189.7 8.2 %collect.1 = (bf16[32,16,7168]{2,1,0:T(8,128)(2,1)}, bf16[32,16,2048]{2,1,0:T(8,128)(2,1)}) custom-call(s32[8]{0:T(128)} %get-tuple-element.73.table_ref.early_ref, bf16[32,9216]{1,0:T(8,128)(2,1)} %get-tuple-element.52.refs_0_.refs_4_, bf16[32,9216]{1,0:T(8,128)(2,1)} %copy-done, bf16[32,9216]{1,0:T(8,128)(2,1)} %copy-done.1, bf16[32,9216]{1,0:T(8,128)(2,1)} %copy-done.2), custom_call_target="tpu_custom_call" | custom-call | tf_op jit(solution)/shard_map/collect/pallas_call | solution.py:379
  197.9 13.7 %collective-permute-done.14.refs_0_ = bf16[32,9216]{1,0:T(8,128)(2,1)S(1)} collective-permute-done((bf16[32,9216]{1,0:T(8,128)(2,1)}, bf16[32,9216]{1,0:T(8,128)(2,1)S(1)}, u32[]{:S(2)}, u32[]{:S(2)}) %collective-permute-start.14) | collective-permute-done | bytes 589856 | tf_op jit(solution)/shard_map/ppermute | solution.py:20
  211.6 1.8 collective-permute-done.16.refs_2_
  213.4 15.3 %collective-permute-done.17.refs_3_ = bf16[32,9216]{1,0:T(8,128)(2,1)} collective-permute-done((bf16[32,9216]{1,0:T(8,128)(2,1)}, bf16[32,9216]{1,0:T(8,128)(2,1)}, u32[]{:S(2)}, u32[]{:S(2)}) %collective-permute-start.17) | collective-permute-done | bytes 589856 | tf_op jit(solution)/shard_map/ppermute | solution.py:20
  228.7 4.9 %finish.1 = (bf16[32,16,7168]{2,1,0:T(8,128)(2,1)}, bf16[32,16,2048]{2,1,0:T(8,128)(2,1)}) custom-call(s32[8]{0:T(128)} %get-tuple-element.72.late_ref, s32[8]{0:T(128)} %get-tuple-element.73.table_ref.early_ref, bf16[32,9216]{1,0:T(8,128)(2,1)} %copy-done.9, bf16[32,9216]{1,0:T(8,128)(2,1)} %copy-done.10, ...), custom_call_target="tpu_custom_call", output_to_operand_aliasing={{0}: (10, {}), {1}: (11, {})} | custom-call | tf_op jit(solution)/shard_map/finish/pallas_call | solution.py:391
  (83 shorter events, 5.9 us)
Async XLA Ops:
  0.6 4.7 %collective-permute-start = (s32[1,2,8]{2,1,0:T(2,128)}, s32[1,2,8]{2,1,0:T(2,128)S(1)}, u32[]{:S(2)}, u32[]{:S(2)}) collective-permute-start(s32[1,2,8]{2,1,0:T(2,128)} %bitcast.20), channel_id=1, source_target_pairs={{0,4},{1,5},{2,6},{3,7},{4,0},{5,1},{6,2},{7,3},{8,12},{9,13},{10,... | collective-permute-start | bytes 200 | tf_op jit(solution)/shard_map/ppermute | solution.py:20
  5.4 2.3 copy-start.12
  6.1 5.4 %collective-permute-start.1 = (s32[2,2,8]{2,1,0:T(2,128)S(1)}, s32[2,2,8]{2,1,0:T(2,128)S(1)}, u32[]{:S(2)}, u32[]{:S(2)}) collective-permute-start(s32[2,2,8]{2,1,0:T(2,128)S(1)} %pad_add_fusion.1), channel_id=1, source_target_pairs={{0,2},{1,3},{2,0},{3,1},{4,6},{5,7},{6,4},{7,5},{8,10},{9,11},{10,... | collective-permute-start | bytes 392 | tf_op jit(solution)/shard_map/ppermute | solution.py:20
  7.6 11.2 %copy-start.17 = (f32[2,8]{1,0:T(2,128)S(1)}, f32[2,8]{1,0:T(2,128)}, u32[]{:S(2)}) copy-start(f32[2,8]{1,0:T(2,128)} %param.12) | copy-start | bytes 196
  7.6 11.4 %copy-start.11 = (s32[2,8]{1,0:T(2,128)S(1)}, s32[2,8]{1,0:T(2,128)}, u32[]{:S(2)}) copy-start(s32[2,8]{1,0:T(2,128)} %param.11) | copy-start | bytes 196
  11.0 8.0 %copy-start.13 = (s32[1,2,8]{2,1,0:T(2,128)S(1)}, s32[1,2,8]{2,1,0:T(2,128)}, u32[]{:S(2)}) copy-start(s32[1,2,8]{2,1,0:T(2,128)} %copy-done.12) | copy-start | bytes 196
  11.0 26.8 %collective-permute-start.3 = (bf16[32,9216]{1,0:T(8,128)(2,1)}, bf16[32,9216]{1,0:T(8,128)(2,1)S(1)}, u32[]{:S(2)}, u32[]{:S(2)}) collective-permute-start(bf16[32,9216]{1,0:T(8,128)(2,1)} %get-tuple-element.34), channel_id=1, source_target_pairs={{0,4},{1,5},{2,6},{3,7},{4,0},{5,1},{6,2},{7,3},{8,12},{9,13},{10,... | collective-permute-start | bytes 1769480 | tf_op jit(solution)/shard_map/ppermute | solution.py:20
  11.4 0.6 copy-start.14
  15.6 38.7 %collective-permute-start.2 = (bf16[32,9216]{1,0:T(8,128)(2,1)}, bf16[32,9216]{1,0:T(8,128)(2,1)S(1)}, u32[]{:S(2)}, u32[]{:S(2)}) collective-permute-start(bf16[32,9216]{1,0:T(8,128)(2,1)} %get-tuple-element.33), channel_id=1, source_target_pairs={{0,2},{1,3},{2,0},{3,1},{4,6},{5,7},{6,4},{7,5},{8,10},{9,11},{10,... | collective-permute-start | bytes 1769480 | tf_op jit(solution)/shard_map/ppermute | solution.py:20
  16.1 50.3 %collective-permute-start.4 = (bf16[32,9216]{1,0:T(8,128)(2,1)}, bf16[32,9216]{1,0:T(8,128)(2,1)S(1)}, u32[]{:S(2)}, u32[]{:S(2)}) collective-permute-start(bf16[32,9216]{1,0:T(8,128)(2,1)} %get-tuple-element.35), channel_id=1, source_target_pairs={{0,6},{1,7},{2,4},{3,5},{4,2},{5,3},{6,0},{7,1},{8,14},{9,15},{10,... | collective-permute-start | bytes 1769480 | tf_op jit(solution)/shard_map/ppermute | solution.py:20
  19.7 3.6 %collective-permute-start.7 = (s32[4,2,8]{2,1,0:T(2,128)S(1)}, s32[4,2,8]{2,1,0:T(2,128)S(1)}, u32[]{:S(2)}, u32[]{:S(2)}) collective-permute-start(s32[4,2,8]{2,1,0:T(2,128)S(1)} %pad_add_fusion), channel_id=1, source_target_pairs={{0,1},{1,0},{2,3},{3,2},{4,5},{5,4},{6,7},{7,6},{8,9},{9,8},{10,11... | collective-permute-start | bytes 776 | tf_op jit(solution)/shard_map/ppermute | solution.py:20
  23.3 0.6 copy-start.15
  28.1 26.2 %copy-start.21 = (bf16[32,9216]{1,0:T(8,128)(2,1)S(1)}, bf16[32,9216]{1,0:T(8,128)(2,1)}, u32[]{:S(2)}) copy-start(bf16[32,9216]{1,0:T(8,128)(2,1)} %get-tuple-element.42) | copy-start | bytes 1769476
  28.1 70.7 %collective-permute-start.8 = (bf16[32,9216]{1,0:T(8,128)(2,1)}, bf16[32,9216]{1,0:T(8,128)(2,1)S(1)}, u32[]{:S(2)}, u32[]{:S(2)}) collective-permute-start(bf16[32,9216]{1,0:T(8,128)(2,1)} %get-tuple-element.39), channel_id=1, source_target_pairs={{0,1},{1,0},{2,3},{3,2},{4,5},{5,4},{6,7},{7,6},{8,9},{9,8},{10,11... | collective-permute-start | bytes 1769480 | tf_op jit(solution)/shard_map/ppermute | solution.py:20
  32.5 67.1 %collective-permute-start.9 = (bf16[32,9216]{1,0:T(8,128)(2,1)}, bf16[32,9216]{1,0:T(8,128)(2,1)}, u32[]{:S(2)}, u32[]{:S(2)}) collective-permute-start(bf16[32,9216]{1,0:T(8,128)(2,1)} %get-tuple-element.40), channel_id=1, source_target_pairs={{0,3},{1,2},{2,1},{3,0},{4,7},{5,6},{6,5},{7,4},{8,11},{9,10},{10,... | collective-permute-start | bytes 1769480 | tf_op jit(solution)/shard_map/ppermute | solution.py:20
  37.8 28.6 %copy-start.3 = (bf16[32,9216]{1,0:T(8,128)(2,1)}, bf16[32,9216]{1,0:T(8,128)(2,1)S(1)}, u32[]{:S(2)}) copy-start(bf16[32,9216]{1,0:T(8,128)(2,1)S(1)} %collective-permute-done.3.refs_2_.refs_4_) | copy-start | bytes 1769476
  37.8 61.7 %collective-permute-start.10 = (bf16[32,9216]{1,0:T(8,128)(2,1)}, bf16[32,9216]{1,0:T(8,128)(2,1)}, u32[]{:S(2)}, u32[]{:S(2)}) collective-permute-start(bf16[32,9216]{1,0:T(8,128)(2,1)} %get-tuple-element.41), channel_id=1, source_target_pairs={{0,5},{1,4},{2,7},{3,6},{4,1},{5,0},{6,3},{7,2},{8,13},{9,12},{10,... | collective-permute-start | bytes 1769480 | tf_op jit(solution)/shard_map/ppermute | solution.py:20
  54.3 12.1 %copy-start.4 = (bf16[32,9216]{1,0:T(8,128)(2,1)}, bf16[32,9216]{1,0:T(8,128)(2,1)S(1)}, u32[]{:S(2)}) copy-start(bf16[32,9216]{1,0:T(8,128)(2,1)S(1)} %collective-permute-done.2.refs_1_.refs_3_) | copy-start | bytes 1769476
  54.3 85.5 %collective-permute-start.11 = (bf16[32,9216]{1,0:T(8,128)(2,1)S(1)}, bf16[32,9216]{1,0:T(8,128)(2,1)}, u32[]{:S(2)}, u32[]{:S(2)}) collective-permute-start(bf16[32,9216]{1,0:T(8,128)(2,1)S(1)} %copy-done.21), channel_id=1, source_target_pairs={{0,7},{1,6},{2,5},{3,4},{4,3},{5,2},{6,1},{7,0},{8,15},{9,14},{10,... | collective-permute-start | bytes 1769480 | tf_op jit(solution)/shard_map/ppermute | solution.py:20
  66.4 0.8 copy-start.5
  77.1 1.7 collective-permute-start.5
  79.8 8.4 %collective-permute-start.6 = (f32[2,256,128]{2,1,0:T(8,128)S(1)}, f32[2,256,128]{2,1,0:T(8,128)S(1)}, u32[]{:S(2)}, u32[]{:S(2)}) collective-permute-start(f32[2,256,128]{2,1,0:T(8,128)S(1)} %add.25), channel_id=1, source_target_pairs={{0,16},{8,24},{16,0},{24,8},{1,17},{9,25},{17,1},{25,9},{2,18},{10... | collective-permute-start | bytes 786440 | tf_op jit(solution)/shard_map/ppermute | solution.py:20
  98.7 54.5 %copy-start.18 = (s32[2,2]{1,0:T(2,128)S(1)}, s32[2,2]{1,0:T(2,128)}, u32[]{:S(2)}) copy-start(s32[2,2]{1,0:T(2,128)} %get-tuple-element.46) | copy-start | bytes 52
  98.7 74.4 %collective-permute-start.18 = (bf16[32,9216]{1,0:T(8,128)(2,1)}, bf16[32,9216]{1,0:T(8,128)(2,1)S(1)}, u32[]{:S(2)}, u32[]{:S(2)}) collective-permute-start(bf16[32,9216]{1,0:T(8,128)(2,1)} %get-tuple-element.53), channel_id=1, source_target_pairs={{0,2},{1,3},{2,0},{3,1},{4,6},{5,7},{6,4},{7,5},{8,10},{9,11},{10,... | collective-permute-start | bytes 1769480 | tf_op jit(solution)/shard_map/ppermute | solution.py:20
  98.8 41.1 %copy-start.6 = (bf16[32,9216]{1,0:T(8,128)(2,1)}, bf16[32,9216]{1,0:T(8,128)(2,1)S(1)}, u32[]{:S(2)}) copy-start(bf16[32,9216]{1,0:T(8,128)(2,1)S(1)} %collective-permute-done.8.refs_0_.refs_6_) | copy-start | bytes 1769476
  98.8 75.2 %collective-permute-start.19 = (bf16[32,9216]{1,0:T(8,128)(2,1)}, bf16[32,9216]{1,0:T(8,128)(2,1)S(1)}, u32[]{:S(2)}, u32[]{:S(2)}) collective-permute-start(bf16[32,9216]{1,0:T(8,128)(2,1)} %get-tuple-element.54), channel_id=1, source_target_pairs={{0,4},{1,5},{2,6},{3,7},{4,0},{5,1},{6,2},{7,3},{8,12},{9,13},{10,... | collective-permute-start | bytes 1769480 | tf_op jit(solution)/shard_map/ppermute | solution.py:20
  149.8 27.7 %copy-start.16 = (s32[4,2]{1,0:T(4,128)S(1)}, s32[4,2]{1,0:T(4,128)}, u32[]{:S(2)}) copy-start(s32[4,2]{1,0:T(4,128)} %get-tuple-element.44) | copy-start | bytes 100
  149.8 27.7 %copy-start.19 = (s32[1,2]{1,0:T(1,128)S(1)}, s32[1,2]{1,0:T(1,128)}, u32[]{:S(2)}) copy-start(s32[1,2]{1,0:T(1,128)} %get-tuple-element.47) | copy-start | bytes 28
  149.8 27.7 %copy-start.20 = (s32[1,2]{1,0:T(1,128)S(1)}, s32[1,2]{1,0:T(1,128)}, u32[]{:S(2)}) copy-start(s32[1,2]{1,0:T(1,128)} %get-tuple-element.45) | copy-start | bytes 28
  149.8 28.4 %copy-start.7 = (f32[2,256,128]{2,1,0:T(8,128)S(1)}, f32[2,256,128]{2,1,0:T(8,128)}, u32[]{:S(2)}) copy-start(f32[2,256,128]{2,1,0:T(8,128)} %add.26.sums_ref) | copy-start | bytes 786436
  149.8 1.8 collective-permute-start.12
  152.6 8.4 %collective-permute-start.13 = (f32[2,256,128]{2,1,0:T(8,128)S(1)}, f32[2,256,128]{2,1,0:T(8,128)S(1)}, u32[]{:S(2)}, u32[]{:S(2)}) collective-permute-start(f32[2,256,128]{2,1,0:T(8,128)S(1)} %add.27), channel_id=1, source_target_pairs={{0,16},{8,24},{16,0},{24,8},{1,17},{9,25},{17,1},{25,9},{2,18},{10... | collective-permute-start | bytes 786440 | tf_op jit(solution)/shard_map/ppermute | solution.py:20
  153.2 35.7 %collective-permute-start.20 = (bf16[32,9216]{1,0:T(8,128)(2,1)}, bf16[32,9216]{1,0:T(8,128)(2,1)S(1)}, u32[]{:S(2)}, u32[]{:S(2)}) collective-permute-start(bf16[32,9216]{1,0:T(8,128)(2,1)} %get-tuple-element.55), channel_id=1, source_target_pairs={{0,6},{1,7},{2,4},{3,5},{4,2},{5,3},{6,0},{7,1},{8,14},{9,15},{10,... | collective-permute-start | bytes 1769480 | tf_op jit(solution)/shard_map/ppermute | solution.py:20
  161.7 16.5 %copy-start.8 = (f32[2,256,128]{2,1,0:T(8,128)S(1)}, f32[2,256,128]{2,1,0:T(8,128)}, u32[]{:S(2)}) copy-start(f32[2,256,128]{2,1,0:T(8,128)} %add.28.sums_ref) | copy-start | bytes 786436
  171.5 40.1 %collective-permute-start.14 = (bf16[32,9216]{1,0:T(8,128)(2,1)}, bf16[32,9216]{1,0:T(8,128)(2,1)S(1)}, u32[]{:S(2)}, u32[]{:S(2)}) collective-permute-start(bf16[32,9216]{1,0:T(8,128)(2,1)} %get-tuple-element.48), channel_id=1, source_target_pairs={{0,1},{1,0},{2,3},{3,2},{4,5},{5,4},{6,7},{7,6},{8,9},{9,8},{10,11... | collective-permute-start | bytes 1769480 | tf_op jit(solution)/shard_map/ppermute | solution.py:20
  173.1 38.5 %collective-permute-start.15 = (bf16[32,9216]{1,0:T(8,128)(2,1)}, bf16[32,9216]{1,0:T(8,128)(2,1)S(1)}, u32[]{:S(2)}, u32[]{:S(2)}) collective-permute-start(bf16[32,9216]{1,0:T(8,128)(2,1)} %get-tuple-element.49), channel_id=1, source_target_pairs={{0,3},{1,2},{2,1},{3,0},{4,7},{5,6},{6,5},{7,4},{8,11},{9,10},{10,... | collective-permute-start | bytes 1769480 | tf_op jit(solution)/shard_map/ppermute | solution.py:20
  173.1 15.8 %copy-start = (bf16[32,9216]{1,0:T(8,128)(2,1)}, bf16[32,9216]{1,0:T(8,128)(2,1)S(1)}, u32[]{:S(2)}) copy-start(bf16[32,9216]{1,0:T(8,128)(2,1)S(1)} %collective-permute-done.18.refs_1_.refs_5_) | copy-start | bytes 1769476
  173.1 40.3 %collective-permute-start.16 = (bf16[32,9216]{1,0:T(8,128)(2,1)}, bf16[32,9216]{1,0:T(8,128)(2,1)}, u32[]{:S(2)}, u32[]{:S(2)}) collective-permute-start(bf16[32,9216]{1,0:T(8,128)(2,1)} %get-tuple-element.50), channel_id=1, source_target_pairs={{0,5},{1,4},{2,7},{3,6},{4,1},{5,0},{6,3},{7,2},{8,13},{9,12},{10,... | collective-permute-start | bytes 1769480 | tf_op jit(solution)/shard_map/ppermute | solution.py:20
  174.0 14.9 %copy-start.1 = (bf16[32,9216]{1,0:T(8,128)(2,1)}, bf16[32,9216]{1,0:T(8,128)(2,1)S(1)}, u32[]{:S(2)}) copy-start(bf16[32,9216]{1,0:T(8,128)(2,1)S(1)} %collective-permute-done.19.refs_2_.refs_6_) | copy-start | bytes 1769476
  174.0 54.7 %collective-permute-start.17 = (bf16[32,9216]{1,0:T(8,128)(2,1)}, bf16[32,9216]{1,0:T(8,128)(2,1)}, u32[]{:S(2)}, u32[]{:S(2)}) collective-permute-start(bf16[32,9216]{1,0:T(8,128)(2,1)} %get-tuple-element.51), channel_id=1, source_target_pairs={{0,7},{1,6},{2,5},{3,4},{4,3},{5,2},{6,1},{7,0},{8,15},{9,14},{10,... | collective-permute-start | bytes 1769480 | tf_op jit(solution)/shard_map/ppermute | solution.py:20
  188.9 0.8 copy-start.2
  211.6 17.1 %copy-start.9 = (bf16[32,9216]{1,0:T(8,128)(2,1)}, bf16[32,9216]{1,0:T(8,128)(2,1)S(1)}, u32[]{:S(2)}) copy-start(bf16[32,9216]{1,0:T(8,128)(2,1)S(1)} %collective-permute-done.14.refs_0_) | copy-start | bytes 1769476
  211.6 17.1 %copy-start.10 = (bf16[32,9216]{1,0:T(8,128)(2,1)}, bf16[32,9216]{1,0:T(8,128)(2,1)S(1)}, u32[]{:S(2)}) copy-start(bf16[32,9216]{1,0:T(8,128)(2,1)S(1)} %collective-permute-done.15.refs_1_) | copy-start | bytes 1769476

commit v2 on v1

--- a/solution.py
+++ b/solution.py
@@ -14,6 +14,22 @@
 F32 = jnp.float32
 ANY = pl.BlockSpec(memory_space=pl.ANY)
 SMEM = pl.BlockSpec(memory_space=pltpu.SMEM)
+VMEM = pl.BlockSpec(memory_space=pltpu.VMEM)
+HBM = pl.BlockSpec(memory_space=pltpu.HBM)
+
+
+def plan(groups):
+    steps = [groups >> (i + 1) for i in range(groups.bit_length() - 1)]
+    half, last = groups // 2, steps[-1]
+    if groups > 4:
+        steps[0] += half // 2
+    out = []
+    for part in (0, last):
+        near = [d for d in range(half) if d & last == part]
+        far = [d for d in range(half, groups) if d & last == part]
+        out.append(near + far)
+    home = [list(part) for part in out]
+    return steps, out, home
 
 
 def swap(x, axis, count, offset):
@@ -22,7 +38,7 @@
 
 def pick_kernel(groups, me_ref, ids_ref, fin, fout, table_ref, *refs):
     outs = refs[:groups]
-    hold, in_sem, out_sem = refs[groups:]
+    (in_sem,) = refs[groups:]
     exp_count, rank, wide = fin.shape
     base = me_ref[0] * exp_count
     loads = []
@@ -41,24 +57,17 @@
             e = jnp.maximum(picks[c], 0)
             rows = pl.ds(c * rank, rank)
             one = pltpu.make_async_copy(
-                fin.at[e], hold.at[m, rows, pl.ds(0, wide)], in_sem.at[m, c, 0]
+                fin.at[e], outs[m].at[rows, pl.ds(0, wide)], in_sem.at[m, c, 0]
             )
             two = pltpu.make_async_copy(
-                fout.at[e], hold.at[m, rows, pl.ds(wide, fout.shape[2])], in_sem.at[m, c, 1]
+                fout.at[e], outs[m].at[rows, pl.ds(wide, fout.shape[2])], in_sem.at[m, c, 1]
             )
             one.start()
             two.start()
             loads.append((one, two))
-    stores = []
-    for m in range(groups):
-        for c in range(CAP):
-            for load in loads[m * CAP + c]:
-                load.wait()
-        store = pltpu.make_async_copy(hold.at[m], outs[m], out_sem.at[m])
-        store.start()
-        stores.append(store)
-    for store in stores:
-        store.wait()
+    for pair in loads:
+        for load in pair:
+            load.wait()
 
 
 def project_kernel(groups, in_tiles, tiles, mask_ref, x_ref, g_ref, *refs):
@@ -170,8 +179,8 @@
 
 def finish_kernel(late, early, late_ref, early_ref, *refs):
     a, b = late // CAP, early // CAP
-    late_hbm, early_hbm = refs[:a], refs[a : a + b]
-    in_hbm, out_hbm, held, kept, stage, total, held_sem, kept_sem, out_sem = refs[a + b + 2 :]
+    late_refs, early_hbm = refs[:a], refs[a : a + b]
+    in_hbm, out_hbm, kept, stage, total, kept_sem, out_sem = refs[a + b + 2 :]
     rank, full = total.shape
     wide = in_hbm.shape[2]
 
@@ -186,9 +195,6 @@
         for r in range(s):
             fresh = fresh & (late_ref[r] != late_ref[s])
         return fresh
-
-    def load_late(j):
-        return pltpu.make_async_copy(late_hbm[j], held.at[j], held_sem.at[j])
 
     def load_early(m):
         return pltpu.make_async_copy(place(early_hbm, m, rank), kept.at[m], kept_sem.at[m])
@@ -202,26 +208,22 @@
             ),
         )
 
-    for j in range(a):
-        load_late(j).start()
     for m in range(early):
 
         @pl.when(used(m))
         def _():
             load_early(m).start()
 
-    for j in range(a):
-        load_late(j).wait()
     for s in range(late):
 
         @pl.when(first(s))
         def _():
-            total[...] = held[s // CAP, pl.ds((s % CAP) * rank, rank), :].astype(F32)
+            total[...] = place(late_refs, s, rank)[...].astype(F32)
             for r in range(s + 1, late):
 
                 @pl.when(late_ref[r] == late_ref[s])
                 def _():
-                    total[...] += held[r // CAP, pl.ds((r % CAP) * rank, rank), :].astype(F32)
+                    total[...] += place(late_refs, r, rank)[...].astype(F32)
 
             for m in range(early):
 
@@ -259,21 +261,18 @@
     both = CAP * rank
     piece = jax.ShapeDtypeStruct((both, full), BF)
 
-    def pick(lists):
+    def pick(lists, fast):
         count = lists.shape[0]
         return pl.pallas_call(
             functools.partial(pick_kernel, count),
-            out_shape=[jax.ShapeDtypeStruct((count, CAP), jnp.int32)] + [piece] * count,
-            in_specs=[SMEM, SMEM, ANY, ANY],
-            out_specs=[SMEM] + [ANY] * count,
-            scratch_shapes=[
-                pltpu.VMEM((count, both, full), BF),
-                pltpu.SemaphoreType.DMA((count, CAP, 2)),
-                pltpu.SemaphoreType.DMA((count,)),
-            ],
+            out_shape=[jax.ShapeDtypeStruct((count, CAP), jnp.int32)]
+            + [pltpu.VMEM((both, full), BF) if fast else piece] * count,
+            in_specs=[SMEM, SMEM, HBM, HBM],
+            out_specs=[SMEM] + [VMEM] * count,
+            scratch_shapes=[pltpu.SemaphoreType.DMA((count, CAP, 2))],
         )(me_arr, lists, factor_in, factor_out)
 
-    steps = [groups >> (i + 1) for i in range(groups.bit_length() - 1)]
+    steps, chunks, homes = plan(groups)
     lists, known = adapter_ids[None], [0]
     slot_table, sent, got = {}, {}, {}
     arrivals = []
@@ -283,17 +282,11 @@
         lists = jnp.concatenate([lists, fresh], axis=0)
         known = known + [d ^ step for d in known]
     arrivals.append(([0], adapter_ids[None]))
-    for which, fresh in arrivals:
-        picked = pick(fresh)
+    for n, (which, fresh) in enumerate(arrivals):
+        picked = pick(fresh, n == 0)
         for m, d in enumerate(which):
             slot_table[d] = picked[0][m]
             sent[d] = picked[1 + m]
-    last = steps[-1]
-    chunks = [
-        [d for d in known if not d & last],
-        [d for d in known if d & last],
-    ]
-    chunks = [sorted(c, key=lambda d: (d >= groups // 2, d)) for c in chunks]
     for chunk in chunks:
         for d in chunk:
             got[d] = sent[d] if d == 0 else swap(sent[d], "adapter", groups, d)
@@ -348,8 +341,9 @@
         )(part, weight[:, n * rows : (n + 1) * rows], activations, cotangent)
         sums.append(part)
         weighted.append(done[-1])
-        for m, d in enumerate(chunk):
-            back[d] = done[m] if d == 0 else swap(done[m], "adapter", groups, d)
+        for d in homes[n]:
+            mine = done[chunk.index(d)]
+            back[d] = mine if d == 0 else swap(mine, "adapter", groups, d)
 
     everything = [d for c in chunks for d in c]
     input_grad = pl.pallas_call(
@@ -369,42 +363,45 @@
     per_slot = jnp.sum(per_slot.reshape(groups * CAP, rank), axis=1)
     router_grad = jnp.sum(by_request * per_slot[:, None, None], axis=0)
 
-    tables = [jnp.concatenate([slot_table[d] for d in c]) for c in chunks]
-    early, late = len(chunks[0]) * CAP, len(chunks[1]) * CAP
+    stages = [homes[0], homes[1][:-1], homes[1][-1:]]
+    tables = [jnp.concatenate([slot_table[d] for d in stage]) for stage in stages]
+    early = len(stages[0]) * CAP
     block = math.gcd(exp_count, 4)
-    grads = [
-        jax.ShapeDtypeStruct(factor_in.shape, BF),
-        jax.ShapeDtypeStruct(factor_out.shape, BF),
-    ]
     grads = pl.pallas_call(
         functools.partial(collect_kernel, early),
-        out_shape=grads,
+        out_shape=[
+            jax.ShapeDtypeStruct(factor_in.shape, BF),
+            jax.ShapeDtypeStruct(factor_out.shape, BF),
+        ],
         grid=(exp_count // block,),
-        in_specs=[SMEM] + [pl.BlockSpec(memory_space=pltpu.VMEM)] * len(chunks[0]),
+        in_specs=[SMEM] + [VMEM] * len(stages[0]),
         out_specs=[
             pl.BlockSpec((block, rank, wide), lambda i: (i, 0, 0)),
             pl.BlockSpec((block, rank, narrow), lambda i: (i, 0, 0)),
         ],
         scratch_shapes=[pltpu.VMEM((rank, full), F32)],
         name="collect",
-    )(tables[0], *[back[d] for d in chunks[0]])
-    grad_factor_in, grad_factor_out = pl.pallas_call(
-        functools.partial(finish_kernel, late, early),
-        out_shape=[jax.ShapeDtypeStruct(g.shape, BF) for g in grads],
-        in_specs=[SMEM] * 2 + [ANY] * (groups + 2),
-        out_specs=[ANY] * 2,
-        scratch_shapes=[
-            pltpu.VMEM((len(chunks[1]), both, full), BF),
-            pltpu.VMEM((early, rank, full), BF),
-            pltpu.VMEM((late, rank, full), BF),
-            pltpu.VMEM((rank, full), F32),
-            pltpu.SemaphoreType.DMA((len(chunks[1]),)),
-            pltpu.SemaphoreType.DMA((early,)),
-            pltpu.SemaphoreType.DMA((late, 2)),
-        ],
-        input_output_aliases={groups + 2: 0, groups + 3: 1},
-        name="finish",
-    )(tables[1], tables[0], *[back[d] for d in chunks[1]], *[back[d] for d in chunks[0]], *grads)
+    )(tables[0], *[back[d] for d in stages[0]])
+    seen, seen_table = list(stages[0]), tables[0]
+    for n in (1, 2):
+        late, early = len(stages[n]) * CAP, len(seen) * CAP
+        arrays = len(stages[n]) + len(seen)
+        grads = pl.pallas_call(
+            functools.partial(finish_kernel, late, early),
+            out_shape=[jax.ShapeDtypeStruct(g.shape, BF) for g in grads],
+            in_specs=[SMEM] * 2 + [VMEM] * len(stages[n]) + [ANY] * len(seen) + [HBM] * 2,
+            out_specs=[HBM] * 2,
+            scratch_shapes=[
+                pltpu.VMEM((early, rank, full), BF),
+                pltpu.VMEM((late, rank, full), BF),
+                pltpu.VMEM((rank, full), F32),
+                pltpu.SemaphoreType.DMA((early,)),
+                pltpu.SemaphoreType.DMA((late, 2)),
+            ],
+            input_output_aliases={arrays + 2: 0, arrays + 3: 1},
+        )(tables[n], seen_table, *[back[d] for d in stages[n] + seen], *grads)
+        seen, seen_table = seen + stages[n], jnp.concatenate([seen_table, tables[n]])
+    grad_factor_in, grad_factor_out = grads
     return (input_grad, grad_factor_in, grad_factor_out, router_grad)
 
 

time: 235 us -> 241 us (1.026)
  the two profiles are of different devices: /device:TPU:22 before, /device:TPU:0 now
where the time goes in v2:
time: 241 us; the launch traced here: 240 us
  waiting for transfers between devices  92.1 us (38%)
  Pallas kernels  76 us (32%)
  starting transfers between devices  49.3 us (20%)
  local copies, waits for them, and re-layouts  10.8 us (4%)
  other arithmetic  10.6 us (4%)
    ppermute x21, waiting for transfers between devices, swap(): return lax.ppermute(x, axis, [(i, i ^ offset) for i in range(count)])  92.1 us
    ppermute x21, starting transfers between devices, swap(): return lax.ppermute(x, axis, [(i, i ^ offset) for i in range(count)])  49.3 us
    pallas_call x2, Pallas kernels, body(): pl.pallas_call(functools.partial(project_kernel, count, in_tiles, tiles),...  19.7 us
    pallas_call x2, Pallas kernels, body(): pl.pallas_call(functools.partial(term_kernel, count, in_tiles), out_shape...  19.4 us
    pallas_call x4, Pallas kernels, pick(): pl.pallas_call(functools.partial(pick_kernel, count), out_shape=[jax.Shap...  12.5 us
    pallas_call x1, Pallas kernels, body(): pl.pallas_call(functools.partial(input_kernel, len(chunks), groups), out_...  9.47 us
    pallas_call x1, Pallas kernels, body(): pl.pallas_call(functools.partial(collect_kernel, early), out_shape=[jax.S...  8.09 us
    pallas_call x2, Pallas kernels, body(): pl.pallas_call(functools.partial(finish_kernel, late, early), out_shape=[...  6.87 us
  transfers between devices with their start and end apart: 21, of which 9 were waited for; matrix products, arithmetic and copies ran while one was open for 7% of the time, Pallas kernels for 26%

profile of v2, /device:TPU:0, one launch (start us, length us, event | category | flops | bytes accessed | tf_op | source)
XLA Modules:
  0.0 239.7 jit_solution(12803918132984487123)
XLA Ops:
  0.6 5.1 %collective-permute-start = (s32[1,2,8]{2,1,0:T(2,128)}, s32[1,2,8]{2,1,0:T(2,128)S(1)}, u32[]{:S(2)}, u32[]{:S(2)}) collective-permute-start(s32[1,2,8]{2,1,0:T(2,128)} %bitcast.20), channel_id=1, source_target_pairs={{0,6},{1,7},{2,4},{3,5},{4,2},{5,3},{6,0},{7,1},{8,14},{9,15},{10,... | collective-permute-start | bytes 200 | tf_op jit(solution)/shard_map/ppermute | solution.py:36
  5.8 0.8 reshape.172
  8.3 2.5 %shard_map.104 = (s32[1,2]{1,0:T(1,128)}, bf16[32,9216]{1,0:T(8,128)(2,1)S(1)}) custom-call(s32[1]{0:T(128)} %bitcast.1.me_ref, s32[1,2,8]{2,1,0:T(2,128)} %copy-done.13, bf16[32,16,7168]{2,1,0:T(8,128)(2,1)} %fin.7, bf16[32,16,2048]{2,1,0:T(8,128)(2,1)} %fout.7), custom_call_target="tpu_custom_call" | custom-call | tf_op jit(solution)/shard_map/pallas_call | solution.py:266
  10.8 3.9 %collective-permute-start.4 = (bf16[32,9216]{1,0:T(8,128)(2,1)S(1)}, bf16[32,9216]{1,0:T(8,128)(2,1)S(1)}, u32[]{:S(2)}, u32[]{:S(2)}) collective-permute-start(bf16[32,9216]{1,0:T(8,128)(2,1)S(1)} %get-tuple-element.37), channel_id=1, source_target_pairs={{0,6},{1,7},{2,4},{3,5},{4,2},{5,3},{6,0},{7,1},{8,14},{9,15},{10,... | collective-permute-start | bytes 1769480 | tf_op jit(solution)/shard_map/ppermute | solution.py:36
  15.3 3.2 %shard_map.103 = (s32[2,2]{1,0:T(2,128)}, bf16[32,9216]{1,0:T(8,128)(2,1)}, bf16[32,9216]{1,0:T(8,128)(2,1)}) custom-call(s32[1]{0:T(128)} %bitcast.1.me_ref, s32[2,2,8]{2,1,0:T(2,128)} %copy-done.15, bf16[32,16,7168]{2,1,0:T(8,128)(2,1)} %fin.7, bf16[32,16,2048]{2,1,0:T(8,128)(2,1)} %fout.7), custom_call_target="tpu_custom_call" | custom-call | tf_op jit(solution)/shard_map/pallas_call | solution.py:266
  18.4 1.2 collective-permute-start.2
  21.1 1.5 collective-permute-start.7
  22.9 1.9 collective-permute-done.7.ids_ref
  25.3 4.1 %shard_map.107 = (s32[4,2]{1,0:T(4,128)}, bf16[32,9216]{1,0:T(8,128)(2,1)}, bf16[32,9216]{1,0:T(8,128)(2,1)}, bf16[32,9216]{1,0:T(8,128)(2,1)}, bf16[32,9216]{1,0:T(8,128)(2,1)}) custom-call(s32[1]{0:T(128)} %bitcast.1.me_ref, s32[4,2,8]{2,1,0:T(2,128)} %copy-done.16, bf16[32,16,7168]{2,1,0:T(8,128)(2,1)} %fin.7, bf16[32,16,2048]{2,1,0:T(8,128)(2,1)} %fout.7), custom_call_target="tpu_custom_call" | custom-call | tf_op jit(solution)/shard_map/pallas_call | solution.py:266
  29.4 1.6 collective-permute-start.8
  31.0 0.9 collective-permute-start.9
  31.9 13.6 %collective-permute-start.10 = (bf16[32,9216]{1,0:T(8,128)(2,1)}, bf16[32,9216]{1,0:T(8,128)(2,1)S(1)}, u32[]{:S(2)}, u32[]{:S(2)}) collective-permute-start(bf16[32,9216]{1,0:T(8,128)(2,1)} %get-tuple-element.43), channel_id=1, source_target_pairs={{0,5},{1,4},{2,7},{3,6},{4,1},{5,0},{6,3},{7,2},{8,13},{9,12},{10,... | collective-permute-start | bytes 1769480 | tf_op jit(solution)/shard_map/ppermute | solution.py:36
  46.0 2.7 %shard_map.102 = (s32[1,2]{1,0:T(1,128)}, bf16[32,9216]{1,0:T(8,128)(2,1)}) custom-call(s32[1]{0:T(128)} %bitcast.1.me_ref, s32[1,2,8]{2,1,0:T(2,128)} %bitcast.22, bf16[32,16,7168]{2,1,0:T(8,128)(2,1)} %fin.7, bf16[32,16,2048]{2,1,0:T(8,128)(2,1)} %fout.7), custom_call_target="tpu_custom_call" | custom-call | tf_op jit(solution)/shard_map/pallas_call | solution.py:266
  48.7 18.2 %collective-permute-done.3.refs_2_.refs_4_ = bf16[32,9216]{1,0:T(8,128)(2,1)S(1)} collective-permute-done((bf16[32,9216]{1,0:T(8,128)(2,1)}, bf16[32,9216]{1,0:T(8,128)(2,1)S(1)}, u32[]{:S(2)}, u32[]{:S(2)}) %collective-permute-start.3) | collective-permute-done | bytes 589856 | tf_op jit(solution)/shard_map/ppermute | solution.py:36
  66.9 0.8 copy-done.5
  67.7 9.9 %shard_map.105 = f32[2,256,128]{2,1,0:T(8,128)} custom-call(f32[2,128]{1,0:T(2,128)} %get-tuple-element.72.mask_ref, bf16[512,7168]{1,0:T(8,128)(2,1)} %x_ref.7, bf16[512,2048]{1,0:T(8,128)(2,1)} %g_ref.7, bf16[32,9216]{1,0:T(8,128)(2,1)} %get-tuple-element.34.refs_0_.refs_2_, bf16[32,9216]{1,0:T(8,128)(2,1)} %copy-done.4, bf16[32,9216]{1,0:T(8,128)(2,1)} %copy-done.5, ...), custom_call_target="tpu_custom_call" | custom-call | tf_op jit(solution)/shard_map/pallas_call | solution.py:322
  77.6 1.7 collective-permute-done.5
  79.3 1.0 add.25
  80.3 1.8 collective-permute-start.6
  82.9 5.8 %collective-permute-done.6 = f32[2,256,128]{2,1,0:T(8,128)S(1)} collective-permute-done((f32[2,256,128]{2,1,0:T(8,128)S(1)}, f32[2,256,128]{2,1,0:T(8,128)S(1)}, u32[]{:S(2)}, u32[]{:S(2)}) %collective-permute-start.6) | collective-permute-done | bytes 262176 | tf_op jit(solution)/shard_map/ppermute | solution.py:36
  89.4 9.7 %shard_map.106 = (bf16[32,9216]{1,0:T(8,128)(2,1)}, bf16[32,9216]{1,0:T(8,128)(2,1)}, bf16[32,9216]{1,0:T(8,128)(2,1)}, bf16[32,9216]{1,0:T(8,128)(2,1)}, bf16[512,128]{1,0:T(8,128)(2,1)}) custom-call(f32[2,256,128]{2,1,0:T(8,128)} %add.26.sums_ref, f32[2,128]{1,0:T(2,128)} %get-tuple-element.71.weight_ref, bf16[512,7168]{1,0:T(8,128)(2,1)} %x_ref.7, ...), custom_call_target="tpu_custom_call" | custom-call | tf_op jit(solution)/shard_map/pallas_call | solution.py:334
  99.2 5.1 %collective-permute-done.10.refs_2_.refs_8_ = bf16[32,9216]{1,0:T(8,128)(2,1)S(1)} collective-permute-done((bf16[32,9216]{1,0:T(8,128)(2,1)}, bf16[32,9216]{1,0:T(8,128)(2,1)S(1)}, u32[]{:S(2)}, u32[]{:S(2)}) %collective-permute-start.10) | collective-permute-done | bytes 589856 | tf_op jit(solution)/shard_map/ppermute | solution.py:36
  104.3 0.8 copy-done.8
  105.2 9.9 %shard_map.108 = f32[2,256,128]{2,1,0:T(8,128)} custom-call(f32[2,128]{1,0:T(2,128)} %get-tuple-element.40.mask_ref, bf16[512,7168]{1,0:T(8,128)(2,1)} %x_ref.7, bf16[512,2048]{1,0:T(8,128)(2,1)} %g_ref.7, bf16[32,9216]{1,0:T(8,128)(2,1)} %copy-done.6, bf16[32,9216]{1,0:T(8,128)(2,1)} %copy-done.7, bf16[32,9216]{1,0:T(8,128)(2,1)} %copy-done.8, ...), custom_call_target="tpu_custom_call" | custom-call | tf_op jit(solution)/shard_map/pallas_call | solution.py:322
  115.0 12.2 %collective-permute-start.15 = (bf16[32,9216]{1,0:T(8,128)(2,1)}, bf16[32,9216]{1,0:T(8,128)(2,1)S(1)}, u32[]{:S(2)}, u32[]{:S(2)}) collective-permute-start(bf16[32,9216]{1,0:T(8,128)(2,1)} %get-tuple-element.52), channel_id=1, source_target_pairs={{0,2},{1,3},{2,0},{3,1},{4,6},{5,7},{6,4},{7,5},{8,10},{9,11},{10,... | collective-permute-start | bytes 1769480 | tf_op jit(solution)/shard_map/ppermute | solution.py:36
  127.2 1.3 collective-permute-start.16
  128.5 1.0 add.27
  129.4 1.6 collective-permute-start.13
  131.6 1.4 collective-permute-start.17
  133.0 4.8 %collective-permute-done.13 = f32[2,256,128]{2,1,0:T(8,128)S(1)} collective-permute-done((f32[2,256,128]{2,1,0:T(8,128)S(1)}, f32[2,256,128]{2,1,0:T(8,128)S(1)}, u32[]{:S(2)}, u32[]{:S(2)}) %collective-permute-start.13) | collective-permute-done | bytes 262176 | tf_op jit(solution)/shard_map/ppermute | solution.py:36
  138.5 9.7 %shard_map.109 = (bf16[32,9216]{1,0:T(8,128)(2,1)}, bf16[32,9216]{1,0:T(8,128)(2,1)}, bf16[32,9216]{1,0:T(8,128)(2,1)}, bf16[32,9216]{1,0:T(8,128)(2,1)}, bf16[512,128]{1,0:T(8,128)(2,1)}) custom-call(f32[2,256,128]{2,1,0:T(8,128)} %add.28.sums_ref, f32[2,128]{1,0:T(2,128)} %get-tuple-element.70.weight_ref, bf16[512,7168]{1,0:T(8,128)(2,1)} %x_ref.7, ...), custom_call_target="tpu_custom_call" | custom-call | tf_op jit(solution)/shard_map/pallas_call | solution.py:334
  148.3 1.5 collective-permute-start.14
  149.7 1.5 collective-permute-start.18
  151.2 2.5 %collective-permute-done.15.refs_1_.refs_4_.refs_2_ = bf16[32,9216]{1,0:T(8,128)(2,1)S(1)} collective-permute-done((bf16[32,9216]{1,0:T(8,128)(2,1)}, bf16[32,9216]{1,0:T(8,128)(2,1)S(1)}, u32[]{:S(2)}, u32[]{:S(2)}) %collective-permute-start.15) | collective-permute-done | bytes 589856 | tf_op jit(solution)/shard_map/ppermute | solution.py:36
  153.7 28.6 %collective-permute-done.16.refs_2_.refs_5_.refs_3_ = bf16[32,9216]{1,0:T(8,128)(2,1)S(1)} collective-permute-done((bf16[32,9216]{1,0:T(8,128)(2,1)S(1)}, bf16[32,9216]{1,0:T(8,128)(2,1)S(1)}, u32[]{:S(2)}, u32[]{:S(2)}) %collective-permute-start.16) | collective-permute-done | bytes 589856 | tf_op jit(solution)/shard_map/ppermute | solution.py:36
  182.3 1.4 slice_bitcast_fusion
  183.7 1.3 concatenate.27.early_ref
  185.0 1.3 pad_add_fusion.2.late_ref
  186.2 1.0 fusion.1
  187.3 1.0 fusion
  188.6 0.8 select_reduce_fusion.1
  190.0 9.5 %input.1 = f32[512,7168]{1,0:T(8,128)} custom-call(bf16[512,128]{1,0:T(8,128)(2,1)} %get-tuple-element.39.refs_0_, bf16[512,128]{1,0:T(8,128)(2,1)} %get-tuple-element.45.refs_1_, bf16[32,9216]{1,0:T(8,128)(2,1)} %get-tuple-element.34.refs_0_.refs_2_, bf16[32,9216]{1,0:T(8,128)(2,1)} %copy-done.4, bf16[32,9216]{1,0:T(8,128)(2,1)} %copy-done.5, ...), custom_call_target="tpu_custom_call" | custom-call | tf_op jit(solution)/shard_map/input/pallas_call | solution.py:349
  199.5 0.8 copy-done.2
  200.4 8.1 %collect.1 = (bf16[32,16,7168]{2,1,0:T(8,128)(2,1)}, bf16[32,16,2048]{2,1,0:T(8,128)(2,1)}) custom-call(s32[8]{0:T(128)} %pad_add_fusion.3.table_ref.early_ref, bf16[32,9216]{1,0:T(8,128)(2,1)} %get-tuple-element.51.refs_0_.refs_3_.refs_1_, bf16[32,9216]{1,0:T(8,128)(2,1)} %copy-done, bf16[32,9216]{1,0:T(8,128)(2,1)} %copy-done.1, bf16[32,9216]{1,0:T(8,128)(2,1)} %copy-done.2), custom_call_target="tpu_custom_call" | custom-call | tf_op jit(solution)/shard_map/collect/pallas_call | solution.py:370
  208.5 23.5 %collective-permute-done.20.refs_2_.refs_7_ = bf16[32,9216]{1,0:T(8,128)(2,1)S(1)} collective-permute-done((bf16[32,9216]{1,0:T(8,128)(2,1)}, bf16[32,9216]{1,0:T(8,128)(2,1)S(1)}, u32[]{:S(2)}, u32[]{:S(2)}) %collective-permute-start.20) | collective-permute-done | bytes 589856 | tf_op jit(solution)/shard_map/ppermute | solution.py:36
  232.0 0.8 copy-done.11
  232.8 3.8 %shard_map.110 = (bf16[32,16,7168]{2,1,0:T(8,128)(2,1)}, bf16[32,16,2048]{2,1,0:T(8,128)(2,1)}) custom-call(s32[6]{0:T(128)} %pad_add_fusion.2.late_ref, s32[8]{0:T(128)} %pad_add_fusion.3.table_ref.early_ref, bf16[32,9216]{1,0:T(8,128)(2,1)} %copy-done.9, bf16[32,9216]{1,0:T(8,128)(2,1)} %copy-done.10, ...), custom_call_target="tpu_custom_call", output_to_operand_aliasing={{0}: (9, {}), {1}: (10, {})} | custom-call | tf_op jit(solution)/shard_map/pallas_call | solution.py:389
  236.7 3.0 %shard_map.111 = (bf16[32,16,7168]{2,1,0:T(8,128)(2,1)}, bf16[32,16,2048]{2,1,0:T(8,128)(2,1)}) custom-call(s32[2]{0:T(128)} %get-tuple-element.69.late_ref, s32[14]{0:T(128)} %concatenate.27.early_ref, bf16[32,9216]{1,0:T(8,128)(2,1)} %collective-permute-done.14.refs_0_, ...), custom_call_target="tpu_custom_call", output_to_operand_aliasing={{0}: (10, {}), {1}: (11, {})} | custom-call | tf_op jit(solution)/shard_map/pallas_call | solution.py:389
  (88 shorter events, 9.1 us)
Async XLA Ops:
  0.6 6.9 %collective-permute-start = (s32[1,2,8]{2,1,0:T(2,128)}, s32[1,2,8]{2,1,0:T(2,128)S(1)}, u32[]{:S(2)}, u32[]{:S(2)}) collective-permute-start(s32[1,2,8]{2,1,0:T(2,128)} %bitcast.20), channel_id=1, source_target_pairs={{0,6},{1,7},{2,4},{3,5},{4,2},{5,3},{6,0},{7,1},{8,14},{9,15},{10,... | collective-permute-start | bytes 200 | tf_op jit(solution)/shard_map/ppermute | solution.py:36
  7.5 0.7 copy-start.13
  8.2 6.5 %collective-permute-start.1 = (s32[2,2,8]{2,1,0:T(2,128)S(1)}, s32[2,2,8]{2,1,0:T(2,128)S(1)}, u32[]{:S(2)}, u32[]{:S(2)}) collective-permute-start(s32[2,2,8]{2,1,0:T(2,128)S(1)} %pad_add_fusion.1), channel_id=1, source_target_pairs={{0,2},{1,3},{2,0},{3,1},{4,6},{5,7},{6,4},{7,5},{8,10},{9,11},{10,... | collective-permute-start | bytes 392 | tf_op jit(solution)/shard_map/ppermute | solution.py:36
  8.2 12.1 %copy-start.20 = (f32[2,8]{1,0:T(2,128)S(1)}, f32[2,8]{1,0:T(2,128)}, u32[]{:S(2)}) copy-start(f32[2,8]{1,0:T(2,128)} %param.12) | copy-start | bytes 196
  8.2 12.2 %copy-start.12 = (s32[2,8]{1,0:T(2,128)S(1)}, s32[2,8]{1,0:T(2,128)}, u32[]{:S(2)}) copy-start(s32[2,8]{1,0:T(2,128)} %param.11) | copy-start | bytes 196
  10.8 9.6 %copy-start.14 = (s32[1,2,8]{2,1,0:T(2,128)S(1)}, s32[1,2,8]{2,1,0:T(2,128)}, u32[]{:S(2)}) copy-start(s32[1,2,8]{2,1,0:T(2,128)} %copy-done.13) | copy-start | bytes 196
  10.8 21.1 %collective-permute-start.4 = (bf16[32,9216]{1,0:T(8,128)(2,1)S(1)}, bf16[32,9216]{1,0:T(8,128)(2,1)S(1)}, u32[]{:S(2)}, u32[]{:S(2)}) collective-permute-start(bf16[32,9216]{1,0:T(8,128)(2,1)S(1)} %get-tuple-element.37), channel_id=1, source_target_pairs={{0,6},{1,7},{2,4},{3,5},{4,2},{5,3},{6,0},{7,1},{8,14},{9,15},{10,... | collective-permute-start | bytes 1769480 | tf_op jit(solution)/shard_map/ppermute | solution.py:36
  14.7 0.6 copy-start.15
  18.4 27.0 %collective-permute-start.2 = (bf16[32,9216]{1,0:T(8,128)(2,1)}, bf16[32,9216]{1,0:T(8,128)(2,1)S(1)}, u32[]{:S(2)}, u32[]{:S(2)}) collective-permute-start(bf16[32,9216]{1,0:T(8,128)(2,1)} %get-tuple-element.35), channel_id=1, source_target_pairs={{0,2},{1,3},{2,0},{3,1},{4,6},{5,7},{6,4},{7,5},{8,10},{9,11},{10,... | collective-permute-start | bytes 1769480 | tf_op jit(solution)/shard_map/ppermute | solution.py:36
  19.6 0.6 copy-start.17
  19.6 47.3 %collective-permute-start.3 = (bf16[32,9216]{1,0:T(8,128)(2,1)}, bf16[32,9216]{1,0:T(8,128)(2,1)S(1)}, u32[]{:S(2)}, u32[]{:S(2)}) collective-permute-start(bf16[32,9216]{1,0:T(8,128)(2,1)} %get-tuple-element.36), channel_id=1, source_target_pairs={{0,4},{1,5},{2,6},{3,7},{4,0},{5,1},{6,2},{7,3},{8,12},{9,13},{10,... | collective-permute-start | bytes 1769480 | tf_op jit(solution)/shard_map/ppermute | solution.py:36
  21.1 3.6 %collective-permute-start.7 = (s32[4,2,8]{2,1,0:T(2,128)S(1)}, s32[4,2,8]{2,1,0:T(2,128)S(1)}, u32[]{:S(2)}, u32[]{:S(2)}) collective-permute-start(s32[4,2,8]{2,1,0:T(2,128)S(1)} %pad_add_fusion), channel_id=1, source_target_pairs={{0,1},{1,0},{2,3},{3,2},{4,5},{5,4},{6,7},{7,6},{8,9},{9,8},{10,11... | collective-permute-start | bytes 776 | tf_op jit(solution)/shard_map/ppermute | solution.py:36
  24.7 0.6 copy-start.16
  29.4 69.8 %collective-permute-start.8 = (bf16[32,9216]{1,0:T(8,128)(2,1)}, bf16[32,9216]{1,0:T(8,128)(2,1)S(1)}, u32[]{:S(2)}, u32[]{:S(2)}) collective-permute-start(bf16[32,9216]{1,0:T(8,128)(2,1)} %get-tuple-element.41), channel_id=1, source_target_pairs={{0,1},{1,0},{2,3},{3,2},{4,5},{5,4},{6,7},{7,6},{8,9},{9,8},{10,11... | collective-permute-start | bytes 1769480 | tf_op jit(solution)/shard_map/ppermute | solution.py:36
  31.0 68.2 %collective-permute-start.9 = (bf16[32,9216]{1,0:T(8,128)(2,1)}, bf16[32,9216]{1,0:T(8,128)(2,1)S(1)}, u32[]{:S(2)}, u32[]{:S(2)}) collective-permute-start(bf16[32,9216]{1,0:T(8,128)(2,1)} %get-tuple-element.42), channel_id=1, source_target_pairs={{0,3},{1,2},{2,1},{3,0},{4,7},{5,6},{6,5},{7,4},{8,11},{9,10},{10,... | collective-permute-start | bytes 1769480 | tf_op jit(solution)/shard_map/ppermute | solution.py:36
  31.9 35.0 %copy-start.3 = (bf16[32,9216]{1,0:T(8,128)(2,1)}, bf16[32,9216]{1,0:T(8,128)(2,1)S(1)}, u32[]{:S(2)}) copy-start(bf16[32,9216]{1,0:T(8,128)(2,1)S(1)} %collective-permute-done.4.refs_3_.refs_5_) | copy-start | bytes 1769476
  31.9 72.5 %collective-permute-start.10 = (bf16[32,9216]{1,0:T(8,128)(2,1)}, bf16[32,9216]{1,0:T(8,128)(2,1)S(1)}, u32[]{:S(2)}, u32[]{:S(2)}) collective-permute-start(bf16[32,9216]{1,0:T(8,128)(2,1)} %get-tuple-element.43), channel_id=1, source_target_pairs={{0,5},{1,4},{2,7},{3,6},{4,1},{5,0},{6,3},{7,2},{8,13},{9,12},{10,... | collective-permute-start | bytes 1769480 | tf_op jit(solution)/shard_map/ppermute | solution.py:36
  45.4 21.5 %copy-start.4 = (bf16[32,9216]{1,0:T(8,128)(2,1)}, bf16[32,9216]{1,0:T(8,128)(2,1)S(1)}, u32[]{:S(2)}) copy-start(bf16[32,9216]{1,0:T(8,128)(2,1)S(1)} %collective-permute-done.2.refs_1_.refs_3_) | copy-start | bytes 1769476
  45.4 58.9 %collective-permute-start.11 = (bf16[32,9216]{1,0:T(8,128)(2,1)}, bf16[32,9216]{1,0:T(8,128)(2,1)}, u32[]{:S(2)}, u32[]{:S(2)}) collective-permute-start(bf16[32,9216]{1,0:T(8,128)(2,1)} %get-tuple-element.44), channel_id=1, source_target_pairs={{0,7},{1,6},{2,5},{3,4},{4,3},{5,2},{6,1},{7,0},{8,15},{9,14},{10,... | collective-permute-start | bytes 1769480 | tf_op jit(solution)/shard_map/ppermute | solution.py:36
  66.9 0.8 copy-start.5
  77.6 1.7 collective-permute-start.5
  80.3 8.4 %collective-permute-start.6 = (f32[2,256,128]{2,1,0:T(8,128)S(1)}, f32[2,256,128]{2,1,0:T(8,128)S(1)}, u32[]{:S(2)}, u32[]{:S(2)}) collective-permute-start(f32[2,256,128]{2,1,0:T(8,128)S(1)} %add.25), channel_id=1, source_target_pairs={{0,16},{8,24},{16,0},{24,8},{1,17},{9,25},{17,1},{25,9},{2,18},{10... | collective-permute-start | bytes 786440 | tf_op jit(solution)/shard_map/ppermute | solution.py:36
  99.1 28.1 %copy-start.22 = (bf16[32,9216]{1,0:T(8,128)(2,1)S(1)}, bf16[32,9216]{1,0:T(8,128)(2,1)}, u32[]{:S(2)}) copy-start(bf16[32,9216]{1,0:T(8,128)(2,1)} %get-tuple-element.53) | copy-start | bytes 1769476
  99.1 31.9 %copy-start.21 = (s32[2,2]{1,0:T(2,128)S(1)}, s32[2,2]{1,0:T(2,128)}, u32[]{:S(2)}) copy-start(s32[2,2]{1,0:T(2,128)} %get-tuple-element.48) | copy-start | bytes 52
  99.1 31.9 %copy-start.18 = (s32[1,2]{1,0:T(1,128)S(1)}, s32[1,2]{1,0:T(1,128)}, u32[]{:S(2)}) copy-start(s32[1,2]{1,0:T(1,128)} %get-tuple-element.49) | copy-start | bytes 28
  99.1 31.9 %copy-start.19 = (s32[1,2]{1,0:T(1,128)S(1)}, s32[1,2]{1,0:T(1,128)}, u32[]{:S(2)}) copy-start(s32[1,2]{1,0:T(1,128)} %get-tuple-element.47) | copy-start | bytes 28
  99.2 5.2 %copy-start.6 = (bf16[32,9216]{1,0:T(8,128)(2,1)}, bf16[32,9216]{1,0:T(8,128)(2,1)S(1)}, u32[]{:S(2)}) copy-start(bf16[32,9216]{1,0:T(8,128)(2,1)S(1)} %collective-permute-done.8.refs_0_.refs_6_) | copy-start | bytes 1769476
  99.2 5.2 %copy-start.7 = (bf16[32,9216]{1,0:T(8,128)(2,1)}, bf16[32,9216]{1,0:T(8,128)(2,1)S(1)}, u32[]{:S(2)}) copy-start(bf16[32,9216]{1,0:T(8,128)(2,1)S(1)} %collective-permute-done.9.refs_1_.refs_7_) | copy-start | bytes 1769476
  104.3 0.8 copy-start.8
  115.0 13.4 %collective-permute-start.12 = (f32[2,256,128]{2,1,0:T(8,128)}, f32[2,256,128]{2,1,0:T(8,128)S(1)}, u32[]{:S(2)}, u32[]{:S(2)}) collective-permute-start(f32[2,256,128]{2,1,0:T(8,128)} %shard_map.108), channel_id=1, source_target_pairs={{0,8},{8,0},{16,24},{24,16},{1,9},{9,1},{17,25},{25,17},{2,10},{10... | collective-permute-start | bytes 786440 | tf_op jit(solution)/shard_map/ppermute | solution.py:36
  115.0 38.7 %collective-permute-start.15 = (bf16[32,9216]{1,0:T(8,128)(2,1)}, bf16[32,9216]{1,0:T(8,128)(2,1)S(1)}, u32[]{:S(2)}, u32[]{:S(2)}) collective-permute-start(bf16[32,9216]{1,0:T(8,128)(2,1)} %get-tuple-element.52), channel_id=1, source_target_pairs={{0,2},{1,3},{2,0},{3,1},{4,6},{5,7},{6,4},{7,5},{8,10},{9,11},{10,... | collective-permute-start | bytes 1769480 | tf_op jit(solution)/shard_map/ppermute | solution.py:36
  127.2 55.1 %collective-permute-start.16 = (bf16[32,9216]{1,0:T(8,128)(2,1)S(1)}, bf16[32,9216]{1,0:T(8,128)(2,1)S(1)}, u32[]{:S(2)}, u32[]{:S(2)}) collective-permute-start(bf16[32,9216]{1,0:T(8,128)(2,1)S(1)} %copy-done.22), channel_id=1, source_target_pairs={{0,4},{1,5},{2,6},{3,7},{4,0},{5,1},{6,2},{7,3},{8,12},{9,13},{10,... | collective-permute-start | bytes 1769480 | tf_op jit(solution)/shard_map/ppermute | solution.py:36
  129.4 8.4 %collective-permute-start.13 = (f32[2,256,128]{2,1,0:T(8,128)S(1)}, f32[2,256,128]{2,1,0:T(8,128)S(1)}, u32[]{:S(2)}, u32[]{:S(2)}) collective-permute-start(f32[2,256,128]{2,1,0:T(8,128)S(1)} %add.27), channel_id=1, source_target_pairs={{0,16},{8,24},{16,0},{24,8},{1,17},{9,25},{17,1},{25,9},{2,18},{10... | collective-permute-start | bytes 786440 | tf_op jit(solution)/shard_map/ppermute | solution.py:36
  131.6 67.9 %collective-permute-start.17 = (bf16[32,9216]{1,0:T(8,128)(2,1)}, bf16[32,9216]{1,0:T(8,128)(2,1)S(1)}, u32[]{:S(2)}, u32[]{:S(2)}) collective-permute-start(bf16[32,9216]{1,0:T(8,128)(2,1)} %get-tuple-element.54), channel_id=1, source_target_pairs={{0,6},{1,7},{2,4},{3,5},{4,2},{5,3},{6,0},{7,1},{8,14},{9,15},{10,... | collective-permute-start | bytes 1769480 | tf_op jit(solution)/shard_map/ppermute | solution.py:36
  148.3 88.4 %collective-permute-start.14 = (bf16[32,9216]{1,0:T(8,128)(2,1)}, bf16[32,9216]{1,0:T(8,128)(2,1)}, u32[]{:S(2)}, u32[]{:S(2)}) collective-permute-start(bf16[32,9216]{1,0:T(8,128)(2,1)} %get-tuple-element.50), channel_id=1, source_target_pairs={{0,7},{1,6},{2,5},{3,4},{4,3},{5,2},{6,1},{7,0},{8,15},{9,14},{10,... | collective-permute-start | bytes 1769480 | tf_op jit(solution)/shard_map/ppermute | solution.py:36
  149.7 58.7 %collective-permute-start.18 = (bf16[32,9216]{1,0:T(8,128)(2,1)}, bf16[32,9216]{1,0:T(8,128)(2,1)S(1)}, u32[]{:S(2)}, u32[]{:S(2)}) collective-permute-start(bf16[32,9216]{1,0:T(8,128)(2,1)} %get-tuple-element.55), channel_id=1, source_target_pairs={{0,1},{1,0},{2,3},{3,2},{4,5},{5,4},{6,7},{7,6},{8,9},{9,8},{10,11... | collective-permute-start | bytes 1769480 | tf_op jit(solution)/shard_map/ppermute | solution.py:36
  153.7 45.8 %copy-start = (bf16[32,9216]{1,0:T(8,128)(2,1)}, bf16[32,9216]{1,0:T(8,128)(2,1)S(1)}, u32[]{:S(2)}) copy-start(bf16[32,9216]{1,0:T(8,128)(2,1)S(1)} %collective-permute-done.15.refs_1_.refs_4_.refs_2_) | copy-start | bytes 1769476
  153.7 54.8 %collective-permute-start.19 = (bf16[32,9216]{1,0:T(8,128)(2,1)}, bf16[32,9216]{1,0:T(8,128)(2,1)S(1)}, u32[]{:S(2)}, u32[]{:S(2)}) collective-permute-start(bf16[32,9216]{1,0:T(8,128)(2,1)} %get-tuple-element.56), channel_id=1, source_target_pairs={{0,3},{1,2},{2,1},{3,0},{4,7},{5,6},{6,5},{7,4},{8,11},{9,10},{10,... | collective-permute-start | bytes 1769480 | tf_op jit(solution)/shard_map/ppermute | solution.py:36
  182.3 17.2 %copy-start.1 = (bf16[32,9216]{1,0:T(8,128)(2,1)}, bf16[32,9216]{1,0:T(8,128)(2,1)S(1)}, u32[]{:S(2)}) copy-start(bf16[32,9216]{1,0:T(8,128)(2,1)S(1)} %collective-permute-done.16.refs_2_.refs_5_.refs_3_) | copy-start | bytes 1769476
  182.3 49.7 %collective-permute-start.20 = (bf16[32,9216]{1,0:T(8,128)(2,1)}, bf16[32,9216]{1,0:T(8,128)(2,1)S(1)}, u32[]{:S(2)}, u32[]{:S(2)}) collective-permute-start(bf16[32,9216]{1,0:T(8,128)(2,1)} %get-tuple-element.57), channel_id=1, source_target_pairs={{0,5},{1,4},{2,7},{3,6},{4,1},{5,0},{6,3},{7,2},{8,13},{9,12},{10,... | collective-permute-start | bytes 1769480 | tf_op jit(solution)/shard_map/ppermute | solution.py:36
  199.5 0.9 copy-start.2
  208.5 23.6 %copy-start.9 = (bf16[32,9216]{1,0:T(8,128)(2,1)}, bf16[32,9216]{1,0:T(8,128)(2,1)S(1)}, u32[]{:S(2)}) copy-start(bf16[32,9216]{1,0:T(8,128)(2,1)S(1)} %collective-permute-done.18.refs_0_.refs_5_) | copy-start | bytes 1769476
  208.5 23.5 %copy-start.10 = (bf16[32,9216]{1,0:T(8,128)(2,1)}, bf16[32,9216]{1,0:T(8,128)(2,1)S(1)}, u32[]{:S(2)}) copy-start(bf16[32,9216]{1,0:T(8,128)(2,1)S(1)} %collective-permute-done.19.refs_1_.refs_6_) | copy-start | bytes 1769476
  232.0 0.8 copy-start.11

commit v3 on v2

--- a/solution.py
+++ b/solution.py
@@ -38,7 +38,10 @@
 
 def pick_kernel(groups, me_ref, ids_ref, fin, fout, table_ref, *refs):
     outs = refs[:groups]
-    (in_sem,) = refs[groups:]
+    in_sem, ids, ids_sem = refs[groups:]
+    fetch = pltpu.make_async_copy(ids_ref, ids, ids_sem)
+    fetch.start()
+    fetch.wait()
     exp_count, rank, wide = fin.shape
     base = me_ref[0] * exp_count
     loads = []
@@ -47,7 +50,7 @@
         picks = [jnp.int32(-1)] * CAP
         for b in range(ids_ref.shape[1]):
             for k in range(ids_ref.shape[2]):
-                local = ids_ref[m, b, k] - base
+                local = ids[m, b, k] - base
                 mine = (local >= 0) & (local < exp_count)
                 for c in range(CAP):
                     picks[c] = jnp.where(mine & (found == c), local, picks[c])
@@ -177,36 +180,45 @@
         out_ref[s] = total[:, wide:].astype(BF)
 
 
-def finish_kernel(late, early, late_ref, early_ref, *refs):
+def fresh(table_ref, s):
+    new = table_ref[s] >= 0
+    for r in range(s):
+        new = new & (table_ref[r] != table_ref[s])
+    return new
+
+
+def stores(table_ref, s, stage, in_hbm, out_hbm, out_sem):
+    e = jnp.maximum(table_ref[s], 0)
+    wide, narrow = in_hbm.shape[2], out_hbm.shape[2]
+    return (
+        pltpu.make_async_copy(stage.at[s, :, pl.ds(0, wide)], in_hbm.at[e], out_sem.at[s, 0]),
+        pltpu.make_async_copy(stage.at[s, :, pl.ds(wide, narrow)], out_hbm.at[e], out_sem.at[s, 1]),
+    )
+
+
+def finish_kernel(late, early, ends, late_ref, early_ref, end_ref, *refs):
     a, b = late // CAP, early // CAP
     late_refs, early_hbm = refs[:a], refs[a : a + b]
-    in_hbm, out_hbm, kept, stage, total, kept_sem, out_sem = refs[a + b + 2 :]
-    rank, full = total.shape
-    wide = in_hbm.shape[2]
+    in_hbm, out_hbm, ahead, kept, stage, total, kept_sem, out_sem = refs[a + b + 2 :]
+    rank, _ = total.shape
+
+    def load_early(m):
+        return pltpu.make_async_copy(place(early_hbm, m, rank), kept.at[m], kept_sem.at[m])
 
     def used(m):
         hit = late_ref[0] == early_ref[m]
         for s in range(1, late):
             hit = hit | (late_ref[s] == early_ref[m])
+        for s in range(ends):
+            hit = hit | (end_ref[s] == early_ref[m])
         return hit & (early_ref[m] >= 0)
 
-    def first(s):
-        fresh = late_ref[s] >= 0
-        for r in range(s):
-            fresh = fresh & (late_ref[r] != late_ref[s])
-        return fresh
-
-    def load_early(m):
-        return pltpu.make_async_copy(place(early_hbm, m, rank), kept.at[m], kept_sem.at[m])
-
-    def stores(s):
-        e = jnp.maximum(late_ref[s], 0)
-        return (
-            pltpu.make_async_copy(stage.at[s, :, pl.ds(0, wide)], in_hbm.at[e], out_sem.at[s, 0]),
-            pltpu.make_async_copy(
-                stage.at[s, :, pl.ds(wide, full - wide)], out_hbm.at[e], out_sem.at[s, 1]
-            ),
-        )
+    def add(e, known, known_ref, terms):
+        for m in range(known):
+
+            @pl.when((known_ref[m] == e) & (e >= 0))
+            def _():
+                total[...] += terms(m)[...].astype(F32)
 
     for m in range(early):
 
@@ -214,33 +226,64 @@
         def _():
             load_early(m).start()
 
+    for m in range(early):
+
+        @pl.when(used(m))
+        def _():
+            load_early(m).wait()
+
     for s in range(late):
 
-        @pl.when(first(s))
-        def _():
-            total[...] = place(late_refs, s, rank)[...].astype(F32)
-            for r in range(s + 1, late):
-
-                @pl.when(late_ref[r] == late_ref[s])
+        @pl.when(fresh(late_ref, s))
+        def _():
+            total[...] = jnp.zeros_like(total)
+            add(late_ref[s], late, late_ref, lambda m: place(late_refs, m, rank))
+            add(late_ref[s], early, early_ref, lambda m: kept.at[m])
+            stage[s] = total[...].astype(BF)
+            for store in stores(late_ref, s, stage, in_hbm, out_hbm, out_sem):
+                store.start()
+
+    for s in range(ends):
+        total[...] = jnp.zeros_like(total)
+        add(end_ref[s], late, late_ref, lambda m: place(late_refs, m, rank))
+        add(end_ref[s], early, early_ref, lambda m: kept.at[m])
+        ahead[s] = total[...]
+
+    for s in range(late):
+
+        @pl.when(fresh(late_ref, s))
+        def _():
+            for store in stores(late_ref, s, stage, in_hbm, out_hbm, out_sem):
+                store.wait()
+
+
+def end_kernel(ends, end_ref, *refs):
+    end_refs, ahead = refs[: ends // CAP], refs[ends // CAP]
+    in_hbm, out_hbm, stage, out_sem = refs[ends // CAP + 3 :]
+    rank = stage.shape[1]
+    for s in range(ends):
+
+        @pl.when(fresh(end_ref, s))
+        def _():
+            stage[s] = (place(end_refs, s, rank)[...].astype(F32) + ahead[s]).astype(BF)
+            for r in range(s + 1, ends):
+
+                @pl.when(end_ref[r] == end_ref[s])
                 def _():
-                    total[...] += place(late_refs, r, rank)[...].astype(F32)
-
-            for m in range(early):
-
-                @pl.when(late_ref[s] == early_ref[m])
-                def _():
-                    load_early(m).wait()
-                    total[...] += kept[m].astype(F32)
-
-            stage[s] = total[...].astype(BF)
-            for store in stores(s):
+                    total = ahead[s]
+                    for m in range(s, ends):
+                        same = (end_ref[m] == end_ref[s]).astype(F32)
+                        total = total + same * place(end_refs, m, rank)[...].astype(F32)
+                    stage[s] = total.astype(BF)
+
+            for store in stores(end_ref, s, stage, in_hbm, out_hbm, out_sem):
                 store.start()
 
-    for s in range(late):
-
-        @pl.when(first(s))
-        def _():
-            for store in stores(s):
+    for s in range(ends):
+
+        @pl.when(fresh(end_ref, s))
+        def _():
+            for store in stores(end_ref, s, stage, in_hbm, out_hbm, out_sem):
                 store.wait()
 
 
@@ -267,10 +310,14 @@
             functools.partial(pick_kernel, count),
             out_shape=[jax.ShapeDtypeStruct((count, CAP), jnp.int32)]
             + [pltpu.VMEM((both, full), BF) if fast else piece] * count,
-            in_specs=[SMEM, SMEM, HBM, HBM],
+            in_specs=[SMEM, VMEM, HBM, HBM],
             out_specs=[SMEM] + [VMEM] * count,
-            scratch_shapes=[pltpu.SemaphoreType.DMA((count, CAP, 2))],
-        )(me_arr, lists, factor_in, factor_out)
+            scratch_shapes=[
+                pltpu.SemaphoreType.DMA((count, CAP, 2)),
+                pltpu.SMEM(lists.shape, jnp.int32),
+                pltpu.SemaphoreType.DMA,
+            ],
+        )(me_arr, pltpu.with_memory_space_constraint(lists, pltpu.VMEM), factor_in, factor_out)
 
     steps, chunks, homes = plan(groups)
     lists, known = adapter_ids[None], [0]
@@ -382,25 +429,37 @@
         scratch_shapes=[pltpu.VMEM((rank, full), F32)],
         name="collect",
     )(tables[0], *[back[d] for d in stages[0]])
-    seen, seen_table = list(stages[0]), tables[0]
-    for n in (1, 2):
-        late, early = len(stages[n]) * CAP, len(seen) * CAP
-        arrays = len(stages[n]) + len(seen)
-        grads = pl.pallas_call(
-            functools.partial(finish_kernel, late, early),
-            out_shape=[jax.ShapeDtypeStruct(g.shape, BF) for g in grads],
-            in_specs=[SMEM] * 2 + [VMEM] * len(stages[n]) + [ANY] * len(seen) + [HBM] * 2,
-            out_specs=[HBM] * 2,
-            scratch_shapes=[
-                pltpu.VMEM((early, rank, full), BF),
-                pltpu.VMEM((late, rank, full), BF),
-                pltpu.VMEM((rank, full), F32),
-                pltpu.SemaphoreType.DMA((early,)),
-                pltpu.SemaphoreType.DMA((late, 2)),
-            ],
-            input_output_aliases={arrays + 2: 0, arrays + 3: 1},
-        )(tables[n], seen_table, *[back[d] for d in stages[n] + seen], *grads)
-        seen, seen_table = seen + stages[n], jnp.concatenate([seen_table, tables[n]])
+    late, ends = len(stages[1]) * CAP, len(stages[2]) * CAP
+    arrays = len(stages[0]) + len(stages[1])
+    *grads, ahead = pl.pallas_call(
+        functools.partial(finish_kernel, late, early, ends),
+        out_shape=[jax.ShapeDtypeStruct(g.shape, BF) for g in grads]
+        + [pltpu.VMEM((ends, rank, full), F32)],
+        in_specs=[SMEM] * 3 + [VMEM] * len(stages[1]) + [ANY] * len(stages[0]) + [HBM] * 2,
+        out_specs=[HBM] * 2 + [VMEM],
+        scratch_shapes=[
+            pltpu.VMEM((early, rank, full), BF),
+            pltpu.VMEM((late, rank, full), BF),
+            pltpu.VMEM((rank, full), F32),
+            pltpu.SemaphoreType.DMA((early,)),
+            pltpu.SemaphoreType.DMA((late, 2)),
+        ],
+        input_output_aliases={arrays + 3: 0, arrays + 4: 1},
+        name="finish1",
+    )(tables[1], tables[0], tables[2], *[back[d] for d in stages[1] + stages[0]], *grads)
+    on_chip = [pltpu.with_memory_space_constraint(back[d], pltpu.VMEM) for d in stages[2]]
+    grads = pl.pallas_call(
+        functools.partial(end_kernel, ends),
+        out_shape=[jax.ShapeDtypeStruct(g.shape, BF) for g in grads],
+        in_specs=[SMEM] + [VMEM] * (len(stages[2]) + 1) + [HBM] * 2,
+        out_specs=[HBM] * 2,
+        scratch_shapes=[
+            pltpu.VMEM((ends, rank, full), BF),
+            pltpu.SemaphoreType.DMA((ends, 2)),
+        ],
+        input_output_aliases={len(stages[2]) + 2: 0, len(stages[2]) + 3: 1},
+        name="finish2",
+    )(tables[2], *on_chip, pltpu.with_memory_space_constraint(ahead, pltpu.VMEM), *grads)
     grad_factor_in, grad_factor_out = grads
     return (input_grad, grad_factor_in, grad_factor_out, router_grad)
 

time: 241 us -> 240 us (level)
  waiting for transfers between devices: 92.1 us -> 97.7 us
  local copies, waits for them, and re-layouts: 10.8 us -> 6.54 us
  other arithmetic: 10.6 us -> 6.78 us
    ppermute x21, waiting for transfers between devices: 92.1 us -> 97.7 us  [swap(): return lax.ppermute(x, axis, [(i, i ^ offset) for i in range(count)])]
  transfers between devices with their start and end apart: 21 -> 21, of which waited for: 9 -> 9; matrix products, arithmetic and copies ran while one was open for 7% -> 4% of each run, Pallas kernels for 26% -> 27%
where the time goes in v3:
time: 240 us; the launch traced here: 239 us
  waiting for transfers between devices  97.7 us (41%)
  Pallas kernels  75.1 us (31%)
  starting transfers between devices  51.6 us (22%)
  other arithmetic  6.78 us (3%)
  local copies, waits for them, and re-layouts  6.54 us (3%)
    ppermute x21, waiting for transfers between devices, swap(): return lax.ppermute(x, axis, [(i, i ^ offset) for i in range(count)])  97.7 us
    ppermute x21, starting transfers between devices, swap(): return lax.ppermute(x, axis, [(i, i ^ offset) for i in range(count)])  51.6 us
    pallas_call x2, Pallas kernels, body(): pl.pallas_call(functools.partial(project_kernel, count, in_tiles, tiles),...  19.7 us
    pallas_call x2, Pallas kernels, body(): pl.pallas_call(functools.partial(term_kernel, count, in_tiles), out_shape...  19.5 us
    pallas_call x4, Pallas kernels, pick(): pl.pallas_call(functools.partial(pick_kernel, count), out_shape=[jax.Shap...  11.8 us
    pallas_call x1, Pallas kernels, body(): pl.pallas_call(functools.partial(input_kernel, len(chunks), groups), out_...  9.47 us
    pallas_call x1, Pallas kernels, body(): pl.pallas_call(functools.partial(collect_kernel, early), out_shape=[jax.S...  8.09 us
    pallas_call x1, Pallas kernels, body(): pl.pallas_call(functools.partial(finish_kernel, late, early, ends), out_s...  4.89 us
  transfers between devices with their start and end apart: 21, of which 9 were waited for; matrix products, arithmetic and copies ran while one was open for 4% of the time, Pallas kernels for 27%

profile of v3, /device:TPU:0, one launch (start us, length us, event | category | flops | bytes accessed | tf_op | source)
XLA Modules:
  0.0 238.8 jit_solution(3657210989446508221)
XLA Ops:
  0.6 5.1 %collective-permute-start = (s32[1,2,8]{2,1,0:T(2,128)}, s32[1,2,8]{2,1,0:T(2,128)S(1)}, u32[]{:S(2)}, u32[]{:S(2)}) collective-permute-start(s32[1,2,8]{2,1,0:T(2,128)} %bitcast.18), channel_id=1, source_target_pairs={{0,6},{1,7},{2,4},{3,5},{4,2},{5,3},{6,0},{7,1},{8,14},{9,15},{10,... | collective-permute-start | bytes 200 | tf_op jit(solution)/shard_map/ppermute | solution.py:36
  5.8 0.8 reshape.172
  6.6 0.7 broadcast_xor_fusion
  7.5 0.7 pad_add_fusion.1
  8.2 2.3 shard_map.104
  10.5 3.9 %collective-permute-start.4 = (bf16[32,9216]{1,0:T(8,128)(2,1)S(1)}, bf16[32,9216]{1,0:T(8,128)(2,1)S(1)}, u32[]{:S(2)}, u32[]{:S(2)}) collective-permute-start(bf16[32,9216]{1,0:T(8,128)(2,1)S(1)} %get-tuple-element.38), channel_id=1, source_target_pairs={{0,6},{1,7},{2,4},{3,5},{4,2},{5,3},{6,0},{7,1},{8,14},{9,15},{10,... | collective-permute-start | bytes 1769480 | tf_op jit(solution)/shard_map/ppermute | solution.py:36
  14.4 3.1 %shard_map.103 = (s32[2,2]{1,0:T(2,128)}, bf16[32,9216]{1,0:T(8,128)(2,1)}, bf16[32,9216]{1,0:T(8,128)(2,1)}) custom-call(s32[1]{0:T(128)} %bitcast.1.me_ref, s32[2,2,8]{2,1,0:T(2,128)S(1)} %collective-permute-done.1.ids_ref, bf16[32,16,7168]{2,1,0:T(8,128)(2,1)} %fin.7, bf16[32,16,2048]{2,1,0:T(8,128)(2,1)} %fout.7), custom_call_target="tpu_custom_call" | custom-call | tf_op jit(solution)/shard_map/pallas_call | solution.py:309
  17.5 1.2 collective-permute-start.2
  18.6 0.7 collective-permute-start.3
  19.6 1.6 collective-permute-start.7
  21.4 1.9 collective-permute-done.7.ids_ref
  23.2 4.0 %shard_map.107 = (s32[4,2]{1,0:T(4,128)}, bf16[32,9216]{1,0:T(8,128)(2,1)}, bf16[32,9216]{1,0:T(8,128)(2,1)}, bf16[32,9216]{1,0:T(8,128)(2,1)}, bf16[32,9216]{1,0:T(8,128)(2,1)}) custom-call(s32[1]{0:T(128)} %bitcast.1.me_ref, s32[4,2,8]{2,1,0:T(2,128)S(1)} %collective-permute-done.7.ids_ref, bf16[32,16,7168]{2,1,0:T(8,128)(2,1)} %fin.7, ...), custom_call_target="tpu_custom_call" | custom-call | tf_op jit(solution)/shard_map/pallas_call | solution.py:309
  27.2 1.6 collective-permute-start.8
  28.8 0.8 collective-permute-start.9
  29.5 15.6 %collective-permute-start.10 = (bf16[32,9216]{1,0:T(8,128)(2,1)}, bf16[32,9216]{1,0:T(8,128)(2,1)S(1)}, u32[]{:S(2)}, u32[]{:S(2)}) collective-permute-start(bf16[32,9216]{1,0:T(8,128)(2,1)} %get-tuple-element.44), channel_id=1, source_target_pairs={{0,5},{1,4},{2,7},{3,6},{4,1},{5,0},{6,3},{7,2},{8,13},{9,12},{10,... | collective-permute-start | bytes 1769480 | tf_op jit(solution)/shard_map/ppermute | solution.py:36
  45.7 2.6 %shard_map.102 = (s32[1,2]{1,0:T(1,128)}, bf16[32,9216]{1,0:T(8,128)(2,1)}) custom-call(s32[1]{0:T(128)} %bitcast.1.me_ref, s32[1,2,8]{2,1,0:T(2,128)S(1)} %bitcast.21, bf16[32,16,7168]{2,1,0:T(8,128)(2,1)} %fin.7, bf16[32,16,2048]{2,1,0:T(8,128)(2,1)} %fout.7), custom_call_target="tpu_custom_call" | custom-call | tf_op jit(solution)/shard_map/pallas_call | solution.py:309
  48.3 18.3 %collective-permute-done.3.refs_2_.refs_4_ = bf16[32,9216]{1,0:T(8,128)(2,1)S(1)} collective-permute-done((bf16[32,9216]{1,0:T(8,128)(2,1)}, bf16[32,9216]{1,0:T(8,128)(2,1)S(1)}, u32[]{:S(2)}, u32[]{:S(2)}) %collective-permute-start.3) | collective-permute-done | bytes 589856 | tf_op jit(solution)/shard_map/ppermute | solution.py:36
  66.6 0.8 copy-done.3
  67.4 9.9 %shard_map.105 = f32[2,256,128]{2,1,0:T(8,128)} custom-call(f32[2,128]{1,0:T(2,128)} %get-tuple-element.74.mask_ref, bf16[512,7168]{1,0:T(8,128)(2,1)} %x_ref.7, bf16[512,2048]{1,0:T(8,128)(2,1)} %g_ref.7, bf16[32,9216]{1,0:T(8,128)(2,1)} %get-tuple-element.35.refs_0_.refs_2_, bf16[32,9216]{1,0:T(8,128)(2,1)} %copy-done.2, bf16[32,9216]{1,0:T(8,128)(2,1)} %copy-done.3, ...), custom_call_target="tpu_custom_call" | custom-call | tf_op jit(solution)/shard_map/pallas_call | solution.py:369
  77.3 1.7 collective-permute-done.5
  79.0 1.0 add.25
  80.0 1.8 collective-permute-start.6
  82.6 5.8 %collective-permute-done.6 = f32[2,256,128]{2,1,0:T(8,128)S(1)} collective-permute-done((f32[2,256,128]{2,1,0:T(8,128)S(1)}, f32[2,256,128]{2,1,0:T(8,128)S(1)}, u32[]{:S(2)}, u32[]{:S(2)}) %collective-permute-start.6) | collective-permute-done | bytes 262176 | tf_op jit(solution)/shard_map/ppermute | solution.py:36
  88.4 0.7 add.26.sums_ref
  89.2 9.7 %shard_map.106 = (bf16[32,9216]{1,0:T(8,128)(2,1)}, bf16[32,9216]{1,0:T(8,128)(2,1)}, bf16[32,9216]{1,0:T(8,128)(2,1)}, bf16[32,9216]{1,0:T(8,128)(2,1)}, bf16[512,128]{1,0:T(8,128)(2,1)}) custom-call(f32[2,256,128]{2,1,0:T(8,128)} %add.26.sums_ref, f32[2,128]{1,0:T(2,128)} %get-tuple-element.73.weight_ref, bf16[512,7168]{1,0:T(8,128)(2,1)} %x_ref.7, ...), custom_call_target="tpu_custom_call" | custom-call | tf_op jit(solution)/shard_map/pallas_call | solution.py:381
  98.9 5.1 %collective-permute-done.10.refs_2_.refs_8_ = bf16[32,9216]{1,0:T(8,128)(2,1)S(1)} collective-permute-done((bf16[32,9216]{1,0:T(8,128)(2,1)}, bf16[32,9216]{1,0:T(8,128)(2,1)S(1)}, u32[]{:S(2)}, u32[]{:S(2)}) %collective-permute-start.10) | collective-permute-done | bytes 589856 | tf_op jit(solution)/shard_map/ppermute | solution.py:36
  104.0 0.8 copy-done.5
  104.9 9.9 %shard_map.108 = f32[2,256,128]{2,1,0:T(8,128)} custom-call(f32[2,128]{1,0:T(2,128)} %get-tuple-element.41.mask_ref, bf16[512,7168]{1,0:T(8,128)(2,1)} %x_ref.7, bf16[512,2048]{1,0:T(8,128)(2,1)} %g_ref.7, bf16[32,9216]{1,0:T(8,128)(2,1)} %copy-done.4, bf16[32,9216]{1,0:T(8,128)(2,1)} %collective-permute-done.9.refs_1_.refs_7_, bf16[32,9216]{1,0:T(8,128)(2,1)} %copy-done.5, ...), custom_call_target="tpu_custom_call" | custom-call | tf_op jit(solution)/shard_map/pallas_call | solution.py:369
  114.8 12.2 %collective-permute-start.18 = (bf16[32,9216]{1,0:T(8,128)(2,1)}, bf16[32,9216]{1,0:T(8,128)(2,1)S(1)}, u32[]{:S(2)}, u32[]{:S(2)}) collective-permute-start(bf16[32,9216]{1,0:T(8,128)(2,1)} %get-tuple-element.56), channel_id=1, source_target_pairs={{0,2},{1,3},{2,0},{3,1},{4,6},{5,7},{6,4},{7,5},{8,10},{9,11},{10,... | collective-permute-start | bytes 1769480 | tf_op jit(solution)/shard_map/ppermute | solution.py:36
  127.0 1.3 collective-permute-start.19
  128.2 1.0 add.27
  129.2 1.6 collective-permute-start.13
  130.8 0.7 pad_add_fusion.3.table_ref.early_ref
  131.5 1.4 collective-permute-start.20
  132.9 4.7 %collective-permute-done.13 = f32[2,256,128]{2,1,0:T(8,128)S(1)} collective-permute-done((f32[2,256,128]{2,1,0:T(8,128)S(1)}, f32[2,256,128]{2,1,0:T(8,128)S(1)}, u32[]{:S(2)}, u32[]{:S(2)}) %collective-permute-start.13) | collective-permute-done | bytes 262176 | tf_op jit(solution)/shard_map/ppermute | solution.py:36
  137.6 0.7 add.28.sums_ref
  138.3 9.8 %shard_map.109 = (bf16[32,9216]{1,0:T(8,128)(2,1)}, bf16[32,9216]{1,0:T(8,128)(2,1)}, bf16[32,9216]{1,0:T(8,128)(2,1)}, bf16[32,9216]{1,0:T(8,128)(2,1)}, bf16[512,128]{1,0:T(8,128)(2,1)}) custom-call(f32[2,256,128]{2,1,0:T(8,128)} %add.28.sums_ref, f32[2,128]{1,0:T(2,128)} %get-tuple-element.72.weight_ref, bf16[512,7168]{1,0:T(8,128)(2,1)} %x_ref.7, ...), custom_call_target="tpu_custom_call" | custom-call | tf_op jit(solution)/shard_map/pallas_call | solution.py:381
  148.1 1.5 collective-permute-start.14
  149.6 1.5 collective-permute-start.15
  151.1 2.2 collective-permute-done.18.refs_1_.refs_4_
  153.4 28.9 %collective-permute-done.19.refs_2_.refs_5_ = bf16[32,9216]{1,0:T(8,128)(2,1)S(1)} collective-permute-done((bf16[32,9216]{1,0:T(8,128)(2,1)}, bf16[32,9216]{1,0:T(8,128)(2,1)S(1)}, u32[]{:S(2)}, u32[]{:S(2)}) %collective-permute-start.19) | collective-permute-done | bytes 589856 | tf_op jit(solution)/shard_map/ppermute | solution.py:36
  184.1 0.7 reduce_sum.72
  184.7 9.5 %input.1 = f32[512,7168]{1,0:T(8,128)} custom-call(bf16[512,128]{1,0:T(8,128)(2,1)} %get-tuple-element.40.refs_0_, bf16[512,128]{1,0:T(8,128)(2,1)} %get-tuple-element.46.refs_1_, bf16[32,9216]{1,0:T(8,128)(2,1)} %get-tuple-element.35.refs_0_.refs_2_, bf16[32,9216]{1,0:T(8,128)(2,1)} %copy-done.2, bf16[32,9216]{1,0:T(8,128)(2,1)} %copy-done.3, ...), custom_call_target="tpu_custom_call" | custom-call | tf_op jit(solution)/shard_map/input/pallas_call | solution.py:396
  194.2 0.8 copy-done.8
  195.1 8.1 %collect.1 = (bf16[32,16,7168]{2,1,0:T(8,128)(2,1)}, bf16[32,16,2048]{2,1,0:T(8,128)(2,1)}) custom-call(s32[8]{0:T(128)} %pad_add_fusion.3.table_ref.early_ref, bf16[32,9216]{1,0:T(8,128)(2,1)} %get-tuple-element.55.refs_0_.refs_3_, bf16[32,9216]{1,0:T(8,128)(2,1)} %copy-done.6, bf16[32,9216]{1,0:T(8,128)(2,1)} %copy-done.7, bf16[32,9216]{1,0:T(8,128)(2,1)} %copy-done.8), custom_call_target="tpu_custom_call" | custom-call | tf_op jit(solution)/shard_map/collect/pallas_call | solution.py:417
  203.2 28.9 %collective-permute-done.17.refs_2_ = bf16[32,9216]{1,0:T(8,128)(2,1)} collective-permute-done((bf16[32,9216]{1,0:T(8,128)(2,1)}, bf16[32,9216]{1,0:T(8,128)(2,1)}, u32[]{:S(2)}, u32[]{:S(2)}) %collective-permute-start.17) | collective-permute-done | bytes 589856 | tf_op jit(solution)/shard_map/ppermute | solution.py:36
  232.1 4.9 %finish1.1 = (bf16[32,16,7168]{2,1,0:T(8,128)(2,1)}, bf16[32,16,2048]{2,1,0:T(8,128)(2,1)}, f32[2,16,9216]{2,1,0:T(8,128)S(1)}) custom-call(s32[6]{0:T(128)} %pad_add_fusion.2.late_ref, s32[8]{0:T(128)} %pad_add_fusion.3.table_ref.early_ref, s32[2]{0:T(128)} %get-tuple-element.71.end_ref, ...), custom_call_target="tpu_custom_call", output_to_operand_aliasing={{0}: (10, {}), {1}: (11, {})} | custom-call | tf_op jit(solution)/shard_map/finish1/pallas_call | solution.py:434
  237.0 1.6 finish2.1
  (75 shorter events, 4.1 us)
Async XLA Ops:
  0.6 6.9 %collective-permute-start = (s32[1,2,8]{2,1,0:T(2,128)}, s32[1,2,8]{2,1,0:T(2,128)S(1)}, u32[]{:S(2)}, u32[]{:S(2)}) collective-permute-start(s32[1,2,8]{2,1,0:T(2,128)} %bitcast.18), channel_id=1, source_target_pairs={{0,6},{1,7},{2,4},{3,5},{4,2},{5,3},{6,0},{7,1},{8,14},{9,15},{10,... | collective-permute-start | bytes 200 | tf_op jit(solution)/shard_map/ppermute | solution.py:36
  8.2 6.2 %collective-permute-start.1 = (s32[2,2,8]{2,1,0:T(2,128)S(1)}, s32[2,2,8]{2,1,0:T(2,128)S(1)}, u32[]{:S(2)}, u32[]{:S(2)}) collective-permute-start(s32[2,2,8]{2,1,0:T(2,128)S(1)} %pad_add_fusion.1), channel_id=1, source_target_pairs={{0,2},{1,3},{2,0},{3,1},{4,6},{5,7},{6,4},{7,5},{8,10},{9,11},{10,... | collective-permute-start | bytes 392 | tf_op jit(solution)/shard_map/ppermute | solution.py:36
  8.2 11.2 %copy-start.13 = (f32[2,8]{1,0:T(2,128)S(1)}, f32[2,8]{1,0:T(2,128)}, u32[]{:S(2)}) copy-start(f32[2,8]{1,0:T(2,128)} %param.12) | copy-start | bytes 196
  8.2 11.3 %copy-start = (s32[2,8]{1,0:T(2,128)S(1)}, s32[2,8]{1,0:T(2,128)}, u32[]{:S(2)}) copy-start(s32[2,8]{1,0:T(2,128)} %param.11) | copy-start | bytes 196
  10.5 19.0 %collective-permute-start.4 = (bf16[32,9216]{1,0:T(8,128)(2,1)S(1)}, bf16[32,9216]{1,0:T(8,128)(2,1)S(1)}, u32[]{:S(2)}, u32[]{:S(2)}) collective-permute-start(bf16[32,9216]{1,0:T(8,128)(2,1)S(1)} %get-tuple-element.38), channel_id=1, source_target_pairs={{0,6},{1,7},{2,4},{3,5},{4,2},{5,3},{6,0},{7,1},{8,14},{9,15},{10,... | collective-permute-start | bytes 1769480 | tf_op jit(solution)/shard_map/ppermute | solution.py:36
  17.5 27.7 %collective-permute-start.2 = (bf16[32,9216]{1,0:T(8,128)(2,1)}, bf16[32,9216]{1,0:T(8,128)(2,1)S(1)}, u32[]{:S(2)}, u32[]{:S(2)}) collective-permute-start(bf16[32,9216]{1,0:T(8,128)(2,1)} %get-tuple-element.36), channel_id=1, source_target_pairs={{0,2},{1,3},{2,0},{3,1},{4,6},{5,7},{6,4},{7,5},{8,10},{9,11},{10,... | collective-permute-start | bytes 1769480 | tf_op jit(solution)/shard_map/ppermute | solution.py:36
  18.6 48.0 %collective-permute-start.3 = (bf16[32,9216]{1,0:T(8,128)(2,1)}, bf16[32,9216]{1,0:T(8,128)(2,1)S(1)}, u32[]{:S(2)}, u32[]{:S(2)}) collective-permute-start(bf16[32,9216]{1,0:T(8,128)(2,1)} %get-tuple-element.37), channel_id=1, source_target_pairs={{0,4},{1,5},{2,6},{3,7},{4,0},{5,1},{6,2},{7,3},{8,12},{9,13},{10,... | collective-permute-start | bytes 1769480 | tf_op jit(solution)/shard_map/ppermute | solution.py:36
  19.6 3.7 %collective-permute-start.7 = (s32[4,2,8]{2,1,0:T(2,128)S(1)}, s32[4,2,8]{2,1,0:T(2,128)S(1)}, u32[]{:S(2)}, u32[]{:S(2)}) collective-permute-start(s32[4,2,8]{2,1,0:T(2,128)S(1)} %pad_add_fusion), channel_id=1, source_target_pairs={{0,1},{1,0},{2,3},{3,2},{4,5},{5,4},{6,7},{7,6},{8,9},{9,8},{10,11... | collective-permute-start | bytes 776 | tf_op jit(solution)/shard_map/ppermute | solution.py:36
  27.2 71.7 %collective-permute-start.8 = (bf16[32,9216]{1,0:T(8,128)(2,1)}, bf16[32,9216]{1,0:T(8,128)(2,1)S(1)}, u32[]{:S(2)}, u32[]{:S(2)}) collective-permute-start(bf16[32,9216]{1,0:T(8,128)(2,1)} %get-tuple-element.42), channel_id=1, source_target_pairs={{0,1},{1,0},{2,3},{3,2},{4,5},{5,4},{6,7},{7,6},{8,9},{9,8},{10,11... | collective-permute-start | bytes 1769480 | tf_op jit(solution)/shard_map/ppermute | solution.py:36
  28.8 70.1 %collective-permute-start.9 = (bf16[32,9216]{1,0:T(8,128)(2,1)}, bf16[32,9216]{1,0:T(8,128)(2,1)}, u32[]{:S(2)}, u32[]{:S(2)}) collective-permute-start(bf16[32,9216]{1,0:T(8,128)(2,1)} %get-tuple-element.43), channel_id=1, source_target_pairs={{0,3},{1,2},{2,1},{3,0},{4,7},{5,6},{6,5},{7,4},{8,11},{9,10},{10,... | collective-permute-start | bytes 1769480 | tf_op jit(solution)/shard_map/ppermute | solution.py:36
  29.5 37.1 %copy-start.1 = (bf16[32,9216]{1,0:T(8,128)(2,1)}, bf16[32,9216]{1,0:T(8,128)(2,1)S(1)}, u32[]{:S(2)}) copy-start(bf16[32,9216]{1,0:T(8,128)(2,1)S(1)} %collective-permute-done.4.refs_3_.refs_5_) | copy-start | bytes 1769476
  29.5 74.5 %collective-permute-start.10 = (bf16[32,9216]{1,0:T(8,128)(2,1)}, bf16[32,9216]{1,0:T(8,128)(2,1)S(1)}, u32[]{:S(2)}, u32[]{:S(2)}) collective-permute-start(bf16[32,9216]{1,0:T(8,128)(2,1)} %get-tuple-element.44), channel_id=1, source_target_pairs={{0,5},{1,4},{2,7},{3,6},{4,1},{5,0},{6,3},{7,2},{8,13},{9,12},{10,... | collective-permute-start | bytes 1769480 | tf_op jit(solution)/shard_map/ppermute | solution.py:36
  45.1 21.5 %copy-start.2 = (bf16[32,9216]{1,0:T(8,128)(2,1)}, bf16[32,9216]{1,0:T(8,128)(2,1)S(1)}, u32[]{:S(2)}) copy-start(bf16[32,9216]{1,0:T(8,128)(2,1)S(1)} %collective-permute-done.2.refs_1_.refs_3_) | copy-start | bytes 1769476
  45.1 58.9 %collective-permute-start.11 = (bf16[32,9216]{1,0:T(8,128)(2,1)}, bf16[32,9216]{1,0:T(8,128)(2,1)}, u32[]{:S(2)}, u32[]{:S(2)}) collective-permute-start(bf16[32,9216]{1,0:T(8,128)(2,1)} %get-tuple-element.45), channel_id=1, source_target_pairs={{0,7},{1,6},{2,5},{3,4},{4,3},{5,2},{6,1},{7,0},{8,15},{9,14},{10,... | collective-permute-start | bytes 1769480 | tf_op jit(solution)/shard_map/ppermute | solution.py:36
  66.6 0.8 copy-start.3
  77.3 1.7 collective-permute-start.5
  80.0 8.4 %collective-permute-start.6 = (f32[2,256,128]{2,1,0:T(8,128)S(1)}, f32[2,256,128]{2,1,0:T(8,128)S(1)}, u32[]{:S(2)}, u32[]{:S(2)}) collective-permute-start(f32[2,256,128]{2,1,0:T(8,128)S(1)} %add.25), channel_id=1, source_target_pairs={{0,16},{8,24},{16,0},{24,8},{1,17},{9,25},{17,1},{25,9},{2,18},{10... | collective-permute-start | bytes 786440 | tf_op jit(solution)/shard_map/ppermute | solution.py:36
  98.9 32.0 %copy-start.14 = (s32[2,2]{1,0:T(2,128)S(1)}, s32[2,2]{1,0:T(2,128)}, u32[]{:S(2)}) copy-start(s32[2,2]{1,0:T(2,128)} %get-tuple-element.50) | copy-start | bytes 52
  98.9 32.0 %copy-start.15 = (s32[1,2]{1,0:T(1,128)S(1)}, s32[1,2]{1,0:T(1,128)}, u32[]{:S(2)}) copy-start(s32[1,2]{1,0:T(1,128)} %get-tuple-element.51) | copy-start | bytes 28
  98.9 32.0 %copy-start.16 = (s32[1,2]{1,0:T(1,128)S(1)}, s32[1,2]{1,0:T(1,128)}, u32[]{:S(2)}) copy-start(s32[1,2]{1,0:T(1,128)} %get-tuple-element.49) | copy-start | bytes 28
  98.9 5.1 %copy-start.4 = (bf16[32,9216]{1,0:T(8,128)(2,1)}, bf16[32,9216]{1,0:T(8,128)(2,1)S(1)}, u32[]{:S(2)}) copy-start(bf16[32,9216]{1,0:T(8,128)(2,1)S(1)} %collective-permute-done.8.refs_0_.refs_6_) | copy-start | bytes 1769476
  104.0 0.8 copy-start.5
  114.7 67.6 %copy-start.12 = (s32[4,2]{1,0:T(4,128)S(1)}, s32[4,2]{1,0:T(4,128)}, u32[]{:S(2)}) copy-start(s32[4,2]{1,0:T(4,128)} %get-tuple-element.47) | copy-start | bytes 100
  114.7 68.8 %copy-start.9 = (f32[2,256,128]{2,1,0:T(8,128)S(1)}, f32[2,256,128]{2,1,0:T(8,128)}, u32[]{:S(2)}) copy-start(f32[2,256,128]{2,1,0:T(8,128)} %add.26.sums_ref) | copy-start | bytes 786436
  114.7 13.5 %collective-permute-start.12 = (f32[2,256,128]{2,1,0:T(8,128)}, f32[2,256,128]{2,1,0:T(8,128)S(1)}, u32[]{:S(2)}, u32[]{:S(2)}) collective-permute-start(f32[2,256,128]{2,1,0:T(8,128)} %shard_map.108), channel_id=1, source_target_pairs={{0,8},{8,0},{16,24},{24,16},{1,9},{9,1},{17,25},{25,17},{2,10},{10... | collective-permute-start | bytes 786440 | tf_op jit(solution)/shard_map/ppermute | solution.py:36
  114.8 38.6 %collective-permute-start.18 = (bf16[32,9216]{1,0:T(8,128)(2,1)}, bf16[32,9216]{1,0:T(8,128)(2,1)S(1)}, u32[]{:S(2)}, u32[]{:S(2)}) collective-permute-start(bf16[32,9216]{1,0:T(8,128)(2,1)} %get-tuple-element.56), channel_id=1, source_target_pairs={{0,2},{1,3},{2,0},{3,1},{4,6},{5,7},{6,4},{7,5},{8,10},{9,11},{10,... | collective-permute-start | bytes 1769480 | tf_op jit(solution)/shard_map/ppermute | solution.py:36
  127.0 55.3 %collective-permute-start.19 = (bf16[32,9216]{1,0:T(8,128)(2,1)}, bf16[32,9216]{1,0:T(8,128)(2,1)S(1)}, u32[]{:S(2)}, u32[]{:S(2)}) collective-permute-start(bf16[32,9216]{1,0:T(8,128)(2,1)} %get-tuple-element.57), channel_id=1, source_target_pairs={{0,4},{1,5},{2,6},{3,7},{4,0},{5,1},{6,2},{7,3},{8,12},{9,13},{10,... | collective-permute-start | bytes 1769480 | tf_op jit(solution)/shard_map/ppermute | solution.py:36
  129.2 8.4 %collective-permute-start.13 = (f32[2,256,128]{2,1,0:T(8,128)S(1)}, f32[2,256,128]{2,1,0:T(8,128)S(1)}, u32[]{:S(2)}, u32[]{:S(2)}) collective-permute-start(f32[2,256,128]{2,1,0:T(8,128)S(1)} %add.27), channel_id=1, source_target_pairs={{0,16},{8,24},{16,0},{24,8},{1,17},{9,25},{17,1},{25,9},{2,18},{10... | collective-permute-start | bytes 786440 | tf_op jit(solution)/shard_map/ppermute | solution.py:36
  131.5 62.7 %collective-permute-start.20 = (bf16[32,9216]{1,0:T(8,128)(2,1)}, bf16[32,9216]{1,0:T(8,128)(2,1)S(1)}, u32[]{:S(2)}, u32[]{:S(2)}) collective-permute-start(bf16[32,9216]{1,0:T(8,128)(2,1)} %get-tuple-element.58), channel_id=1, source_target_pairs={{0,6},{1,7},{2,4},{3,5},{4,2},{5,3},{6,0},{7,1},{8,14},{9,15},{10,... | collective-permute-start | bytes 1769480 | tf_op jit(solution)/shard_map/ppermute | solution.py:36
  138.3 45.3 %copy-start.10 = (f32[2,256,128]{2,1,0:T(8,128)S(1)}, f32[2,256,128]{2,1,0:T(8,128)}, u32[]{:S(2)}) copy-start(f32[2,256,128]{2,1,0:T(8,128)} %add.28.sums_ref) | copy-start | bytes 786436
  148.1 88.9 %collective-permute-start.14 = (bf16[32,9216]{1,0:T(8,128)(2,1)}, bf16[32,9216]{1,0:T(8,128)(2,1)S(1)}, u32[]{:S(2)}, u32[]{:S(2)}) collective-permute-start(bf16[32,9216]{1,0:T(8,128)(2,1)} %get-tuple-element.48), channel_id=1, source_target_pairs={{0,7},{1,6},{2,5},{3,4},{4,3},{5,2},{6,1},{7,0},{8,15},{9,14},{10,... | collective-permute-start | bytes 1769480 | tf_op jit(solution)/shard_map/ppermute | solution.py:36
  149.6 53.5 %collective-permute-start.15 = (bf16[32,9216]{1,0:T(8,128)(2,1)}, bf16[32,9216]{1,0:T(8,128)(2,1)S(1)}, u32[]{:S(2)}, u32[]{:S(2)}) collective-permute-start(bf16[32,9216]{1,0:T(8,128)(2,1)} %get-tuple-element.52), channel_id=1, source_target_pairs={{0,1},{1,0},{2,3},{3,2},{4,5},{5,4},{6,7},{7,6},{8,9},{9,8},{10,11... | collective-permute-start | bytes 1769480 | tf_op jit(solution)/shard_map/ppermute | solution.py:36
  153.4 40.8 %copy-start.6 = (bf16[32,9216]{1,0:T(8,128)(2,1)}, bf16[32,9216]{1,0:T(8,128)(2,1)S(1)}, u32[]{:S(2)}) copy-start(bf16[32,9216]{1,0:T(8,128)(2,1)S(1)} %collective-permute-done.18.refs_1_.refs_4_) | copy-start | bytes 1769476
  153.4 49.8 %collective-permute-start.16 = (bf16[32,9216]{1,0:T(8,128)(2,1)}, bf16[32,9216]{1,0:T(8,128)(2,1)}, u32[]{:S(2)}, u32[]{:S(2)}) collective-permute-start(bf16[32,9216]{1,0:T(8,128)(2,1)} %get-tuple-element.53), channel_id=1, source_target_pairs={{0,3},{1,2},{2,1},{3,0},{4,7},{5,6},{6,5},{7,4},{8,11},{9,10},{10,... | collective-permute-start | bytes 1769480 | tf_op jit(solution)/shard_map/ppermute | solution.py:36
  182.3 11.9 %copy-start.7 = (bf16[32,9216]{1,0:T(8,128)(2,1)}, bf16[32,9216]{1,0:T(8,128)(2,1)S(1)}, u32[]{:S(2)}) copy-start(bf16[32,9216]{1,0:T(8,128)(2,1)S(1)} %collective-permute-done.19.refs_2_.refs_5_) | copy-start | bytes 1769476
  182.3 49.8 %collective-permute-start.17 = (bf16[32,9216]{1,0:T(8,128)(2,1)}, bf16[32,9216]{1,0:T(8,128)(2,1)}, u32[]{:S(2)}, u32[]{:S(2)}) collective-permute-start(bf16[32,9216]{1,0:T(8,128)(2,1)} %get-tuple-element.54), channel_id=1, source_target_pairs={{0,5},{1,4},{2,7},{3,6},{4,1},{5,0},{6,3},{7,2},{8,13},{9,12},{10,... | collective-permute-start | bytes 1769480 | tf_op jit(solution)/shard_map/ppermute | solution.py:36
  194.2 0.8 copy-start.8
  203.2 29.0 %copy-start.11 = (bf16[32,9216]{1,0:T(8,128)(2,1)}, bf16[32,9216]{1,0:T(8,128)(2,1)S(1)}, u32[]{:S(2)}) copy-start(bf16[32,9216]{1,0:T(8,128)(2,1)S(1)} %collective-permute-done.15.refs_0_) | copy-start | bytes 1769476

commit v4 on v3

--- a/solution.py
+++ b/solution.py
@@ -36,14 +36,14 @@
     return lax.ppermute(x, axis, [(i, i ^ offset) for i in range(count)])
 
 
-def pick_kernel(groups, me_ref, ids_ref, fin, fout, table_ref, *refs):
+def pick_kernel(groups, ids_ref, fin, fout, table_ref, *refs):
     outs = refs[:groups]
     in_sem, ids, ids_sem = refs[groups:]
     fetch = pltpu.make_async_copy(ids_ref, ids, ids_sem)
     fetch.start()
     fetch.wait()
     exp_count, rank, wide = fin.shape
-    base = me_ref[0] * exp_count
+    base = lax.axis_index("adapter") * exp_count
     loads = []
     for m in range(groups):
         found = jnp.int32(0)
@@ -300,7 +300,6 @@
     full = wide + narrow
     tile = math.gcd(wide, narrow)
     in_tiles, tiles = wide // tile, full // tile
-    me_arr = me.astype(jnp.int32).reshape(1)
     both = CAP * rank
     piece = jax.ShapeDtypeStruct((both, full), BF)
 
@@ -310,14 +309,14 @@
             functools.partial(pick_kernel, count),
             out_shape=[jax.ShapeDtypeStruct((count, CAP), jnp.int32)]
             + [pltpu.VMEM((both, full), BF) if fast else piece] * count,
-            in_specs=[SMEM, VMEM, HBM, HBM],
+            in_specs=[VMEM, HBM, HBM],
             out_specs=[SMEM] + [VMEM] * count,
             scratch_shapes=[
                 pltpu.SemaphoreType.DMA((count, CAP, 2)),
                 pltpu.SMEM(lists.shape, jnp.int32),
                 pltpu.SemaphoreType.DMA,
             ],
-        )(me_arr, pltpu.with_memory_space_constraint(lists, pltpu.VMEM), factor_in, factor_out)
+        )(pltpu.with_memory_space_constraint(lists, pltpu.VMEM), factor_in, factor_out)
 
     steps, chunks, homes = plan(groups)
     lists, known = adapter_ids[None], [0]

time: 240 us -> 240 us (level)
  no operation moved by 1% of the time
where the time goes in v4:
time: 240 us; the launch traced here: 239 us
  waiting for transfers between devices  97.7 us (41%)
  Pallas kernels  75.1 us (31%)
  starting transfers between devices  51.6 us (22%)
  other arithmetic  6.78 us (3%)
  local copies, waits for them, and re-layouts  6.54 us (3%)
    ppermute x21, waiting for transfers between devices, swap(): return lax.ppermute(x, axis, [(i, i ^ offset) for i in range(count)])  97.7 us
    ppermute x21, starting transfers between devices, swap(): return lax.ppermute(x, axis, [(i, i ^ offset) for i in range(count)])  51.6 us
    pallas_call x2, Pallas kernels, body(): pl.pallas_call(functools.partial(project_kernel, count, in_tiles, tiles),...  19.7 us
    pallas_call x2, Pallas kernels, body(): pl.pallas_call(functools.partial(term_kernel, count, in_tiles), out_shape...  19.5 us
    pallas_call x4, Pallas kernels, pick(): pl.pallas_call(functools.partial(pick_kernel, count), out_shape=[jax.Shap...  11.8 us
    pallas_call x1, Pallas kernels, body(): pl.pallas_call(functools.partial(input_kernel, len(chunks), groups), out_...  9.47 us
    pallas_call x1, Pallas kernels, body(): pl.pallas_call(functools.partial(collect_kernel, early), out_shape=[jax.S...  8.09 us
    pallas_call x1, Pallas kernels, body(): pl.pallas_call(functools.partial(finish_kernel, late, early, ends), out_s...  4.89 us
  transfers between devices with their start and end apart: 21, of which 9 were waited for; matrix products, arithmetic and copies ran while one was open for 4% of the time, Pallas kernels for 27%

profile of v4, /device:TPU:0, one launch (start us, length us, event | category | flops | bytes accessed | tf_op | source)
XLA Modules:
  0.0 238.8 jit_solution(10223752768990928758)
XLA Ops:
  0.6 5.1 %collective-permute-start = (s32[1,2,8]{2,1,0:T(2,128)}, s32[1,2,8]{2,1,0:T(2,128)S(1)}, u32[]{:S(2)}, u32[]{:S(2)}) collective-permute-start(s32[1,2,8]{2,1,0:T(2,128)} %bitcast.17), channel_id=1, source_target_pairs={{0,6},{1,7},{2,4},{3,5},{4,2},{5,3},{6,0},{7,1},{8,14},{9,15},{10,... | collective-permute-start | bytes 200 | tf_op jit(solution)/shard_map/ppermute | solution.py:36
  5.8 0.8 reshape.169
  6.6 0.7 broadcast_xor_fusion
  7.5 0.7 pad_add_fusion.1
  8.2 2.3 shard_map.104
  10.5 3.9 %collective-permute-start.4 = (bf16[32,9216]{1,0:T(8,128)(2,1)S(1)}, bf16[32,9216]{1,0:T(8,128)(2,1)S(1)}, u32[]{:S(2)}, u32[]{:S(2)}) collective-permute-start(bf16[32,9216]{1,0:T(8,128)(2,1)S(1)} %get-tuple-element.38), channel_id=1, source_target_pairs={{0,6},{1,7},{2,4},{3,5},{4,2},{5,3},{6,0},{7,1},{8,14},{9,15},{10,... | collective-permute-start | bytes 1769480 | tf_op jit(solution)/shard_map/ppermute | solution.py:36
  14.4 3.1 %shard_map.103 = (s32[2,2]{1,0:T(2,128)}, bf16[32,9216]{1,0:T(8,128)(2,1)}, bf16[32,9216]{1,0:T(8,128)(2,1)}) custom-call(s32[2,2,8]{2,1,0:T(2,128)S(1)} %collective-permute-done.1.ids_ref, bf16[32,16,7168]{2,1,0:T(8,128)(2,1)} %fin.7, bf16[32,16,2048]{2,1,0:T(8,128)(2,1)} %fout.7), custom_call_target="tpu_custom_call" | custom-call | tf_op jit(solution)/shard_map/pallas_call | solution.py:308
  17.5 1.2 collective-permute-start.2
  18.6 0.7 collective-permute-start.3
  19.6 1.6 collective-permute-start.7
  21.4 1.9 collective-permute-done.7.ids_ref
  23.2 4.0 %shard_map.107 = (s32[4,2]{1,0:T(4,128)}, bf16[32,9216]{1,0:T(8,128)(2,1)}, bf16[32,9216]{1,0:T(8,128)(2,1)}, bf16[32,9216]{1,0:T(8,128)(2,1)}, bf16[32,9216]{1,0:T(8,128)(2,1)}) custom-call(s32[4,2,8]{2,1,0:T(2,128)S(1)} %collective-permute-done.7.ids_ref, bf16[32,16,7168]{2,1,0:T(8,128)(2,1)} %fin.7, bf16[32,16,2048]{2,1,0:T(8,128)(2,1)} %fout.7), custom_call_target="tpu_custom_call" | custom-call | tf_op jit(solution)/shard_map/pallas_call | solution.py:308
  27.2 1.6 collective-permute-start.8
  28.8 0.8 collective-permute-start.9
  29.6 15.6 %collective-permute-start.10 = (bf16[32,9216]{1,0:T(8,128)(2,1)}, bf16[32,9216]{1,0:T(8,128)(2,1)S(1)}, u32[]{:S(2)}, u32[]{:S(2)}) collective-permute-start(bf16[32,9216]{1,0:T(8,128)(2,1)} %get-tuple-element.44), channel_id=1, source_target_pairs={{0,5},{1,4},{2,7},{3,6},{4,1},{5,0},{6,3},{7,2},{8,13},{9,12},{10,... | collective-permute-start | bytes 1769480 | tf_op jit(solution)/shard_map/ppermute | solution.py:36
  45.7 2.6 %shard_map.102 = (s32[1,2]{1,0:T(1,128)}, bf16[32,9216]{1,0:T(8,128)(2,1)}) custom-call(s32[1,2,8]{2,1,0:T(2,128)S(1)} %bitcast.20, bf16[32,16,7168]{2,1,0:T(8,128)(2,1)} %fin.7, bf16[32,16,2048]{2,1,0:T(8,128)(2,1)} %fout.7), custom_call_target="tpu_custom_call" | custom-call | tf_op jit(solution)/shard_map/pallas_call | solution.py:308
  48.3 18.3 %collective-permute-done.3.refs_2_.refs_4_ = bf16[32,9216]{1,0:T(8,128)(2,1)S(1)} collective-permute-done((bf16[32,9216]{1,0:T(8,128)(2,1)}, bf16[32,9216]{1,0:T(8,128)(2,1)S(1)}, u32[]{:S(2)}, u32[]{:S(2)}) %collective-permute-start.3) | collective-permute-done | bytes 589856 | tf_op jit(solution)/shard_map/ppermute | solution.py:36
  66.6 0.8 copy-done.3
  67.4 9.9 %shard_map.105 = f32[2,256,128]{2,1,0:T(8,128)} custom-call(f32[2,128]{1,0:T(2,128)} %get-tuple-element.74.mask_ref, bf16[512,7168]{1,0:T(8,128)(2,1)} %x_ref.7, bf16[512,2048]{1,0:T(8,128)(2,1)} %g_ref.7, bf16[32,9216]{1,0:T(8,128)(2,1)} %get-tuple-element.35.refs_0_.refs_2_, bf16[32,9216]{1,0:T(8,128)(2,1)} %copy-done.2, bf16[32,9216]{1,0:T(8,128)(2,1)} %copy-done.3, ...), custom_call_target="tpu_custom_call" | custom-call | tf_op jit(solution)/shard_map/pallas_call | solution.py:368
  77.3 1.7 collective-permute-done.5
  79.0 1.0 add.25
  80.0 1.8 collective-permute-start.6
  82.6 5.8 %collective-permute-done.6 = f32[2,256,128]{2,1,0:T(8,128)S(1)} collective-permute-done((f32[2,256,128]{2,1,0:T(8,128)S(1)}, f32[2,256,128]{2,1,0:T(8,128)S(1)}, u32[]{:S(2)}, u32[]{:S(2)}) %collective-permute-start.6) | collective-permute-done | bytes 262176 | tf_op jit(solution)/shard_map/ppermute | solution.py:36
  88.4 0.7 add.26.sums_ref
  89.2 9.7 %shard_map.106 = (bf16[32,9216]{1,0:T(8,128)(2,1)}, bf16[32,9216]{1,0:T(8,128)(2,1)}, bf16[32,9216]{1,0:T(8,128)(2,1)}, bf16[32,9216]{1,0:T(8,128)(2,1)}, bf16[512,128]{1,0:T(8,128)(2,1)}) custom-call(f32[2,256,128]{2,1,0:T(8,128)} %add.26.sums_ref, f32[2,128]{1,0:T(2,128)} %get-tuple-element.73.weight_ref, bf16[512,7168]{1,0:T(8,128)(2,1)} %x_ref.7, ...), custom_call_target="tpu_custom_call" | custom-call | tf_op jit(solution)/shard_map/pallas_call | solution.py:380
  98.9 5.1 %collective-permute-done.10.refs_2_.refs_8_ = bf16[32,9216]{1,0:T(8,128)(2,1)S(1)} collective-permute-done((bf16[32,9216]{1,0:T(8,128)(2,1)}, bf16[32,9216]{1,0:T(8,128)(2,1)S(1)}, u32[]{:S(2)}, u32[]{:S(2)}) %collective-permute-start.10) | collective-permute-done | bytes 589856 | tf_op jit(solution)/shard_map/ppermute | solution.py:36
  104.0 0.8 copy-done.5
  104.9 9.9 %shard_map.108 = f32[2,256,128]{2,1,0:T(8,128)} custom-call(f32[2,128]{1,0:T(2,128)} %get-tuple-element.41.mask_ref, bf16[512,7168]{1,0:T(8,128)(2,1)} %x_ref.7, bf16[512,2048]{1,0:T(8,128)(2,1)} %g_ref.7, bf16[32,9216]{1,0:T(8,128)(2,1)} %copy-done.4, bf16[32,9216]{1,0:T(8,128)(2,1)} %collective-permute-done.9.refs_1_.refs_7_, bf16[32,9216]{1,0:T(8,128)(2,1)} %copy-done.5, ...), custom_call_target="tpu_custom_call" | custom-call | tf_op jit(solution)/shard_map/pallas_call | solution.py:368
  114.8 12.2 %collective-permute-start.18 = (bf16[32,9216]{1,0:T(8,128)(2,1)}, bf16[32,9216]{1,0:T(8,128)(2,1)S(1)}, u32[]{:S(2)}, u32[]{:S(2)}) collective-permute-start(bf16[32,9216]{1,0:T(8,128)(2,1)} %get-tuple-element.56), channel_id=1, source_target_pairs={{0,2},{1,3},{2,0},{3,1},{4,6},{5,7},{6,4},{7,5},{8,10},{9,11},{10,... | collective-permute-start | bytes 1769480 | tf_op jit(solution)/shard_map/ppermute | solution.py:36
  127.0 1.3 collective-permute-start.19
  128.2 1.0 add.27
  129.2 1.6 collective-permute-start.13
  130.8 0.7 pad_add_fusion.3.table_ref.early_ref
  131.5 1.4 collective-permute-start.20
  132.9 4.7 %collective-permute-done.13 = f32[2,256,128]{2,1,0:T(8,128)S(1)} collective-permute-done((f32[2,256,128]{2,1,0:T(8,128)S(1)}, f32[2,256,128]{2,1,0:T(8,128)S(1)}, u32[]{:S(2)}, u32[]{:S(2)}) %collective-permute-start.13) | collective-permute-done | bytes 262176 | tf_op jit(solution)/shard_map/ppermute | solution.py:36
  137.6 0.7 add.28.sums_ref
  138.3 9.8 %shard_map.109 = (bf16[32,9216]{1,0:T(8,128)(2,1)}, bf16[32,9216]{1,0:T(8,128)(2,1)}, bf16[32,9216]{1,0:T(8,128)(2,1)}, bf16[32,9216]{1,0:T(8,128)(2,1)}, bf16[512,128]{1,0:T(8,128)(2,1)}) custom-call(f32[2,256,128]{2,1,0:T(8,128)} %add.28.sums_ref, f32[2,128]{1,0:T(2,128)} %get-tuple-element.72.weight_ref, bf16[512,7168]{1,0:T(8,128)(2,1)} %x_ref.7, ...), custom_call_target="tpu_custom_call" | custom-call | tf_op jit(solution)/shard_map/pallas_call | solution.py:380
  148.1 1.5 collective-permute-start.14
  149.6 1.5 collective-permute-start.15
  151.1 2.3 collective-permute-done.18.refs_1_.refs_4_
  153.4 28.9 %collective-permute-done.19.refs_2_.refs_5_ = bf16[32,9216]{1,0:T(8,128)(2,1)S(1)} collective-permute-done((bf16[32,9216]{1,0:T(8,128)(2,1)}, bf16[32,9216]{1,0:T(8,128)(2,1)S(1)}, u32[]{:S(2)}, u32[]{:S(2)}) %collective-permute-start.19) | collective-permute-done | bytes 589856 | tf_op jit(solution)/shard_map/ppermute | solution.py:36
  184.1 0.7 reduce_sum.72
  184.8 9.5 %input.1 = f32[512,7168]{1,0:T(8,128)} custom-call(bf16[512,128]{1,0:T(8,128)(2,1)} %get-tuple-element.40.refs_0_, bf16[512,128]{1,0:T(8,128)(2,1)} %get-tuple-element.46.refs_1_, bf16[32,9216]{1,0:T(8,128)(2,1)} %get-tuple-element.35.refs_0_.refs_2_, bf16[32,9216]{1,0:T(8,128)(2,1)} %copy-done.2, bf16[32,9216]{1,0:T(8,128)(2,1)} %copy-done.3, ...), custom_call_target="tpu_custom_call" | custom-call | tf_op jit(solution)/shard_map/input/pallas_call | solution.py:395
  194.3 0.8 copy-done.8
  195.1 8.1 %collect.1 = (bf16[32,16,7168]{2,1,0:T(8,128)(2,1)}, bf16[32,16,2048]{2,1,0:T(8,128)(2,1)}) custom-call(s32[8]{0:T(128)} %pad_add_fusion.3.table_ref.early_ref, bf16[32,9216]{1,0:T(8,128)(2,1)} %get-tuple-element.55.refs_0_.refs_3_, bf16[32,9216]{1,0:T(8,128)(2,1)} %copy-done.6, bf16[32,9216]{1,0:T(8,128)(2,1)} %copy-done.7, bf16[32,9216]{1,0:T(8,128)(2,1)} %copy-done.8), custom_call_target="tpu_custom_call" | custom-call | tf_op jit(solution)/shard_map/collect/pallas_call | solution.py:416
  203.2 28.9 %collective-permute-done.17.refs_2_ = bf16[32,9216]{1,0:T(8,128)(2,1)} collective-permute-done((bf16[32,9216]{1,0:T(8,128)(2,1)}, bf16[32,9216]{1,0:T(8,128)(2,1)}, u32[]{:S(2)}, u32[]{:S(2)}) %collective-permute-start.17) | collective-permute-done | bytes 589856 | tf_op jit(solution)/shard_map/ppermute | solution.py:36
  232.1 4.9 %finish1.1 = (bf16[32,16,7168]{2,1,0:T(8,128)(2,1)}, bf16[32,16,2048]{2,1,0:T(8,128)(2,1)}, f32[2,16,9216]{2,1,0:T(8,128)S(1)}) custom-call(s32[6]{0:T(128)} %pad_add_fusion.2.late_ref, s32[8]{0:T(128)} %pad_add_fusion.3.table_ref.early_ref, s32[2]{0:T(128)} %get-tuple-element.71.end_ref, ...), custom_call_target="tpu_custom_call", output_to_operand_aliasing={{0}: (10, {}), {1}: (11, {})} | custom-call | tf_op jit(solution)/shard_map/finish1/pallas_call | solution.py:433
  237.0 1.6 finish2.1
  (75 shorter events, 4.1 us)
Async XLA Ops:
  0.6 6.9 %collective-permute-start = (s32[1,2,8]{2,1,0:T(2,128)}, s32[1,2,8]{2,1,0:T(2,128)S(1)}, u32[]{:S(2)}, u32[]{:S(2)}) collective-permute-start(s32[1,2,8]{2,1,0:T(2,128)} %bitcast.17), channel_id=1, source_target_pairs={{0,6},{1,7},{2,4},{3,5},{4,2},{5,3},{6,0},{7,1},{8,14},{9,15},{10,... | collective-permute-start | bytes 200 | tf_op jit(solution)/shard_map/ppermute | solution.py:36
  8.2 11.2 %copy-start.13 = (f32[2,8]{1,0:T(2,128)S(1)}, f32[2,8]{1,0:T(2,128)}, u32[]{:S(2)}) copy-start(f32[2,8]{1,0:T(2,128)} %param.12) | copy-start | bytes 196
  8.2 11.3 %copy-start = (s32[2,8]{1,0:T(2,128)S(1)}, s32[2,8]{1,0:T(2,128)}, u32[]{:S(2)}) copy-start(s32[2,8]{1,0:T(2,128)} %param.11) | copy-start | bytes 196
  8.2 6.2 %collective-permute-start.1 = (s32[2,2,8]{2,1,0:T(2,128)S(1)}, s32[2,2,8]{2,1,0:T(2,128)S(1)}, u32[]{:S(2)}, u32[]{:S(2)}) collective-permute-start(s32[2,2,8]{2,1,0:T(2,128)S(1)} %pad_add_fusion.1), channel_id=1, source_target_pairs={{0,2},{1,3},{2,0},{3,1},{4,6},{5,7},{6,4},{7,5},{8,10},{9,11},{10,... | collective-permute-start | bytes 392 | tf_op jit(solution)/shard_map/ppermute | solution.py:36
  10.5 19.0 %collective-permute-start.4 = (bf16[32,9216]{1,0:T(8,128)(2,1)S(1)}, bf16[32,9216]{1,0:T(8,128)(2,1)S(1)}, u32[]{:S(2)}, u32[]{:S(2)}) collective-permute-start(bf16[32,9216]{1,0:T(8,128)(2,1)S(1)} %get-tuple-element.38), channel_id=1, source_target_pairs={{0,6},{1,7},{2,4},{3,5},{4,2},{5,3},{6,0},{7,1},{8,14},{9,15},{10,... | collective-permute-start | bytes 1769480 | tf_op jit(solution)/shard_map/ppermute | solution.py:36
  17.5 27.7 %collective-permute-start.2 = (bf16[32,9216]{1,0:T(8,128)(2,1)}, bf16[32,9216]{1,0:T(8,128)(2,1)S(1)}, u32[]{:S(2)}, u32[]{:S(2)}) collective-permute-start(bf16[32,9216]{1,0:T(8,128)(2,1)} %get-tuple-element.36), channel_id=1, source_target_pairs={{0,2},{1,3},{2,0},{3,1},{4,6},{5,7},{6,4},{7,5},{8,10},{9,11},{10,... | collective-permute-start | bytes 1769480 | tf_op jit(solution)/shard_map/ppermute | solution.py:36
  18.6 47.9 %collective-permute-start.3 = (bf16[32,9216]{1,0:T(8,128)(2,1)}, bf16[32,9216]{1,0:T(8,128)(2,1)S(1)}, u32[]{:S(2)}, u32[]{:S(2)}) collective-permute-start(bf16[32,9216]{1,0:T(8,128)(2,1)} %get-tuple-element.37), channel_id=1, source_target_pairs={{0,4},{1,5},{2,6},{3,7},{4,0},{5,1},{6,2},{7,3},{8,12},{9,13},{10,... | collective-permute-start | bytes 1769480 | tf_op jit(solution)/shard_map/ppermute | solution.py:36
  19.6 3.7 %collective-permute-start.7 = (s32[4,2,8]{2,1,0:T(2,128)S(1)}, s32[4,2,8]{2,1,0:T(2,128)S(1)}, u32[]{:S(2)}, u32[]{:S(2)}) collective-permute-start(s32[4,2,8]{2,1,0:T(2,128)S(1)} %pad_add_fusion), channel_id=1, source_target_pairs={{0,1},{1,0},{2,3},{3,2},{4,5},{5,4},{6,7},{7,6},{8,9},{9,8},{10,11... | collective-permute-start | bytes 776 | tf_op jit(solution)/shard_map/ppermute | solution.py:36
  27.2 71.7 %collective-permute-start.8 = (bf16[32,9216]{1,0:T(8,128)(2,1)}, bf16[32,9216]{1,0:T(8,128)(2,1)S(1)}, u32[]{:S(2)}, u32[]{:S(2)}) collective-permute-start(bf16[32,9216]{1,0:T(8,128)(2,1)} %get-tuple-element.42), channel_id=1, source_target_pairs={{0,1},{1,0},{2,3},{3,2},{4,5},{5,4},{6,7},{7,6},{8,9},{9,8},{10,11... | collective-permute-start | bytes 1769480 | tf_op jit(solution)/shard_map/ppermute | solution.py:36
  28.8 70.1 %collective-permute-start.9 = (bf16[32,9216]{1,0:T(8,128)(2,1)}, bf16[32,9216]{1,0:T(8,128)(2,1)}, u32[]{:S(2)}, u32[]{:S(2)}) collective-permute-start(bf16[32,9216]{1,0:T(8,128)(2,1)} %get-tuple-element.43), channel_id=1, source_target_pairs={{0,3},{1,2},{2,1},{3,0},{4,7},{5,6},{6,5},{7,4},{8,11},{9,10},{10,... | collective-permute-start | bytes 1769480 | tf_op jit(solution)/shard_map/ppermute | solution.py:36
  29.6 37.1 %copy-start.1 = (bf16[32,9216]{1,0:T(8,128)(2,1)}, bf16[32,9216]{1,0:T(8,128)(2,1)S(1)}, u32[]{:S(2)}) copy-start(bf16[32,9216]{1,0:T(8,128)(2,1)S(1)} %collective-permute-done.4.refs_3_.refs_5_) | copy-start | bytes 1769476
  29.6 74.5 %collective-permute-start.10 = (bf16[32,9216]{1,0:T(8,128)(2,1)}, bf16[32,9216]{1,0:T(8,128)(2,1)S(1)}, u32[]{:S(2)}, u32[]{:S(2)}) collective-permute-start(bf16[32,9216]{1,0:T(8,128)(2,1)} %get-tuple-element.44), channel_id=1, source_target_pairs={{0,5},{1,4},{2,7},{3,6},{4,1},{5,0},{6,3},{7,2},{8,13},{9,12},{10,... | collective-permute-start | bytes 1769480 | tf_op jit(solution)/shard_map/ppermute | solution.py:36
  45.1 21.5 %copy-start.2 = (bf16[32,9216]{1,0:T(8,128)(2,1)}, bf16[32,9216]{1,0:T(8,128)(2,1)S(1)}, u32[]{:S(2)}) copy-start(bf16[32,9216]{1,0:T(8,128)(2,1)S(1)} %collective-permute-done.2.refs_1_.refs_3_) | copy-start | bytes 1769476
  45.1 58.9 %collective-permute-start.11 = (bf16[32,9216]{1,0:T(8,128)(2,1)}, bf16[32,9216]{1,0:T(8,128)(2,1)}, u32[]{:S(2)}, u32[]{:S(2)}) collective-permute-start(bf16[32,9216]{1,0:T(8,128)(2,1)} %get-tuple-element.45), channel_id=1, source_target_pairs={{0,7},{1,6},{2,5},{3,4},{4,3},{5,2},{6,1},{7,0},{8,15},{9,14},{10,... | collective-permute-start | bytes 1769480 | tf_op jit(solution)/shard_map/ppermute | solution.py:36
  66.6 0.8 copy-start.3
  77.3 1.7 collective-permute-start.5
  80.0 8.4 %collective-permute-start.6 = (f32[2,256,128]{2,1,0:T(8,128)S(1)}, f32[2,256,128]{2,1,0:T(8,128)S(1)}, u32[]{:S(2)}, u32[]{:S(2)}) collective-permute-start(f32[2,256,128]{2,1,0:T(8,128)S(1)} %add.25), channel_id=1, source_target_pairs={{0,16},{8,24},{16,0},{24,8},{1,17},{9,25},{17,1},{25,9},{2,18},{10... | collective-permute-start | bytes 786440 | tf_op jit(solution)/shard_map/ppermute | solution.py:36
  98.9 32.0 %copy-start.14 = (s32[2,2]{1,0:T(2,128)S(1)}, s32[2,2]{1,0:T(2,128)}, u32[]{:S(2)}) copy-start(s32[2,2]{1,0:T(2,128)} %get-tuple-element.50) | copy-start | bytes 52
  98.9 32.0 %copy-start.15 = (s32[1,2]{1,0:T(1,128)S(1)}, s32[1,2]{1,0:T(1,128)}, u32[]{:S(2)}) copy-start(s32[1,2]{1,0:T(1,128)} %get-tuple-element.51) | copy-start | bytes 28
  98.9 32.0 %copy-start.16 = (s32[1,2]{1,0:T(1,128)S(1)}, s32[1,2]{1,0:T(1,128)}, u32[]{:S(2)}) copy-start(s32[1,2]{1,0:T(1,128)} %get-tuple-element.49) | copy-start | bytes 28
  98.9 5.1 %copy-start.4 = (bf16[32,9216]{1,0:T(8,128)(2,1)}, bf16[32,9216]{1,0:T(8,128)(2,1)S(1)}, u32[]{:S(2)}) copy-start(bf16[32,9216]{1,0:T(8,128)(2,1)S(1)} %collective-permute-done.8.refs_0_.refs_6_) | copy-start | bytes 1769476
  104.0 0.8 copy-start.5
  114.7 67.6 %copy-start.12 = (s32[4,2]{1,0:T(4,128)S(1)}, s32[4,2]{1,0:T(4,128)}, u32[]{:S(2)}) copy-start(s32[4,2]{1,0:T(4,128)} %get-tuple-element.47) | copy-start | bytes 100
  114.7 68.8 %copy-start.9 = (f32[2,256,128]{2,1,0:T(8,128)S(1)}, f32[2,256,128]{2,1,0:T(8,128)}, u32[]{:S(2)}) copy-start(f32[2,256,128]{2,1,0:T(8,128)} %add.26.sums_ref) | copy-start | bytes 786436
  114.7 13.5 %collective-permute-start.12 = (f32[2,256,128]{2,1,0:T(8,128)}, f32[2,256,128]{2,1,0:T(8,128)S(1)}, u32[]{:S(2)}, u32[]{:S(2)}) collective-permute-start(f32[2,256,128]{2,1,0:T(8,128)} %shard_map.108), channel_id=1, source_target_pairs={{0,8},{8,0},{16,24},{24,16},{1,9},{9,1},{17,25},{25,17},{2,10},{10... | collective-permute-start | bytes 786440 | tf_op jit(solution)/shard_map/ppermute | solution.py:36
  114.8 38.6 %collective-permute-start.18 = (bf16[32,9216]{1,0:T(8,128)(2,1)}, bf16[32,9216]{1,0:T(8,128)(2,1)S(1)}, u32[]{:S(2)}, u32[]{:S(2)}) collective-permute-start(bf16[32,9216]{1,0:T(8,128)(2,1)} %get-tuple-element.56), channel_id=1, source_target_pairs={{0,2},{1,3},{2,0},{3,1},{4,6},{5,7},{6,4},{7,5},{8,10},{9,11},{10,... | collective-permute-start | bytes 1769480 | tf_op jit(solution)/shard_map/ppermute | solution.py:36
  127.0 55.3 %collective-permute-start.19 = (bf16[32,9216]{1,0:T(8,128)(2,1)}, bf16[32,9216]{1,0:T(8,128)(2,1)S(1)}, u32[]{:S(2)}, u32[]{:S(2)}) collective-permute-start(bf16[32,9216]{1,0:T(8,128)(2,1)} %get-tuple-element.57), channel_id=1, source_target_pairs={{0,4},{1,5},{2,6},{3,7},{4,0},{5,1},{6,2},{7,3},{8,12},{9,13},{10,... | collective-permute-start | bytes 1769480 | tf_op jit(solution)/shard_map/ppermute | solution.py:36
  129.2 8.4 %collective-permute-start.13 = (f32[2,256,128]{2,1,0:T(8,128)S(1)}, f32[2,256,128]{2,1,0:T(8,128)S(1)}, u32[]{:S(2)}, u32[]{:S(2)}) collective-permute-start(f32[2,256,128]{2,1,0:T(8,128)S(1)} %add.27), channel_id=1, source_target_pairs={{0,16},{8,24},{16,0},{24,8},{1,17},{9,25},{17,1},{25,9},{2,18},{10... | collective-permute-start | bytes 786440 | tf_op jit(solution)/shard_map/ppermute | solution.py:36
  131.5 62.7 %collective-permute-start.20 = (bf16[32,9216]{1,0:T(8,128)(2,1)}, bf16[32,9216]{1,0:T(8,128)(2,1)S(1)}, u32[]{:S(2)}, u32[]{:S(2)}) collective-permute-start(bf16[32,9216]{1,0:T(8,128)(2,1)} %get-tuple-element.58), channel_id=1, source_target_pairs={{0,6},{1,7},{2,4},{3,5},{4,2},{5,3},{6,0},{7,1},{8,14},{9,15},{10,... | collective-permute-start | bytes 1769480 | tf_op jit(solution)/shard_map/ppermute | solution.py:36
  138.3 45.3 %copy-start.10 = (f32[2,256,128]{2,1,0:T(8,128)S(1)}, f32[2,256,128]{2,1,0:T(8,128)}, u32[]{:S(2)}) copy-start(f32[2,256,128]{2,1,0:T(8,128)} %add.28.sums_ref) | copy-start | bytes 786436
  148.1 88.9 %collective-permute-start.14 = (bf16[32,9216]{1,0:T(8,128)(2,1)}, bf16[32,9216]{1,0:T(8,128)(2,1)S(1)}, u32[]{:S(2)}, u32[]{:S(2)}) collective-permute-start(bf16[32,9216]{1,0:T(8,128)(2,1)} %get-tuple-element.48), channel_id=1, source_target_pairs={{0,7},{1,6},{2,5},{3,4},{4,3},{5,2},{6,1},{7,0},{8,15},{9,14},{10,... | collective-permute-start | bytes 1769480 | tf_op jit(solution)/shard_map/ppermute | solution.py:36
  149.6 53.5 %collective-permute-start.15 = (bf16[32,9216]{1,0:T(8,128)(2,1)}, bf16[32,9216]{1,0:T(8,128)(2,1)S(1)}, u32[]{:S(2)}, u32[]{:S(2)}) collective-permute-start(bf16[32,9216]{1,0:T(8,128)(2,1)} %get-tuple-element.52), channel_id=1, source_target_pairs={{0,1},{1,0},{2,3},{3,2},{4,5},{5,4},{6,7},{7,6},{8,9},{9,8},{10,11... | collective-permute-start | bytes 1769480 | tf_op jit(solution)/shard_map/ppermute | solution.py:36
  153.4 40.8 %copy-start.6 = (bf16[32,9216]{1,0:T(8,128)(2,1)}, bf16[32,9216]{1,0:T(8,128)(2,1)S(1)}, u32[]{:S(2)}) copy-start(bf16[32,9216]{1,0:T(8,128)(2,1)S(1)} %collective-permute-done.18.refs_1_.refs_4_) | copy-start | bytes 1769476
  153.4 49.8 %collective-permute-start.16 = (bf16[32,9216]{1,0:T(8,128)(2,1)}, bf16[32,9216]{1,0:T(8,128)(2,1)}, u32[]{:S(2)}, u32[]{:S(2)}) collective-permute-start(bf16[32,9216]{1,0:T(8,128)(2,1)} %get-tuple-element.53), channel_id=1, source_target_pairs={{0,3},{1,2},{2,1},{3,0},{4,7},{5,6},{6,5},{7,4},{8,11},{9,10},{10,... | collective-permute-start | bytes 1769480 | tf_op jit(solution)/shard_map/ppermute | solution.py:36
  182.3 11.9 %copy-start.7 = (bf16[32,9216]{1,0:T(8,128)(2,1)}, bf16[32,9216]{1,0:T(8,128)(2,1)S(1)}, u32[]{:S(2)}) copy-start(bf16[32,9216]{1,0:T(8,128)(2,1)S(1)} %collective-permute-done.19.refs_2_.refs_5_) | copy-start | bytes 1769476
  182.3 49.8 %collective-permute-start.17 = (bf16[32,9216]{1,0:T(8,128)(2,1)}, bf16[32,9216]{1,0:T(8,128)(2,1)}, u32[]{:S(2)}, u32[]{:S(2)}) collective-permute-start(bf16[32,9216]{1,0:T(8,128)(2,1)} %get-tuple-element.54), channel_id=1, source_target_pairs={{0,5},{1,4},{2,7},{3,6},{4,1},{5,0},{6,3},{7,2},{8,13},{9,12},{10,... | collective-permute-start | bytes 1769480 | tf_op jit(solution)/shard_map/ppermute | solution.py:36
  194.2 0.8 copy-start.8
  203.2 29.0 %copy-start.11 = (bf16[32,9216]{1,0:T(8,128)(2,1)}, bf16[32,9216]{1,0:T(8,128)(2,1)S(1)}, u32[]{:S(2)}) copy-start(bf16[32,9216]{1,0:T(8,128)(2,1)S(1)} %collective-permute-done.15.refs_0_) | copy-start | bytes 1769476
